TPU v7x, 32 devices: a whole 2x2x4 slice. The times are simulated.
32 devices in a mesh: dp: 4 (over z), seq: 4 (over x, core), head: 2 (over y).
Axes of the slice: x: 2, y: 2, z: 4, core: 2. Of those that a mesh axis runs over, the one named last changes fastest.
Arguments:
- layer_in: bfloat16 [4, 1024, 768], P('dp', 'seq'), may hold values from -6 to 6
- cotangent: bfloat16 [4, 1024, 768], P('dp', 'seq'), may hold values from -6 to 6
- w_query: bfloat16 [768, 768], P('dp', 'head'), may hold values from -0.3125 to 0.3125
- w_key: bfloat16 [768, 768], P('dp', 'head'), may hold values from -0.21875 to 0.21875
- w_value: bfloat16 [768, 768], P('dp', 'head'), may hold values from -0.21875 to 0.21875
- w_out: bfloat16 [768, 768], P('dp', 'head'), may hold values from -0.875 to 0.875
- w_up: bfloat16 [768, 3072], P('dp', 'head'), may hold values from -0.21875 to 0.21875
- w_down: bfloat16 [768, 3072], P('dp', 'head'), may hold values from -0.109375 to 0.109375
- query_bias: float32 [768], P('head'), may hold values from -3 to 3
- value_bias: float32 [768], P('head'), may hold values from -3 to 3
- out_bias: float32 [768], replicated, may hold values from -3 to 3
- up_bias: float32 [3072], P('head'), may hold values from -3 to 3
- down_bias: float32 [768], replicated, may hold values from -3 to 3
- attn_gain: float32 [768], replicated, may hold values from 0.5 to 1.5
- attn_shift: float32 [768], replicated, may hold values from -2 to 2
- mlp_gain: float32 [768], replicated, may hold values from 0.5 to 1.5
- mlp_shift: float32 [768], replicated, may hold values from -2 to 2
Outputs:
- layer_out: bfloat16 [4, 1024, 768], P('dp', 'seq')
- grad_in: float32 [4, 1024, 768], P('dp', 'seq')
- grad_w_query: float32 [768, 768], P('dp', 'head')
- grad_w_key: float32 [768, 768], P('dp', 'head')
- grad_w_value: float32 [768, 768], P('dp', 'head')
- grad_w_out: float32 [768, 768], P('dp', 'head')
- grad_w_up: float32 [768, 3072], P('dp', 'head')
- grad_w_down: float32 [768, 3072], P('dp', 'head')
- grad_query_bias: float32 [768], P('head')
- grad_value_bias: float32 [768], P('head')
- grad_out_bias: float32 [768], replicated
- grad_up_bias: float32 [3072], P('head')
- grad_down_bias: float32 [768], replicated
- grad_attn_gain: float32 [768], replicated
- grad_attn_shift: float32 [768], replicated
- grad_mlp_gain: float32 [768], replicated
- grad_mlp_shift: float32 [768], replicated
All inputs are finite; a program needn't handle non-finite values.
Results may differ from a plain program's by a relative error of at most 0.02.
Values may be sent and summed in bfloat16 or wider, within the bound.
No kernel may reach another device: no remote copies, remote signals or barrier semaphores. Data moves between devices by JAX's collectives and lax.ppermute only.
A program may use at most 64 MiB of HBM per device.

v0:
```python
import math

import jax
import jax.numpy as jnp
from jax import lax
from jax.sharding import PartitionSpec as P

HD = 64


NORM_EPS = 1e-05
SQRT_HALF = 0.7071067811865476
INV_ROOT_TWO_PI = 0.3989422804014327


def shortened(shard):

    def short(part):
        return part.astype(jnp.bfloat16) if part.dtype == jnp.float32 else part

    return jax.tree.map(short, shard)


def norm_forward(values, gain_vec, offset):
    mean_val = jnp.mean(values, axis=-1, keepdims=True)
    centred = values - mean_val
    inverse = lax.rsqrt(jnp.mean(centred * centred, axis=-1, keepdims=True) + NORM_EPS)
    normed = centred * inverse
    return (normed, inverse, normed * gain_vec + offset)


def norm_backward(grad_rows, normed, inverse, gain_vec):
    scaled = grad_rows * gain_vec
    back_grad = inverse * (
        scaled
        - jnp.mean(scaled, axis=-1, keepdims=True)
        - normed * jnp.mean(scaled * normed, axis=-1, keepdims=True)
    )
    return (back_grad, jnp.sum(grad_rows * normed, axis=0), jnp.sum(grad_rows, axis=0))


def gelu_value(pre_act):
    return 0.5 * pre_act * (1.0 + jax.scipy.special.erf(pre_act * SQRT_HALF))


def gelu_slope(pre_act):
    return 0.5 * (
        1.0 + jax.scipy.special.erf(pre_act * SQRT_HALF)
    ) + pre_act * INV_ROOT_TWO_PI * jnp.exp(-0.5 * pre_act * pre_act)


def matmul(first_mat, second_mat):
    return jnp.dot(first_mat, second_mat, preferred_element_type=jnp.float32)


def matmul_nt(first_mat, second_mat):
    return lax.dot_general(
        first_mat, second_mat, (((1,), (1,)), ((), ())), preferred_element_type=jnp.float32
    )


def matmul_tn(first_mat, second_mat):
    return lax.dot_general(
        first_mat, second_mat, (((0,), (0,)), ((), ())), preferred_element_type=jnp.float32
    )


def per_device(
    layer_in,
    cotangent,
    w_query,
    w_key,
    w_value,
    w_out,
    w_up,
    w_down,
    query_bias,
    value_bias,
    out_bias,
    up_bias,
    down_bias,
    attn_gain,
    attn_shift,
    mlp_gain,
    mlp_shift,
):
    local_width = w_query.shape[1]
    local_hidden = w_up.shape[1]
    local_heads = local_width // HD
    model_width = layer_in.shape[2]

    def one_clip(grad_sums, clip_pair):
        clip_in, grad_rows = clip_pair
        frames = clip_in.shape[0]
        inputs = clip_in.astype(jnp.float32)
        attn_normed, attn_inverse, attn_affine = norm_forward(inputs, attn_gain, attn_shift)
        attn_act = attn_affine.astype(jnp.bfloat16)
        full_query, full_key, full_value, full_out = (
            lax.all_gather(w_query, "dp", axis=0, tiled=True),
            lax.all_gather(w_key, "dp", axis=0, tiled=True),
            lax.all_gather(w_value, "dp", axis=0, tiled=True),
            lax.all_gather(w_out, "dp", axis=0, tiled=True),
        )
        query = (matmul(attn_act, full_query) + query_bias).astype(jnp.bfloat16)
        key_rows = matmul(attn_act, full_key).astype(jnp.bfloat16)
        value_rows = (matmul(attn_act, full_value) + value_bias).astype(jnp.bfloat16)
        query_h = query.reshape(frames, local_heads, HD)
        run_max = jnp.full((local_heads, frames), -1e30, jnp.float32)
        run_sum = jnp.zeros((local_heads, frames), jnp.float32)
        run_acc = jnp.zeros((local_heads, frames, HD), jnp.float32)
        key_block = lax.all_gather(key_rows, "seq", axis=0, tiled=True)
        value_block = lax.all_gather(value_rows, "seq", axis=0, tiled=True)
        row_count = key_block.shape[0]
        step_size = min(row_count, 512)
        for offset in range(0, row_count, step_size):
            key_part = key_block[offset : offset + step_size].reshape(-1, local_heads, HD)
            value_part = value_block[offset : offset + step_size].reshape(-1, local_heads, HD)
            scores = 0.125 * jnp.einsum(
                "qhe,khe->hqk", query_h, key_part, preferred_element_type=jnp.float32
            )
            new_max = jnp.maximum(run_max, jnp.max(scores, axis=-1))
            exp_scores = jnp.exp(scores - new_max[:, :, None])
            factor = jnp.exp(run_max - new_max)
            run_sum = run_sum * factor + jnp.sum(exp_scores, axis=-1)
            run_acc = run_acc * factor[:, :, None] + jnp.einsum(
                "hqk,khe->hqe",
                exp_scores.astype(jnp.bfloat16),
                value_part,
                preferred_element_type=jnp.float32,
            )
            run_max = new_max
        run_max, run_sum, run_acc = (run_max, run_sum, run_acc)
        log_total = run_max + jnp.log(run_sum)
        weighted = run_acc / run_sum[:, :, None]
        context = (
            jnp.transpose(weighted, (1, 0, 2)).reshape(frames, local_width).astype(jnp.bfloat16)
        )
        attn_part = lax.psum(matmul_nt(context, full_out).astype(jnp.bfloat16), "head").astype(
            jnp.float32
        )
        resid_mid = inputs + attn_part + out_bias
        mlp_normed, mlp_inverse, mlp_affine = norm_forward(resid_mid, mlp_gain, mlp_shift)
        mlp_act = mlp_affine.astype(jnp.bfloat16)
        full_up, full_down = (
            lax.all_gather(w_up, "dp", axis=0, tiled=True),
            lax.all_gather(w_down, "dp", axis=0, tiled=True),
        )
        pre_act = matmul(mlp_act, full_up) + up_bias
        hidden = gelu_value(pre_act).astype(jnp.bfloat16)
        mlp_part = lax.psum(matmul_nt(hidden, full_down).astype(jnp.bfloat16), "head").astype(
            jnp.float32
        )
        layer_out = (resid_mid + mlp_part + down_bias).astype(jnp.bfloat16)
        grad_float = grad_rows.astype(jnp.float32)
        grad_down_bias = jnp.sum(grad_float, axis=0)
        grad_w_down = matmul_tn(grad_rows, hidden)
        back_up, back_down = (
            lax.all_gather(w_up, "dp", axis=0, tiled=True),
            lax.all_gather(w_down, "dp", axis=0, tiled=True),
        )
        d_pre = (matmul(grad_rows, back_down) * gelu_slope(pre_act)).astype(jnp.bfloat16)
        grad_up_bias = jnp.sum(d_pre.astype(jnp.float32), axis=0)
        grad_w_up = matmul_tn(mlp_act, d_pre)
        d_mlp_act = lax.psum(matmul_nt(d_pre, back_up).astype(jnp.bfloat16), "head").astype(
            jnp.float32
        )
        mlp_back, grad_mlp_gain, grad_mlp_shift = norm_backward(
            d_mlp_act, mlp_normed, mlp_inverse, mlp_gain
        )
        d_mid = grad_float + mlp_back
        grad_out_bias = jnp.sum(d_mid, axis=0)
        d_mid_round = d_mid.astype(jnp.bfloat16)
        grad_w_out = matmul_tn(d_mid_round, context)
        back_query, back_key, back_value, back_out = (
            lax.all_gather(w_query, "dp", axis=0, tiled=True),
            lax.all_gather(w_key, "dp", axis=0, tiled=True),
            lax.all_gather(w_value, "dp", axis=0, tiled=True),
            lax.all_gather(w_out, "dp", axis=0, tiled=True),
        )
        d_context = matmul(d_mid_round, back_out).astype(jnp.bfloat16)
        dctx_h = d_context.reshape(frames, local_heads, HD)
        context_float = context.reshape(frames, local_heads, HD).astype(jnp.float32)
        delta_row = jnp.transpose(jnp.sum(dctx_h.astype(jnp.float32) * context_float, axis=-1))
        all_keys, all_values = (
            lax.all_gather(key_rows, "seq", axis=0, tiled=True),
            lax.all_gather(value_rows, "seq", axis=0, tiled=True),
        )
        total_frames = all_keys.shape[0]
        block = math.gcd(total_frames, 512)
        blocks = total_frames // block
        key_blocks = all_keys.reshape(blocks, block, local_heads, HD)
        value_blocks = all_values.reshape(blocks, block, local_heads, HD)

        def key_step(dq_acc, key_pair):
            key_part, value_part = key_pair
            scores = 0.125 * jnp.einsum(
                "qhe,khe->hqk", query_h, key_part, preferred_element_type=jnp.float32
            )
            prob_mat = jnp.exp(scores - log_total[:, :, None])
            d_prob = jnp.einsum(
                "qhe,khe->hqk", dctx_h, value_part, preferred_element_type=jnp.float32
            )
            d_score = (0.125 * prob_mat * (d_prob - delta_row[:, :, None])).astype(jnp.bfloat16)
            dq_acc = dq_acc + jnp.einsum(
                "hqk,khe->qhe", d_score, key_part, preferred_element_type=jnp.float32
            )
            key_grad = jnp.einsum(
                "hqk,qhe->khe", d_score, query_h, preferred_element_type=jnp.float32
            )
            value_grad = jnp.einsum(
                "hqk,qhe->khe",
                prob_mat.astype(jnp.bfloat16),
                dctx_h,
                preferred_element_type=jnp.float32,
            )
            return (dq_acc, jnp.stack((key_grad, value_grad), axis=1))

        dq_acc, kv_terms = lax.scan(
            key_step, jnp.zeros((frames, local_heads, HD), jnp.float32), (key_blocks, value_blocks)
        )
        kv_terms = kv_terms.reshape(total_frames, 2, local_width)
        kv_grads = lax.psum_scatter(
            kv_terms.astype(jnp.bfloat16), "seq", scatter_dimension=0, tiled=True
        ).astype(jnp.float32)
        d_query = dq_acc.reshape(frames, local_width)
        d_key = kv_grads[:, 0]
        d_value = kv_grads[:, 1]
        grad_query_bias = jnp.sum(d_query, axis=0)
        grad_value_bias = jnp.sum(d_value, axis=0)
        query_round = d_query.astype(jnp.bfloat16)
        key_round = d_key.astype(jnp.bfloat16)
        value_round = d_value.astype(jnp.bfloat16)
        grad_w_query = matmul_tn(attn_act, query_round)
        grad_w_key = matmul_tn(attn_act, key_round)
        grad_w_value = matmul_tn(attn_act, value_round)
        attn_terms = (
            matmul_nt(query_round, back_query)
            + matmul_nt(key_round, back_key)
            + matmul_nt(value_round, back_value)
        )
        d_attn_act = lax.psum(attn_terms.astype(jnp.bfloat16), "head").astype(jnp.float32)
        attn_back, grad_attn_gain, grad_attn_shift = norm_backward(
            d_attn_act, attn_normed, attn_inverse, attn_gain
        )
        grad_in = d_mid + attn_back
        grads = (
            grad_w_query,
            grad_w_key,
            grad_w_value,
            grad_w_out,
            grad_w_up,
            grad_w_down,
            grad_query_bias,
            grad_value_bias,
            grad_out_bias,
            grad_up_bias,
            grad_down_bias,
            grad_attn_gain,
            grad_attn_shift,
            grad_mlp_gain,
            grad_mlp_shift,
        )
        return (jax.tree.map(jnp.add, grad_sums, grads), (layer_out, grad_in))

    square_zero = jnp.zeros((model_width, local_width), jnp.float32)
    wide_zero = jnp.zeros((model_width, local_hidden), jnp.float32)
    width_zero = jnp.zeros((model_width,), jnp.float32)
    start_sums = (
        square_zero,
        square_zero,
        square_zero,
        square_zero,
        wide_zero,
        wide_zero,
        jnp.zeros((local_width,), jnp.float32),
        jnp.zeros((local_width,), jnp.float32),
        width_zero,
        jnp.zeros((local_hidden,), jnp.float32),
        width_zero,
        width_zero,
        width_zero,
        width_zero,
        width_zero,
    )
    grad_sums, outputs = lax.scan(one_clip, start_sums, (layer_in, cotangent))
    shard_sums = jax.tree.map(
        lambda part: part.astype(jnp.float32),
        lax.psum_scatter(shortened(grad_sums[0:6]), "dp", scatter_dimension=0, tiled=True),
    )
    shard_grads = jax.tree.map(
        lambda part: part.astype(jnp.float32), lax.psum(shortened(shard_sums), "seq")
    )
    small_grads = lax.psum(grad_sums[6:15], ("dp", "seq"))
    return (
        outputs[0],
        outputs[1],
        shard_grads[0],
        shard_grads[1],
        shard_grads[2],
        shard_grads[3],
        shard_grads[4],
        shard_grads[5],
        small_grads[0],
        small_grads[1],
        small_grads[2],
        small_grads[3],
        small_grads[4],
        small_grads[5],
        small_grads[6],
        small_grads[7],
        small_grads[8],
    )


def solution(mesh):
    return jax.shard_map(
        per_device,
        mesh=mesh,
        in_specs=(
            P("dp", "seq", None),
            P("dp", "seq", None),
            P("dp", "head"),
            P("dp", "head"),
            P("dp", "head"),
            P("dp", "head"),
            P("dp", "head"),
            P("dp", "head"),
            P("head"),
            P("head"),
            P(),
            P("head"),
            P(),
            P(),
            P(),
            P(),
            P(),
        ),
        out_specs=(
            P("dp", "seq", None),
            P("dp", "seq", None),
            P("dp", "head"),
            P("dp", "head"),
            P("dp", "head"),
            P("dp", "head"),
            P("dp", "head"),
            P("dp", "head"),
            P("head"),
            P("head"),
            P(),
            P("head"),
            P(),
            P(),
            P(),
            P(),
            P(),
        ),
        check_vma=False,
    )
```

profile of v0, /device:TPU:0, one launch (start us, length us, event | category | flops | bytes accessed | tf_op | source)
XLA Modules:
  0.0 621.3 jit_solution(18236052324052979757)
XLA Ops:
  8.1 18.5 %all_gather.43 = bf16[768,384]{1,0:T(8,128)(2,1)S(1)} all-gather(bf16[192,384]{1,0:T(8,128)(2,1)} %param.23), channel_id=1, replica_groups=mesh['dp'=4,'seq'=4,'head'=2] {'dp'}, dimensions={0}, use_global_device_ids=true | all-gather | bytes 737280 | tf_op jit(solution)/shard_map/while/body/eval_jaxpr/all_gather | solution.py:101
  30.8 8.7 %all_gather.44 = bf16[1024,384]{1,0:T(8,128)(2,1)S(1)} all-gather(bf16[256,384]{1,0:T(8,128)(2,1)S(1)} %fusion.61), channel_id=1, replica_groups=mesh['dp'=4,'seq'=4,'head'=2] {'seq'}, dimensions={0}, use_global_device_ids=true | all-gather | bytes 983040 | tf_op jit(solution)/shard_map/while/body/eval_jaxpr/all_gather | solution.py:186
  40.5 17.5 %all_gather.40 = bf16[768,384]{1,0:T(8,128)(2,1)S(1)} all-gather(bf16[192,384]{1,0:T(8,128)(2,1)S(1)} %copy-done.33), channel_id=1, replica_groups=mesh['dp'=4,'seq'=4,'head'=2] {'dp'}, dimensions={0}, use_global_device_ids=true | all-gather | bytes 737280 | tf_op jit(solution)/shard_map/while/body/eval_jaxpr/all_gather | solution.py:99
  59.5 16.3 %all_gather.41 = bf16[768,384]{1,0:T(8,128)(2,1)S(1)} all-gather(bf16[192,384]{1,0:T(8,128)(2,1)S(1)} %copy-done.34), channel_id=1, replica_groups=mesh['dp'=4,'seq'=4,'head'=2] {'dp'}, dimensions={0}, use_global_device_ids=true | all-gather | bytes 737280 | tf_op jit(solution)/shard_map/while/body/eval_jaxpr/all_gather | solution.py:100
  77.1 7.6 %all_gather.42 = bf16[1024,384]{1,0:T(8,128)(2,1)S(1)} all-gather(bf16[256,384]{1,0:T(8,128)(2,1)S(1)} %convolution_convert_fusion.10), channel_id=1, replica_groups=mesh['dp'=4,'seq'=4,'head'=2] {'seq'}, dimensions={0}, use_global_device_ids=true | all-gather | bytes 983040 | tf_op jit(solution)/shard_map/while/body/eval_jaxpr/all_gather | solution.py:185
  92.5 16.7 %all_gather.45 = bf16[768,384]{1,0:T(8,128)(2,1)S(1)} all-gather(bf16[192,384]{1,0:T(8,128)(2,1)S(1)} %copy-done.35), channel_id=1, replica_groups=mesh['dp'=4,'seq'=4,'head'=2] {'dp'}, dimensions={0}, use_global_device_ids=true | all-gather | bytes 737280 | tf_op jit(solution)/shard_map/while/body/eval_jaxpr/all_gather | solution.py:102
  109.2 3.8 fusion.23
  118.8 25.1 %all-reduce.8.cloned.1.call-done = bf16[256,768]{1,0:T(8,128)(2,1)} async-done(((bf16[256,768]{1,0:T(8,128)(2,1)}), bf16[256,768]{1,0:T(8,128)(2,1)}) %all-reduce.8.cloned.1.call-update) | async-done | bytes 393232 | tf_op jit(solution)/shard_map/while/body/eval_jaxpr/psum | solution.py:138
  146.5 23.5 %all-gather.3.cloned.1.call-done = bf16[768,1536]{1,0:T(8,128)(2,1)} async-done(((bf16[192,1536]{1,0:T(8,128)(2,1)}), bf16[768,1536]{1,0:T(8,128)(2,1)}) %all-gather.3.cloned.1.call-update) | async-done | bytes 2359312 | tf_op jit(solution)/shard_map/while/body/eval_jaxpr/all_gather | solution.py:145
  170.0 4.1 multiply_convert_fusion.1
  174.1 45.9 %all-gather.5.cloned.1.call-done = bf16[768,1536]{1,0:T(8,128)(2,1)} async-done(((bf16[192,1536]{1,0:T(8,128)(2,1)}), bf16[768,1536]{1,0:T(8,128)(2,1)}) %all-gather.5.cloned.1.call-update) | async-done | bytes 2359312 | tf_op jit(solution)/shard_map/while/body/eval_jaxpr/all_gather | solution.py:159
  220.0 3.9 convert_reduce_fusion
  232.5 18.5 %all-reduce.10.cloned.1.call-done = bf16[256,768]{1,0:T(8,128)(2,1)} async-done(((bf16[256,768]{1,0:T(8,128)(2,1)}), bf16[256,768]{1,0:T(8,128)(2,1)}) %all-reduce.10.cloned.1.call-update) | async-done | bytes 393232 | tf_op jit(solution)/shard_map/while/body/eval_jaxpr/psum | solution.py:164
  256.9 19.8 %while.17 = (s32[]{:T(128)}, f32[256,6,64]{0,2,1:T(8,128)}, bf16[2,512,2,6,64]{1,4,3,2,0:T(8,128)(2,1)}, bf16[2,512,6,64]{1,3,2,0:T(8,128)(2,1)}, bf16[256,6,64]...) while((s32[]{:T(128)}, f32[256,6,64]{0,2,1:T(8,128)}, ...), condition=%wide.region_15.0_spmd.clone, body=%wide.region_14.0_spmd.clone.sunk | while | flops 512163840 | bytes 41310460 | solution.py:218
  290.1 20.1 %reduce-scatter.10.cloned.1.call-done = bf16[256,2,384]{0,2,1:T(8,128)(2,1)} async-done(((bf16[1024,2,384]{0,2,1:T(8,128)(2,1)}), bf16[256,2,384]{0,2,1:T(8,128)(2,1)}) %reduce-scatter.10.cloned.1.call-update) | async-done | bytes 393232 | tf_op jit(solution)/shard_map/while/body/eval_jaxpr/reduce_scatter | solution.py:222
  317.1 4.0 convolution_convert_fusion.7
  323.7 36.4 %reduce-scatter.22.cloned.1.call-done = bf16[192,1536]{1,0:T(8,128)(2,1)} async-done(((bf16[768,1536]{1,0:T(8,128)(2,1)}), bf16[192,1536]{1,0:T(8,128)(2,1)}) %reduce-scatter.22.cloned.1.call-update) | async-done | bytes 589840
  362.4 22.0 %reduce-scatter.12.cloned.1.call-done = bf16[192,384]{1,0:T(8,128)(2,1)} async-done(((bf16[768,384]{1,0:T(8,128)(2,1)}), bf16[192,384]{1,0:T(8,128)(2,1)}) %reduce-scatter.12.cloned.1.call-update) | async-done | bytes 147472 | tf_op jit(solution)/shard_map/reduce_scatter | solution.py:288
  384.4 22.8 %reduce-scatter.18.cloned.1.call-done = bf16[192,384]{1,0:T(8,128)(2,1)} async-done(((bf16[768,384]{1,0:T(8,128)(2,1)}), bf16[192,384]{1,0:T(8,128)(2,1)}) %reduce-scatter.18.cloned.1.call-update) | async-done | bytes 147472 | tf_op jit(solution)/shard_map/reduce_scatter | solution.py:288
  407.1 22.8 %reduce-scatter.14.cloned.1.call-done = bf16[192,384]{1,0:T(8,128)(2,1)} async-done(((bf16[768,384]{1,0:T(8,128)(2,1)}), bf16[192,384]{1,0:T(8,128)(2,1)}) %reduce-scatter.14.cloned.1.call-update) | async-done | bytes 147472 | tf_op jit(solution)/shard_map/reduce_scatter | solution.py:288
  429.9 22.8 %reduce-scatter.16.cloned.1.call-done = bf16[192,384]{1,0:T(8,128)(2,1)} async-done(((bf16[768,384]{1,0:T(8,128)(2,1)}), bf16[192,384]{1,0:T(8,128)(2,1)}) %reduce-scatter.16.cloned.1.call-update) | async-done | bytes 147472 | tf_op jit(solution)/shard_map/reduce_scatter | solution.py:288
  452.7 48.3 %reduce-scatter.20.cloned.1.call-done = bf16[192,1536]{1,0:T(8,128)(2,1)} async-done(((bf16[768,1536]{1,0:T(8,128)(2,1)}), bf16[192,1536]{1,0:T(8,128)(2,1)}) %reduce-scatter.20.cloned.1.call-update) | async-done | bytes 589840 | tf_op jit(solution)/shard_map/reduce_scatter | solution.py:288
  501.1 36.5 %all-reduce.14.cloned.1.call-done = (bf16[256,768]{1,0:T(8,128)(2,1)}, bf16[256,768]{1,0:T(8,128)(2,1)}) async-done(((bf16[256,768]{1,0:T(8,128)(2,1)}, bf16[256,768]{1,0:T(8,128)(2,1)}), (bf16[256,768]{1,0:T(8,128)(2,1)}, bf16[256,768]{1,0:T(8,128)(2,1)})) %all-reduce.14.cloned.1.call-update) | async-done | bytes 786448 | tf_op jit(solution)/shard_map/while/body/eval_jaxpr/psum | solution.py:150
  539.1 62.5 %all-reduce = (f32[384]{0:T(512)}, f32[384]{0:T(512)}, f32[768]{0:T(1024)}, f32[1536]{0:T(1024)}, f32[768]{0:T(1024)}, /*index=5*/f32[768]{0:T(1024)}, f32[768]{0:T(1024)}, f32[768]{0:T(1024)}, f32[768]{0:T(1024)}) all-reduce(f32[384]{0:T(512)S(1)} %reduce_sum.220, ...), channel_id=1, replica_groups=mesh['dp'=4,'seq'=4,'head'=2] {'dp','seq'}, use_global_device_ids=true, to_apply=%region_33.34 | all-reduce | flops 6912 | bytes 55296 | tf_op jit(solution)/shard_map/psum | solution.py:293
  (268 shorter events, 96.7 us)
Async XLA Ops:
  8.0 135.9 %all-reduce.8.cloned.1.call-start = ((), (), s32[]{:S(2)}) async-start(), calls=%async_computation.7 | async-start | bytes 786432 | tf_op jit(solution)/shard_map/while/body/eval_jaxpr/psum | solution.py:138
  115.7 54.2 %copy-start.46 = (f32[768]{0:T(1024)S(1)}, f32[768]{0:T(1024)}, u32[]{:S(2)}) copy-start(f32[768]{0:T(1024)} %param.34) | copy-start | bytes 9220
  115.8 54.2 %copy-start.69 = (f32[768]{0:T(1024)S(1)}, f32[768]{0:T(1024)}, u32[]{:S(2)}) copy-start(f32[768]{0:T(1024)} %param.35) | copy-start | bytes 9220
  115.8 54.2 %copy-start.72 = (f32[1536]{0:T(1024)S(1)}, f32[1536]{0:T(1024)}, u32[]{:S(2)}) copy-start(f32[1536]{0:T(1024)} %param.30) | copy-start | bytes 18436
  117.6 52.4 %all-gather.3.cloned.1.call-start = ((), (), s32[]{:S(2)}) async-start(), calls=%async_computation.8 | async-start | bytes 2949120 | tf_op jit(solution)/shard_map/while/body/eval_jaxpr/all_gather | solution.py:145
  118.2 101.9 %all-gather.5.cloned.1.call-start = ((), (), s32[]{:S(2)}) async-start(), calls=%async_computation.9 | async-start | bytes 2949120 | tf_op jit(solution)/shard_map/while/body/eval_jaxpr/all_gather | solution.py:159
  118.8 132.3 %all-reduce.10.cloned.1.call-start = ((), (), s32[]{:S(2)}) async-start(), calls=%async_computation.10 | async-start | bytes 786432 | tf_op jit(solution)/shard_map/while/body/eval_jaxpr/psum | solution.py:164
  146.5 73.6 %copy-start.20 = (bf16[1,256,768]{2,1,0:T(8,128)(2,1)S(1)}, bf16[1,256,768]{2,1,0:T(8,128)(2,1)}, u32[]{:S(2)}) copy-start(bf16[1,256,768]{2,1,0:T(8,128)(2,1)} %param.20) | copy-start | bytes 1179652
  226.4 83.9 %reduce-scatter.10.cloned.1.call-start = ((), (), s32[]{:S(2)}) async-start(), calls=%async_computation.11 | async-start | bytes 1966080 | tf_op jit(solution)/shard_map/while/body/eval_jaxpr/reduce_scatter | solution.py:222
  282.1 78.0 %reduce-scatter.22.cloned.1.call-start = ((), (), s32[]{:S(2)}) async-start(), calls=%async_computation.17 | async-start | bytes 2949120
  285.5 98.8 %reduce-scatter.12.cloned.1.call-start = ((), (), s32[]{:S(2)}) async-start(), calls=%async_computation.12 | async-start | bytes 737280 | tf_op jit(solution)/shard_map/reduce_scatter | solution.py:288
  288.7 118.5 %reduce-scatter.18.cloned.1.call-start = ((), (), s32[]{:S(2)}) async-start(), calls=%async_computation.15 | async-start | bytes 737280 | tf_op jit(solution)/shard_map/reduce_scatter | solution.py:288
  290.0 139.9 %reduce-scatter.14.cloned.1.call-start = ((), (), s32[]{:S(2)}) async-start(), calls=%async_computation.13 | async-start | bytes 737280 | tf_op jit(solution)/shard_map/reduce_scatter | solution.py:288
  312.8 140.0 %reduce-scatter.16.cloned.1.call-start = ((), (), s32[]{:S(2)}) async-start(), calls=%async_computation.14 | async-start | bytes 737280 | tf_op jit(solution)/shard_map/reduce_scatter | solution.py:288
  314.5 186.6 %reduce-scatter.20.cloned.1.call-start = ((), (), s32[]{:S(2)}) async-start(), calls=%async_computation.16 | async-start | bytes 2949120 | tf_op jit(solution)/shard_map/reduce_scatter | solution.py:288
  317.1 220.5 %all-reduce.14.cloned.1.call-start = ((), (), s32[]{:S(2)}) async-start(), calls=%async_computation.19 | async-start | bytes 1572864 | tf_op jit(solution)/shard_map/while/body/eval_jaxpr/psum | solution.py:150
  323.3 214.3 %copy-start.66 = (f32[256]{0:T(256)S(1)}, f32[256]{0:T(256)}, u32[]{:S(2)}) copy-start(f32[256]{0:T(256)} %copy-done.64) | copy-start | bytes 3076
  323.4 215.7 %copy-start.56 = (f32[768]{0:T(1024)S(1)}, f32[768]{0:T(1024)}, u32[]{:S(2)}) copy-start(f32[768]{0:T(1024)} %get-tuple-element.280) | copy-start | bytes 9220
  323.4 215.7 %copy-start.57 = (f32[768]{0:T(1024)S(1)}, f32[768]{0:T(1024)}, u32[]{:S(2)}) copy-start(f32[768]{0:T(1024)} %get-tuple-element.286) | copy-start | bytes 9220
  323.4 215.7 %copy-start.58 = (f32[768]{0:T(1024)S(1)}, f32[768]{0:T(1024)}, u32[]{:S(2)}) copy-start(f32[768]{0:T(1024)} %get-tuple-element.323) | copy-start | bytes 9220
  323.4 215.7 %copy-start.59 = (f32[768]{0:T(1024)S(1)}, f32[768]{0:T(1024)}, u32[]{:S(2)}) copy-start(f32[768]{0:T(1024)} %get-tuple-element.329) | copy-start | bytes 9220
  323.4 215.7 %copy-start.67 = (f32[1536]{0:T(1024)S(1)}, f32[1536]{0:T(1024)}, u32[]{:S(2)}) copy-start(f32[1536]{0:T(1024)} %get-tuple-element.345) | copy-start | bytes 18436
  323.4 278.2 %copy-start.68 = (f32[768]{0:T(1024)S(1)}, f32[768]{0:T(1024)}, u32[]{:S(2)}) copy-start(f32[768]{0:T(1024)} %param.31) | copy-start | bytes 9220
  323.4 280.7 %all-reduce.12.cloned.1.call-start = ((), (), s32[]{:S(2)}) async-start(), calls=%async_computation.18 | async-start | bytes 3932160 | tf_op jit(solution)/shard_map/psum | solution.py:291
  (69 other events, 631.4 us)
Sparse Core Ops, SparseCore 0:
  117.7 26.1 all-reduce.7
  226.5 24.5 all-reduce.9
  282.2 27.9 reduce-scatter.9
  312.4 47.7 reduce-scatter.21
  362.9 21.4 reduce-scatter.11
  386.5 20.5 reduce-scatter.17
  409.4 20.4 reduce-scatter.13
  432.2 20.4 reduce-scatter.15
  455.0 45.9 reduce-scatter.19
  503.8 33.7 all-reduce.13
  541.0 50.1 all-reduce.11
Sparse Core Ops, SparseCore 1:
  119.6 50.3 all-gather.2
  171.4 48.6 all-gather.4
where the time goes:
time: 622 us; the launch traced here: 621 us
  waiting for transfers between devices  346 us (56%)
  blocking collectives  148 us (24%)
  matrix products  50.3 us (8%)
  local copies, waits for them, and re-layouts  32.5 us (5%)
  other arithmetic  27.5 us (4%)
  between operations  16.2 us (3%)
    reduce_scatter x5, waiting for transfers between devices, per_device(): lax.psum_scatter(shortened(grad_sums[0:6]), 'dp', scatter_dimension=0, ti...  139 us
    psum x1, blocking collectives, per_device(): small_grads = lax.psum(grad_sums[6:15], ('dp', 'seq'))  62.5 us
    all_gather x1, waiting for transfers between devices, one_clip(): lax.all_gather(w_down, 'dp', axis=0, tiled=True)  45.9 us
    unnamed x14, waiting for transfers between devices  37.7 us
    psum x1, waiting for transfers between devices, one_clip(): lax.psum(matmul_nt(hidden, full_down).astype(jnp.bfloat16), 'head')  36.5 us
    psum x1, waiting for transfers between devices, one_clip(): lax.psum(matmul_nt(context, full_out).astype(jnp.bfloat16), 'head')  25.1 us
    all_gather x1, waiting for transfers between devices, one_clip(): lax.all_gather(w_up, 'dp', axis=0, tiled=True)  23.5 us
    reduce_scatter x1, waiting for transfers between devices, one_clip(): lax.psum_scatter(kv_terms.astype(jnp.bfloat16), 'seq', scatter_dimension=...  20.1 us
  transfers between devices with their start and end apart: 13, of which 12 were waited for; matrix products, arithmetic and copies ran while one was open for 6% of the time, Pallas kernels for 0%

commit v1 on v0

v1 whole, which is shorter than its diff:
```python
import jax
import jax.numpy as jnp
from jax import lax
from jax.sharding import PartitionSpec as P

HD = 64
NORM_EPS = 1e-05
SQRT_HALF = 0.7071067811865476
INV_ROOT_TWO_PI = 0.3989422804014327
BF = jnp.bfloat16
F32 = jnp.float32


def mm(a, b):
    return jnp.dot(a, b, preferred_element_type=F32)


def mm_nt(a, b):
    return lax.dot_general(a, b, (((1,), (1,)), ((), ())), preferred_element_type=F32)


def mm_tn(a, b):
    return lax.dot_general(a, b, (((0,), (0,)), ((), ())), preferred_element_type=F32)


def norm_parts(values):
    mean_val = jnp.mean(values, axis=-1, keepdims=True)
    centred = values - mean_val
    inverse = lax.rsqrt(jnp.mean(centred * centred, axis=-1, keepdims=True) + NORM_EPS)
    return centred * inverse, inverse


def norm_backward(grad_rows, normed, inverse, gain_vec):
    scaled = grad_rows * gain_vec
    return inverse * (
        scaled
        - jnp.mean(scaled, axis=-1, keepdims=True)
        - normed * jnp.mean(scaled * normed, axis=-1, keepdims=True)
    )


def after(value, *others):
    return lax.optimization_barrier((value, *others))[0]


def make_moves(mesh):
    n_dp, n_seq, n_head = mesh.shape["dp"], mesh.shape["seq"], mesh.shape["head"]

    def core(v):
        return lax.ppermute(v, "seq", [(i, i ^ 1) for i in range(n_seq)])

    def across(v):
        return lax.ppermute(v, "seq", [(i, i ^ 2) for i in range(n_seq)])

    def beside(v):
        return lax.ppermute(v, "head", [(i, i ^ 1) for i in range(n_head)])

    def corner(v):
        pairs = [
            (s * n_head + h, (s ^ 2) * n_head + (h ^ 1))
            for s in range(n_seq)
            for h in range(n_head)
        ]
        return lax.ppermute(v, ("seq", "head"), pairs)

    def along(v, k):
        return lax.ppermute(v, "dp", [(i, i ^ k) for i in range(n_dp)])

    return n_dp, core, across, beside, corner, along


def per_device(
    mesh,
    layer_in,
    cotangent,
    w_query,
    w_key,
    w_value,
    w_out,
    w_up,
    w_down,
    query_bias,
    value_bias,
    out_bias,
    up_bias,
    down_bias,
    attn_gain,
    attn_shift,
    mlp_gain,
    mlp_shift,
):
    n_dp, core, across, beside, corner, along = make_moves(mesh)
    own_z = lax.axis_index("dp")
    own_s = lax.axis_index("seq")
    own_y = lax.axis_index("head")
    own_x, own_c = own_s // 2, own_s % 2
    fr, width = layer_in.shape[1], layer_in.shape[2]
    quarter = fr // 2
    rows = width // n_dp
    half = rows // 2
    aw = w_query.shape[1] // 2
    fw = w_up.shape[1] // 2
    heads = aw // HD

    def rolled(a):
        return jnp.concatenate(
            [
                lax.dynamic_slice_in_dim(a, own_y * quarter, quarter, 0),
                lax.dynamic_slice_in_dim(a, (1 - own_y) * quarter, quarter, 0),
            ],
            axis=0,
        )

    def weight_cut(w, cols):
        return lax.dynamic_slice(w, (own_c * half, own_x * cols), (half, cols))

    def gathered(piece):
        pieces = [(own_z, piece)] + [(own_z ^ k, along(piece, k)) for k in range(1, n_dp)]
        buf = jnp.zeros((n_dp,) + piece.shape, piece.dtype)
        for at, part in pieces:
            buf = lax.dynamic_update_slice(buf, part[None], (at, 0, 0))
        return buf, pieces[-1][1]

    def merged(buf):
        other = core(buf)
        first = jnp.where(own_c == 0, buf, other)
        second = jnp.where(own_c == 0, other, buf)
        return jnp.stack([first, second], axis=1).reshape(width, buf.shape[2])

    attn_piece = jnp.concatenate(
        [weight_cut(w, aw) for w in (w_query, w_key, w_value, w_out)], axis=1
    )
    attn_buf, attn_last = gathered(attn_piece)
    mine = rolled(layer_in[0])
    rows_in = jnp.concatenate([mine, across(mine)], axis=0)
    inputs = rows_in.astype(F32)
    attn_normed, attn_inverse = norm_parts(inputs)
    attn_act = (attn_normed * attn_gain + attn_shift).astype(BF)
    act_all = jnp.concatenate([attn_act, core(attn_act)], axis=0)
    attn_full = merged(attn_buf)
    wq, wk, wv, wo = (attn_full[:, i * aw : (i + 1) * aw] for i in range(4))

    ff_piece = jnp.concatenate([weight_cut(w, fw) for w in (w_up, w_down)], axis=1)
    ff_piece = after(ff_piece, attn_last)
    ff_buf, _ = gathered(ff_piece)
    cot_mine = after(rolled(cotangent[0]), attn_last)
    cot = jnp.concatenate([cot_mine, across(cot_mine)], axis=0)

    q_bias = lax.dynamic_slice_in_dim(query_bias, own_x * aw, aw, 0)
    v_bias = lax.dynamic_slice_in_dim(value_bias, own_x * aw, aw, 0)
    u_bias = lax.dynamic_slice_in_dim(up_bias, own_x * fw, fw, 0)

    query = (mm(attn_act, wq) + q_bias).astype(BF)
    keys = mm(act_all, wk).astype(BF)
    values = (mm(act_all, wv) + v_bias).astype(BF)

    def head_of(a, h):
        return a[:, h * HD : (h + 1) * HD]

    context, log_total = [], []
    for h in range(heads):
        scores = 0.125 * mm_nt(head_of(query, h), head_of(keys, h))
        row_max = jnp.max(scores, axis=-1, keepdims=True)
        exp_scores = jnp.exp(scores - row_max)
        row_sum = jnp.sum(exp_scores, axis=-1, keepdims=True)
        log_total.append(row_max + jnp.log(row_sum))
        context.append((mm(exp_scores.astype(BF), head_of(values, h)) / row_sum).astype(BF))
    context = jnp.concatenate(context, axis=1)

    def part(a, i):
        return a[i * quarter : (i + 1) * quarter]

    def reduced(partial):
        got = [
            move(part(partial, i).astype(BF))
            for i, move in ((1, beside), (2, across), (3, corner))
        ]
        total = part(partial, 0)
        for g in got:
            total = total + g.astype(F32)
        return total

    def spread(own):
        return jnp.concatenate([own, beside(own), across(own), corner(own)], axis=0)

    def both(own):
        other = beside(own)
        return jnp.where(
            own_y == 0,
            jnp.concatenate([own, other], axis=0),
            jnp.concatenate([other, own], axis=0),
        )

    attn_out = reduced(mm_nt(context, wo))
    resid_mid = part(inputs, 0) + attn_out + out_bias
    mlp_normed, mlp_inverse = norm_parts(resid_mid)
    mlp_own = (mlp_normed * mlp_gain + mlp_shift).astype(BF)
    mlp_act = spread(mlp_own)

    ff_full = merged(ff_buf)
    wu, wd = ff_full[:, :fw], ff_full[:, fw:]
    pre_act = mm(mlp_act, wu) + u_bias
    cdf = 0.5 * (1.0 + jax.scipy.special.erf(pre_act * SQRT_HALF))
    hidden = (pre_act * cdf).astype(BF)
    slope = cdf + pre_act * INV_ROOT_TWO_PI * jnp.exp(-0.5 * pre_act * pre_act)
    d_pre = (mm(cot, wd) * slope).astype(BF)
    d_mlp_act = reduced(mm_nt(d_pre, wu))

    cot_own = part(cot, 0).astype(F32)
    d_mid = cot_own + norm_backward(d_mlp_act, mlp_normed, mlp_inverse, mlp_gain)
    d_mid_all = spread(d_mid.astype(BF))

    layer_out = both((resid_mid + reduced(mm_nt(hidden, wd)) + down_bias).astype(BF))

    def shard_sums(grad):
        cols = grad.shape[1]
        cut = grad.reshape(n_dp, 2, half, cols)
        keep = lax.dynamic_index_in_dim(cut, own_c, 1, keepdims=False)
        give = lax.dynamic_index_in_dim(cut, 1 - own_c, 1, keepdims=False).astype(BF)
        keep = keep + core(give).astype(F32)
        total = lax.dynamic_index_in_dim(keep, own_z, 0, keepdims=False)
        sent = [
            along(lax.dynamic_index_in_dim(keep, own_z ^ k, 0, keepdims=False).astype(BF), k)
            for k in range(1, n_dp)
        ]
        for got in sent:
            total = total + got.astype(F32)
        total = total.astype(BF)
        other = across(total)
        wide = jnp.stack(
            [jnp.where(own_x == 0, total, other), jnp.where(own_x == 0, other, total)], axis=0
        )
        other = core(wide)
        tall = jnp.concatenate(
            [jnp.where(own_c == 0, wide, other), jnp.where(own_c == 0, other, wide)], axis=1
        )
        return tall

    def shard_of(tall, at, cols):
        return jnp.concatenate(
            [tall[0, :, at : at + cols], tall[1, :, at : at + cols]], axis=1
        ).astype(F32)

    ff_shards = shard_sums(jnp.concatenate([mm_tn(mlp_act, d_pre), mm_tn(cot, hidden)], axis=1))
    grad_w_up, grad_w_down = shard_of(ff_shards, 0, fw), shard_of(ff_shards, fw, fw)

    def placed(vec, size):
        return lax.dynamic_update_slice_in_dim(
            jnp.zeros((size,), F32), vec, own_x * vec.shape[0], 0
        )

    def vector_sums(head_parts, whole_parts):
        vec = jnp.concatenate([*head_parts, *whole_parts])
        split = sum(p.shape[0] for p in head_parts)
        k = 1
        while k < n_dp:
            vec = vec + along(vec, k)
            k *= 2
        vec = vec + across(vec)
        vec = vec + core(vec)
        tail = vec[split:]
        tail = tail + beside(tail)
        return vec[:split], tail

    def rowsum(a):
        return jnp.sum(a, axis=0)

    up_sum, early = vector_sums(
        [placed(rowsum(d_pre.astype(F32)), 2 * fw)],
        [
            rowsum(cot_own),
            rowsum(d_mlp_act * mlp_normed),
            rowsum(d_mlp_act),
            rowsum(d_mid),
        ],
    )

    d_context = mm(d_mid_all, wo).astype(BF)
    d_query, d_key, d_value = [], [], []
    for h in range(heads):
        qh, kh, vh = head_of(query, h), head_of(keys, h), head_of(values, h)
        dch, ch = head_of(d_context, h), head_of(context, h)
        delta = jnp.sum(dch.astype(F32) * ch.astype(F32), axis=-1, keepdims=True)
        prob = jnp.exp(0.125 * mm_nt(qh, kh) - log_total[h])
        d_score = (0.125 * prob * (mm_nt(dch, vh) - delta)).astype(BF)
        d_query.append(mm(d_score, kh))
        d_key.append(mm_tn(d_score, qh))
        d_value.append(mm_tn(prob.astype(BF), dch))
    d_query = jnp.concatenate(d_query, axis=1)
    d_kv = jnp.concatenate(d_key + d_value, axis=1)
    own_rows = 2 * fr
    d_kv = d_kv[:own_rows] + core(d_kv[own_rows:].astype(BF)).astype(F32)
    query_round = d_query.astype(BF)
    kv_round = d_kv.astype(BF)
    key_round, value_round = kv_round[:, :aw], kv_round[:, aw:]
    attn_terms = mm_nt(query_round, wq) + mm_nt(key_round, wk) + mm_nt(value_round, wv)
    d_attn_act = reduced(attn_terms)
    grad_in = d_mid + norm_backward(
        d_attn_act, part(attn_normed, 0), part(attn_inverse, 0), attn_gain
    )
    grad_in = both(grad_in.astype(BF)).astype(F32)

    head_sums, late = vector_sums(
        [placed(rowsum(d_query), 2 * aw), placed(rowsum(d_kv[:, aw:]), 2 * aw)],
        [rowsum(attn_terms * attn_normed), rowsum(attn_terms)],
    )
    attn_shards = shard_sums(
        jnp.concatenate(
            [
                mm_tn(attn_act, query_round),
                mm_tn(attn_act, key_round),
                mm_tn(attn_act, value_round),
                mm_tn(d_mid_all, context),
            ],
            axis=1,
        )
    )
    grad_w_query, grad_w_key, grad_w_value, grad_w_out = (
        shard_of(attn_shards, i * aw, aw) for i in range(4)
    )
    return (
        layer_out[None],
        grad_in[None],
        grad_w_query,
        grad_w_key,
        grad_w_value,
        grad_w_out,
        grad_w_up,
        grad_w_down,
        head_sums[: 2 * aw],
        head_sums[2 * aw :],
        early[3 * width :],
        up_sum,
        early[:width],
        late[:width],
        late[width:],
        early[width : 2 * width],
        early[2 * width : 3 * width],
    )


def solution(mesh):
    square = P("dp", "head")
    acts = P("dp", "seq", None)
    return jax.shard_map(
        lambda *args: per_device(mesh, *args),
        mesh=mesh,
        in_specs=(acts,) * 2
        + (square,) * 6
        + (P("head"), P("head"), P(), P("head"), P(), P(), P(), P(), P()),
        out_specs=(acts,) * 2
        + (square,) * 6
        + (P("head"), P("head"), P(), P("head"), P(), P(), P(), P(), P()),
        check_vma=False,
    )
```

time: 622 us -> 267 us (0.43)
  waiting for transfers between devices: 346 us -> 102 us
  blocking collectives: 148 us -> 0 us
  starting transfers between devices: 0.94 us -> 66 us
  matrix products: 50.3 us -> 34.2 us
  between operations: 16.2 us -> 2.14 us
    reduce_scatter x6 -> x0, waiting for transfers between devices: 159 us -> none  [the longest x5 139 us: per_device(): lax.psum_scatter(shortened(grad_sums[0:6]), 'dp', scatter_dimension=0, ti...]
    ppermute x0 -> x54, waiting for transfers between devices: none -> 102 us  [the longest x16 55 us: along(): return lax.ppermute(v, 'dp', [(i, i ^ k) for i in range(n_dp)])]
    all_gather x6 -> x0, blocking collectives: 85.2 us -> none  [the longest x1 18.5 us: one_clip(): lax.all_gather(w_value, 'dp', axis=0, tiled=True)]
    psum x4 -> x0, waiting for transfers between devices: 80.2 us -> none  [the longest x1 36.5 us: one_clip(): lax.psum(matmul_nt(hidden, full_down).astype(jnp.bfloat16), 'head')]
    all_gather x2 -> x0, waiting for transfers between devices: 69.4 us -> none  [the longest x1 45.9 us: one_clip(): lax.all_gather(w_down, 'dp', axis=0, tiled=True)]
    ppermute x0 -> x54, starting transfers between devices: none -> 66 us  [the longest x16 32 us: along(): return lax.ppermute(v, 'dp', [(i, i ^ k) for i in range(n_dp)])]
    psum x1 -> x0, blocking collectives: 62.5 us -> none  [per_device(): small_grads = lax.psum(grad_sums[6:15], ('dp', 'seq'))]
    unnamed x14 -> x0, waiting for transfers between devices: 37.7 us -> none
  transfers between devices with their start and end apart: 13 -> 54, of which waited for: 12 -> 29; matrix products, arithmetic and copies ran while one was open for 6% -> 27% of each run, Pallas kernels for 0% -> 0%
where the time goes in v1:
time: 267 us; the launch traced here: 262 us
  waiting for transfers between devices  102 us (38%)
  starting transfers between devices  66 us (25%)
  matrix products  34.2 us (13%)
  local copies, waits for them, and re-layouts  29.7 us (11%)
  other arithmetic  27.7 us (10%)
    ppermute x16, waiting for transfers between devices, along(): return lax.ppermute(v, 'dp', [(i, i ^ k) for i in range(n_dp)])  55 us
    ppermute x16, starting transfers between devices, along(): return lax.ppermute(v, 'dp', [(i, i ^ k) for i in range(n_dp)])  32 us
    ppermute x6, waiting for transfers between devices, corner(): return lax.ppermute(v, ('seq', 'head'), pairs)  20.2 us
    dot_general x12, matrix products, mm_nt(): lax.dot_general(a, b, (((1,), (1,)), ((), ())), preferred_element_type=F32)  15.9 us
    ppermute x12, waiting for transfers between devices, across(): return lax.ppermute(v, 'seq', [(i, i ^ 2) for i in range(n_seq)])  15.3 us
    ppermute x12, starting transfers between devices, across(): return lax.ppermute(v, 'seq', [(i, i ^ 2) for i in range(n_seq)])  14.3 us
    ppermute x10, waiting for transfers between devices, beside(): return lax.ppermute(v, 'head', [(i, i ^ 1) for i in range(n_head)])  12 us
    ppermute x10, starting transfers between devices, beside(): return lax.ppermute(v, 'head', [(i, i ^ 1) for i in range(n_head)])  10.5 us
  transfers between devices with their start and end apart: 54, of which 29 were waited for; matrix products, arithmetic and copies ran while one was open for 27% of the time, Pallas kernels for 0%

profile of v1, /device:TPU:0, one launch (start us, length us, event | category | flops | bytes accessed | tf_op | source)
XLA Modules:
  0.0 262.2 jit_solution(6123369278468971591)
XLA Ops:
  4.9 3.1 %collective-permute-start.1 = (bf16[96,768]{1,0:T(8,128)(2,1)S(1)}, bf16[96,768]{1,0:T(8,128)(2,1)S(1)}, u32[]{:S(2)}, u32[]{:S(2)}) collective-permute-start(bf16[96,768]{1,0:T(8,128)(2,1)S(1)} %get-tuple-element.41), channel_id=1, source_target_pairs={{0,8},{8,0},{16,24},{24,16},{1,9},{9,1},{17,25},{25,17},{2,10},{10... | collective-permute-start | bytes 442376 | tf_op jit(solution)/shard_map/ppermute | solution.py:67
  8.0 2.6 collective-permute-start.2
  14.4 6.1 %collective-permute-done.3 = bf16[96,768]{1,0:T(8,128)(2,1)S(1)} collective-permute-done((bf16[96,768]{1,0:T(8,128)(2,1)S(1)}, bf16[96,768]{1,0:T(8,128)(2,1)S(1)}, u32[]{:S(2)}, u32[]{:S(2)}) %collective-permute-start.3) | collective-permute-done | bytes 147488 | tf_op jit(solution)/shard_map/ppermute | solution.py:67
  20.5 3.8 %collective-permute-start.12 = (bf16[96,1536]{1,0:T(8,128)(2,1)S(1)}, bf16[96,1536]{1,0:T(8,128)(2,1)S(1)}, u32[]{:S(2)}, u32[]{:S(2)}) collective-permute-start(bf16[96,1536]{1,0:T(8,128)(2,1)S(1)} %pad_maximum_fusion.15), channel_id=1, source_target_pairs={{0,8},{8,0},{16,24},{24,16},{1,9},{9,1},{17,25},{25,17},{2,10},{10... | collective-permute-start | bytes 884744 | tf_op jit(solution)/shard_map/ppermute | solution.py:67
  29.6 5.8 %collective-permute-done.12 = bf16[96,1536]{1,0:T(8,128)(2,1)S(1)} collective-permute-done((bf16[96,1536]{1,0:T(8,128)(2,1)S(1)}, bf16[96,1536]{1,0:T(8,128)(2,1)S(1)}, u32[]{:S(2)}, u32[]{:S(2)}) %collective-permute-start.12) | collective-permute-done | bytes 294944 | tf_op jit(solution)/shard_map/ppermute | solution.py:67
  35.4 12.3 %collective-permute-done.13 = bf16[96,1536]{1,0:T(8,128)(2,1)S(1)} collective-permute-done((bf16[96,1536]{1,0:T(8,128)(2,1)S(1)}, bf16[96,1536]{1,0:T(8,128)(2,1)S(1)}, u32[]{:S(2)}, u32[]{:S(2)}) %collective-permute-start.13) | collective-permute-done | bytes 294944 | tf_op jit(solution)/shard_map/ppermute | solution.py:67
  60.3 3.2 %collective-permute-done.6 = bf16[128,768]{1,0:T(8,128)(2,1)S(1)} collective-permute-done((bf16[128,768]{1,0:T(8,128)(2,1)S(1)}, bf16[128,768]{1,0:T(8,128)(2,1)S(1)}, u32[]{:S(2)}, u32[]{:S(2)}) %collective-permute-start.6) | collective-permute-done | bytes 196640 | tf_op jit(solution)/shard_map/ppermute | solution.py:56
  65.6 3.4 %collective-permute-done.8 = bf16[128,768]{1,0:T(8,128)(2,1)S(1)} collective-permute-done((bf16[128,768]{1,0:T(8,128)(2,1)S(1)}, bf16[128,768]{1,0:T(8,128)(2,1)S(1)}, u32[]{:S(2)}, u32[]{:S(2)}) %collective-permute-start.8) | collective-permute-done | bytes 196640 | tf_op jit(solution)/shard_map/ppermute | solution.py:64
  74.0 3.9 %collective-permute-done.10 = bf16[128,768]{1,0:T(8,128)(2,1)S(1)} collective-permute-done((bf16[128,768]{1,0:T(8,128)(2,1)S(1)}, bf16[128,768]{1,0:T(8,128)(2,1)S(1)}, u32[]{:S(2)}, u32[]{:S(2)}) %collective-permute-start.10) | collective-permute-done | bytes 196640 | tf_op jit(solution)/shard_map/ppermute | solution.py:53
  77.9 3.6 %collective-permute-done.11 = bf16[128,768]{1,0:T(8,128)(2,1)S(1)} collective-permute-done((bf16[128,768]{1,0:T(8,128)(2,1)S(1)}, bf16[128,768]{1,0:T(8,128)(2,1)S(1)}, u32[]{:S(2)}, u32[]{:S(2)}) %collective-permute-start.11) | collective-permute-done | bytes 196640 | tf_op jit(solution)/shard_map/ppermute | solution.py:64
  101.3 3.1 %collective-permute-done.23 = bf16[128,768]{1,0:T(8,128)(2,1)} collective-permute-done((bf16[128,768]{1,0:T(8,128)(2,1)}, bf16[128,768]{1,0:T(8,128)(2,1)}, u32[]{:S(2)}, u32[]{:S(2)}) %collective-permute-start.23) | collective-permute-done | bytes 196640 | tf_op jit(solution)/shard_map/ppermute | solution.py:64
  110.9 4.4 %collective-permute-start.48 = (f32[4608]{0:T(1024)S(1)}, f32[4608]{0:T(1024)S(1)}, u32[]{:S(2)}, u32[]{:S(2)}) collective-permute-start(f32[4608]{0:T(1024)S(1)} %constant_dynamic-update-slice_fusion.3), channel_id=1, source_target_pairs={{0,8},{8,0},{16,24},{24,16},{1,9},{9,1},{17,25},{25,17},{2,10},{10... | collective-permute-start | bytes 55304 | tf_op jit(solution)/shard_map/ppermute | solution.py:67
  117.1 3.3 %collective-permute-start.49 = (f32[4608]{0:T(1024)S(1)}, f32[4608]{0:T(1024)S(1)}, u32[]{:S(2)}, u32[]{:S(2)}) collective-permute-start(f32[4608]{0:T(1024)S(1)} %add.368), channel_id=1, source_target_pairs={{0,16},{8,24},{16,0},{24,8},{1,17},{9,25},{17,1},{25,9},{2,18},{10... | collective-permute-start | bytes 55304 | tf_op jit(solution)/shard_map/ppermute | solution.py:67
  129.0 6.0 %copy.41 = f32[768,1536]{1,0:T(8,128)} copy(f32[768,1536]{0,1:T(8,128)} %pad_maximum_fusion) | data formatting | bytes 9437184 | tf_op jit(solution)/shard_map/concatenate | solution.py:244
  136.4 2.8 %fusion.15 = bf16[4,96,1536]{2,1,0:T(8,128)(2,1)} fusion(f32[4,2,96,1536]{3,2,1,0:T(8,128)} %bitcast.128, s32[]{:T(128)S(6)} %select_n.200), kind=kLoop, calls=%fused_computation.58 | loop fusion | bytes 2359300 | tf_op jit(solution)/shard_map/convert_element_type | solution.py:219
  148.9 3.3 %collective-permute-done.26 = bf16[128,768]{1,0:T(8,128)(2,1)S(1)} collective-permute-done((bf16[128,768]{1,0:T(8,128)(2,1)S(1)}, bf16[128,768]{1,0:T(8,128)(2,1)S(1)}, u32[]{:S(2)}, u32[]{:S(2)}) %collective-permute-start.26) | collective-permute-done | bytes 196640 | tf_op jit(solution)/shard_map/ppermute | solution.py:64
  173.9 4.6 %multiply_reduce_fusion = (f32[768]{0:T(1024)S(1)}, f32[768]{0:T(1024)S(1)}, bf16[512,768]{1,0:T(8,128)(2,1)}, f32[512,768]{1,0:T(8,128)}, f32[512,768]{1,0:T(8,128)}) fusion(f32[512]{0:T(512)S(1)} %copy-done.53, f32[512]{0:T(512)S(1)} %broadcast_multiply_fusion, bf16[256,768]{1,0:T(8,128)(2,1)S(1)} %collective-permute-done, ...), kind=kOutput, calls=%fused_computation.34 | convolution fusion | flops 156498432 | bytes 8464384 | tf_op jit(solution)/shard_map/dot_general | solution.py:19
  182.3 3.0 %collective-permute-start.45 = (f32[2304]{0:T(1024)S(1)}, f32[2304]{0:T(1024)S(1)}, u32[]{:S(2)}, u32[]{:S(2)}) collective-permute-start(f32[2304]{0:T(1024)S(1)} %fusion.143), channel_id=1, source_target_pairs={{0,16},{8,24},{16,0},{24,8},{1,17},{9,25},{17,1},{25,9},{2,18},{10... | collective-permute-start | bytes 27656 | tf_op jit(solution)/shard_map/ppermute | solution.py:67
  196.2 3.7 %collective-permute-done.53 = f32[1536]{0:T(1024)S(1)} collective-permute-done((f32[1536]{0:T(1024)S(1)}, f32[1536]{0:T(1024)S(1)}, u32[]{:S(2)}, u32[]{:S(2)}) %collective-permute-start.53) | collective-permute-done | bytes 6176 | tf_op jit(solution)/shard_map/ppermute | solution.py:56
  202.6 4.7 %collective-permute-done.30 = bf16[128,768]{1,0:T(8,128)(2,1)S(1)} collective-permute-done((bf16[128,768]{1,0:T(8,128)(2,1)S(1)}, bf16[128,768]{1,0:T(8,128)(2,1)S(1)}, u32[]{:S(2)}, u32[]{:S(2)}) %collective-permute-start.30) | collective-permute-done | bytes 196640 | tf_op jit(solution)/shard_map/ppermute | solution.py:64
  223.6 2.6 collective-permute-done.34
  229.0 3.3 %collective-permute-done.39 = bf16[96,1536]{1,0:T(8,128)(2,1)S(1)} collective-permute-done((bf16[96,1536]{1,0:T(8,128)(2,1)S(1)}, bf16[96,1536]{1,0:T(8,128)(2,1)S(1)}, u32[]{:S(2)}, u32[]{:S(2)}) %collective-permute-start.39) | collective-permute-done | bytes 294944 | tf_op jit(solution)/shard_map/ppermute | solution.py:67
  232.3 16.8 %collective-permute-done.40 = bf16[96,1536]{1,0:T(8,128)(2,1)S(1)} collective-permute-done((bf16[96,1536]{1,0:T(8,128)(2,1)S(1)}, bf16[96,1536]{1,0:T(8,128)(2,1)S(1)}, u32[]{:S(2)}, u32[]{:S(2)}) %collective-permute-start.40) | collective-permute-done | bytes 294944 | tf_op jit(solution)/shard_map/ppermute | solution.py:67
  250.6 5.4 %collective-permute-done.42 = bf16[96,1536]{1,0:T(8,128)(2,1)S(1)} collective-permute-done((bf16[96,1536]{1,0:T(8,128)(2,1)S(1)}, bf16[96,1536]{1,0:T(8,128)(2,1)S(1)}, u32[]{:S(2)}, u32[]{:S(2)}) %collective-permute-start.42) | collective-permute-done | bytes 294944 | tf_op jit(solution)/shard_map/ppermute | solution.py:53
  (399 shorter events, 145.2 us)
Async XLA Ops:
  4.9 20.4 %collective-permute-start.1 = (bf16[96,768]{1,0:T(8,128)(2,1)S(1)}, bf16[96,768]{1,0:T(8,128)(2,1)S(1)}, u32[]{:S(2)}, u32[]{:S(2)}) collective-permute-start(bf16[96,768]{1,0:T(8,128)(2,1)S(1)} %get-tuple-element.41), channel_id=1, source_target_pairs={{0,8},{8,0},{16,24},{24,16},{1,9},{9,1},{17,25},{25,17},{2,10},{10... | collective-permute-start | bytes 442376 | tf_op jit(solution)/shard_map/ppermute | solution.py:67
  8.0 18.8 %collective-permute-start.2 = (bf16[96,768]{1,0:T(8,128)(2,1)S(1)}, bf16[96,768]{1,0:T(8,128)(2,1)S(1)}, u32[]{:S(2)}, u32[]{:S(2)}) collective-permute-start(bf16[96,768]{1,0:T(8,128)(2,1)S(1)} %get-tuple-element.41), channel_id=1, source_target_pairs={{0,16},{8,24},{16,0},{24,8},{1,17},{9,25},{17,1},{25,9},{2,18},{10... | collective-permute-start | bytes 442376 | tf_op jit(solution)/shard_map/ppermute | solution.py:67
  10.8 17.5 %collective-permute-start = (bf16[256,768]{1,0:T(8,128)(2,1)S(1)}, bf16[256,768]{1,0:T(8,128)(2,1)S(1)}, u32[]{:S(2)}, u32[]{:S(2)}) collective-permute-start(bf16[256,768]{1,0:T(8,128)(2,1)S(1)} %pad_maximum_fusion.11), channel_id=1, source_target_pairs={{0,4},{2,6},{4,0},{6,2},{1,5},{3,7},{5,1},{7,3},{8,12},{10,14},{12... | collective-permute-start | bytes 1179656 | tf_op jit(solution)/shard_map/ppermute | solution.py:53
  20.5 14.9 %collective-permute-start.12 = (bf16[96,1536]{1,0:T(8,128)(2,1)S(1)}, bf16[96,1536]{1,0:T(8,128)(2,1)S(1)}, u32[]{:S(2)}, u32[]{:S(2)}) collective-permute-start(bf16[96,1536]{1,0:T(8,128)(2,1)S(1)} %pad_maximum_fusion.15), channel_id=1, source_target_pairs={{0,8},{8,0},{16,24},{24,16},{1,9},{9,1},{17,25},{25,17},{2,10},{10... | collective-permute-start | bytes 884744 | tf_op jit(solution)/shard_map/ppermute | solution.py:67
  24.3 23.4 %collective-permute-start.13 = (bf16[96,1536]{1,0:T(8,128)(2,1)S(1)}, bf16[96,1536]{1,0:T(8,128)(2,1)S(1)}, u32[]{:S(2)}, u32[]{:S(2)}) collective-permute-start(bf16[96,1536]{1,0:T(8,128)(2,1)S(1)} %pad_maximum_fusion.15), channel_id=1, source_target_pairs={{0,16},{8,24},{16,0},{24,8},{1,17},{9,25},{17,1},{25,9},{2,18},{10... | collective-permute-start | bytes 884744 | tf_op jit(solution)/shard_map/ppermute | solution.py:67
  25.3 22.4 %collective-permute-start.14 = (bf16[96,1536]{1,0:T(8,128)(2,1)S(1)}, bf16[96,1536]{1,0:T(8,128)(2,1)S(1)}, u32[]{:S(2)}, u32[]{:S(2)}) collective-permute-start(bf16[96,1536]{1,0:T(8,128)(2,1)S(1)} %pad_maximum_fusion.15), channel_id=1, source_target_pairs={{0,24},{8,16},{16,8},{24,0},{1,25},{9,17},{17,9},{25,1},{2,26},{10... | collective-permute-start | bytes 884744 | tf_op jit(solution)/shard_map/ppermute | solution.py:67
  26.9 21.0 %collective-permute-start.20 = (bf16[256,768]{1,0:T(8,128)(2,1)S(1)}, bf16[256,768]{1,0:T(8,128)(2,1)S(1)}, u32[]{:S(2)}, u32[]{:S(2)}) collective-permute-start(bf16[256,768]{1,0:T(8,128)(2,1)S(1)} %pad_maximum_fusion.12), channel_id=1, source_target_pairs={{0,4},{2,6},{4,0},{6,2},{1,5},{3,7},{5,1},{7,3},{8,12},{10,14},{12... | collective-permute-start | bytes 1179656 | tf_op jit(solution)/shard_map/ppermute | solution.py:53
  28.3 19.7 %collective-permute-start.4 = (bf16[4,96,768]{2,1,0:T(8,128)(2,1)S(1)}, bf16[4,96,768]{2,1,0:T(8,128)(2,1)S(1)}, u32[]{:S(2)}, u32[]{:S(2)}) collective-permute-start(bf16[4,96,768]{2,1,0:T(8,128)(2,1)S(1)} %bitcast_dynamic-update-slice_fusion.4), channel_id=1, source_target_pairs={{0,2},{2,0},{4,6},{6,4},{1,3},{3,1},{5,7},{7,5},{8,10},{10,8},{12,... | collective-permute-start | bytes 1769480 | tf_op jit(solution)/shard_map/ppermute | solution.py:50
  35.4 13.3 %collective-permute-start.5 = (bf16[512,768]{1,0:T(8,128)(2,1)S(1)}, bf16[512,768]{1,0:T(8,128)(2,1)S(1)}, u32[]{:S(2)}, u32[]{:S(2)}) collective-permute-start(bf16[512,768]{1,0:T(8,128)(2,1)S(1)} %add_convert_fusion), channel_id=1, source_target_pairs={{0,2},{2,0},{4,6},{6,4},{1,3},{3,1},{5,7},{7,5},{8,10},{10,8},{12,... | collective-permute-start | bytes 2359304 | tf_op jit(solution)/shard_map/ppermute | solution.py:50
  47.8 25.8 %collective-permute-start.15 = (bf16[4,96,1536]{2,1,0:T(8,128)(2,1)S(1)}, bf16[4,96,1536]{2,1,0:T(8,128)(2,1)S(1)}, u32[]{:S(2)}, u32[]{:S(2)}) collective-permute-start(bf16[4,96,1536]{2,1,0:T(8,128)(2,1)S(1)} %bitcast_dynamic-update-slice_fusion), channel_id=1, source_target_pairs={{0,2},{2,0},{4,6},{6,4},{1,3},{3,1},{5,7},{7,5},{8,10},{10,8},{12,... | collective-permute-start | bytes 3538952 | tf_op jit(solution)/shard_map/ppermute | solution.py:50
  71.3 10.3 %collective-permute-start.11 = (bf16[128,768]{1,0:T(8,128)(2,1)S(1)}, bf16[128,768]{1,0:T(8,128)(2,1)S(1)}, u32[]{:S(2)}, u32[]{:S(2)}) collective-permute-start(bf16[128,768]{1,0:T(8,128)(2,1)S(1)} %add_convert_fusion.2), channel_id=1, source_target_pairs={{0,5},{1,4},{2,7},{3,6},{4,1},{5,0},{6,3},{7,2},{8,13},{9,12},{10,... | collective-permute-start | bytes 589832 | tf_op jit(solution)/shard_map/ppermute | solution.py:64
  92.2 12.2 %collective-permute-start.23 = (bf16[128,768]{1,0:T(8,128)(2,1)}, bf16[128,768]{1,0:T(8,128)(2,1)}, u32[]{:S(2)}, u32[]{:S(2)}) collective-permute-start(bf16[128,768]{1,0:T(8,128)(2,1)} %get-tuple-element.64), channel_id=1, source_target_pairs={{0,5},{1,4},{2,7},{3,6},{4,1},{5,0},{6,3},{7,2},{8,13},{9,12},{10,... | collective-permute-start | bytes 589832 | tf_op jit(solution)/shard_map/ppermute | solution.py:64
  94.8 11.6 %collective-permute-start.16 = (bf16[128,768]{1,0:T(8,128)(2,1)}, bf16[128,768]{1,0:T(8,128)(2,1)}, u32[]{:S(2)}, u32[]{:S(2)}) collective-permute-start(bf16[128,768]{1,0:T(8,128)(2,1)} %get-tuple-element.66), channel_id=1, source_target_pairs={{0,1},{1,0},{2,3},{3,2},{4,5},{5,4},{6,7},{7,6},{8,9},{9,8},{10,11... | collective-permute-start | bytes 589832 | tf_op jit(solution)/shard_map/ppermute | solution.py:56
  95.3 11.1 %collective-permute-start.17 = (bf16[128,768]{1,0:T(8,128)(2,1)}, bf16[128,768]{1,0:T(8,128)(2,1)}, u32[]{:S(2)}, u32[]{:S(2)}) collective-permute-start(bf16[128,768]{1,0:T(8,128)(2,1)} %get-tuple-element.68), channel_id=1, source_target_pairs={{0,4},{2,6},{4,0},{6,2},{1,5},{3,7},{5,1},{7,3},{8,12},{10,14},{12... | collective-permute-start | bytes 589832 | tf_op jit(solution)/shard_map/ppermute | solution.py:53
  139.2 71.0 %collective-permute-start.38 = (bf16[4,96,1536]{2,1,0:T(8,128)(2,1)}, bf16[4,96,1536]{2,1,0:T(8,128)(2,1)}, u32[]{:S(2)}, u32[]{:S(2)}) collective-permute-start(bf16[4,96,1536]{2,1,0:T(8,128)(2,1)} %fusion.15), channel_id=1, source_target_pairs={{0,2},{2,0},{4,6},{6,4},{1,3},{3,1},{5,7},{7,5},{8,10},{10,8},{12,... | collective-permute-start | bytes 3538952 | tf_op jit(solution)/shard_map/ppermute | solution.py:50
  143.7 21.9 %collective-permute-start.19 = (bf16[128,768]{1,0:T(8,128)(2,1)}, bf16[128,768]{1,0:T(8,128)(2,1)}, u32[]{:S(2)}, u32[]{:S(2)}) collective-permute-start(bf16[128,768]{1,0:T(8,128)(2,1)} %get-tuple-element.85), channel_id=1, source_target_pairs={{0,1},{1,0},{2,3},{3,2},{4,5},{5,4},{6,7},{7,6},{8,9},{9,8},{10,11... | collective-permute-start | bytes 589832 | tf_op jit(solution)/shard_map/ppermute | solution.py:56
  190.0 22.6 %collective-permute-start.32 = (bf16[4,96,768]{2,1,0:T(8,128)(2,1)S(1)}, bf16[4,96,768]{2,1,0:T(8,128)(2,1)S(1)}, u32[]{:S(2)}, u32[]{:S(2)}) collective-permute-start(bf16[4,96,768]{2,1,0:T(8,128)(2,1)S(1)} %fusion.38), channel_id=1, source_target_pairs={{0,2},{2,0},{4,6},{6,4},{1,3},{3,1},{5,7},{7,5},{8,10},{10,8},{12,... | collective-permute-start | bytes 1769480 | tf_op jit(solution)/shard_map/ppermute | solution.py:50
  192.3 10.3 %collective-permute-start.28 = (bf16[128,768]{1,0:T(8,128)(2,1)S(1)}, bf16[128,768]{1,0:T(8,128)(2,1)S(1)}, u32[]{:S(2)}, u32[]{:S(2)}) collective-permute-start(bf16[128,768]{1,0:T(8,128)(2,1)S(1)} %get-tuple-element.60), channel_id=1, source_target_pairs={{0,1},{1,0},{2,3},{3,2},{4,5},{5,4},{6,7},{7,6},{8,9},{9,8},{10,11... | collective-permute-start | bytes 589832 | tf_op jit(solution)/shard_map/ppermute | solution.py:56
  214.1 12.2 %collective-permute-start.34 = (bf16[96,768]{1,0:T(8,128)(2,1)S(1)}, bf16[96,768]{1,0:T(8,128)(2,1)S(1)}, u32[]{:S(2)}, u32[]{:S(2)}) collective-permute-start(bf16[96,768]{1,0:T(8,128)(2,1)S(1)} %get-tuple-element.56), channel_id=1, source_target_pairs={{0,16},{8,24},{16,0},{24,8},{1,17},{9,25},{17,1},{25,9},{2,18},{10... | collective-permute-start | bytes 442376 | tf_op jit(solution)/shard_map/ppermute | solution.py:67
  215.3 12.4 %collective-permute-start.35 = (bf16[96,768]{1,0:T(8,128)(2,1)S(1)}, bf16[96,768]{1,0:T(8,128)(2,1)S(1)}, u32[]{:S(2)}, u32[]{:S(2)}) collective-permute-start(bf16[96,768]{1,0:T(8,128)(2,1)S(1)} %get-tuple-element.55), channel_id=1, source_target_pairs={{0,24},{8,16},{16,8},{24,0},{1,25},{9,17},{17,9},{25,1},{2,26},{10... | collective-permute-start | bytes 442376 | tf_op jit(solution)/shard_map/ppermute | solution.py:67
  217.3 15.0 %collective-permute-start.39 = (bf16[96,1536]{1,0:T(8,128)(2,1)S(1)}, bf16[96,1536]{1,0:T(8,128)(2,1)S(1)}, u32[]{:S(2)}, u32[]{:S(2)}) collective-permute-start(bf16[96,1536]{1,0:T(8,128)(2,1)S(1)} %get-tuple-element.42), channel_id=1, source_target_pairs={{0,8},{8,0},{16,24},{24,16},{1,9},{9,1},{17,25},{25,17},{2,10},{10... | collective-permute-start | bytes 884744 | tf_op jit(solution)/shard_map/ppermute | solution.py:67
  217.7 31.4 %collective-permute-start.40 = (bf16[96,1536]{1,0:T(8,128)(2,1)S(1)}, bf16[96,1536]{1,0:T(8,128)(2,1)S(1)}, u32[]{:S(2)}, u32[]{:S(2)}) collective-permute-start(bf16[96,1536]{1,0:T(8,128)(2,1)S(1)} %get-tuple-element.44), channel_id=1, source_target_pairs={{0,16},{8,24},{16,0},{24,8},{1,17},{9,25},{17,1},{25,9},{2,18},{10... | collective-permute-start | bytes 884744 | tf_op jit(solution)/shard_map/ppermute | solution.py:67
  222.2 26.9 %collective-permute-start.41 = (bf16[96,1536]{1,0:T(8,128)(2,1)S(1)}, bf16[96,1536]{1,0:T(8,128)(2,1)S(1)}, u32[]{:S(2)}, u32[]{:S(2)}) collective-permute-start(bf16[96,1536]{1,0:T(8,128)(2,1)S(1)} %get-tuple-element.43), channel_id=1, source_target_pairs={{0,24},{8,16},{16,8},{24,0},{1,25},{9,17},{17,9},{25,1},{2,26},{10... | collective-permute-start | bytes 884744 | tf_op jit(solution)/shard_map/ppermute | solution.py:67
  227.8 22.6 %collective-permute-start.36 = (bf16[96,768]{1,0:T(8,128)(2,1)S(1)}, bf16[96,768]{1,0:T(8,128)(2,1)S(1)}, u32[]{:S(2)}, u32[]{:S(2)}) collective-permute-start(bf16[96,768]{1,0:T(8,128)(2,1)S(1)} %fusion.80), channel_id=1, source_target_pairs={{0,4},{2,6},{4,0},{6,2},{1,5},{3,7},{5,1},{7,3},{8,12},{10,14},{12... | collective-permute-start | bytes 442376 | tf_op jit(solution)/shard_map/ppermute | solution.py:53
  (109 other events, 751.3 us)

commit v2 on v1

v2 whole, which is shorter than its diff:
```python
import jax
import jax.numpy as jnp
from jax import lax
from jax.experimental import pallas as pl
from jax.experimental.pallas import tpu as pltpu
from jax.sharding import PartitionSpec as P


HD = 64
NORM_EPS = 1e-05
SQRT_HALF = 0.7071067811865476
INV_ROOT_TWO_PI = 0.3989422804014327
BF = jnp.bfloat16
F32 = jnp.float32


def mm(a, b):
    return jnp.dot(a, b, preferred_element_type=F32)


def mm_nt(a, b):
    return lax.dot_general(a, b, (((1,), (1,)), ((), ())), preferred_element_type=F32)


def mm_tn(a, b):
    return lax.dot_general(a, b, (((0,), (0,)), ((), ())), preferred_element_type=F32)


def norm_parts(values):
    mean_val = jnp.mean(values, axis=-1, keepdims=True)
    centred = values - mean_val
    inverse = lax.rsqrt(jnp.mean(centred * centred, axis=-1, keepdims=True) + NORM_EPS)
    return centred * inverse, inverse


def norm_backward(grad_rows, normed, inverse, gain_vec):
    scaled = grad_rows * gain_vec
    return inverse * (
        scaled
        - jnp.mean(scaled, axis=-1, keepdims=True)
        - normed * jnp.mean(scaled * normed, axis=-1, keepdims=True)
    )


def after(value, *others):
    return lax.optimization_barrier((value, *others))[0]


MIB = 1024 * 1024
VM = pl.BlockSpec(memory_space=pltpu.VMEM)


def assemble(pieces):
    n, (rows, cols) = len(pieces), pieces[0].shape

    def kernel(*refs):
        own = lax.axis_index("dp")
        for k in range(n):
            at = pl.multiple_of(jnp.bitwise_xor(own, k) * rows, rows)
            refs[n][pl.ds(at, rows), :] = refs[k][...]

    return pl.pallas_call(
        kernel,
        out_shape=jax.ShapeDtypeStruct((n * rows, cols), pieces[0].dtype),
        in_specs=[VM] * n,
        out_specs=VM,
        cost_estimate=pl.CostEstimate(
            flops=0, transcendentals=0, bytes_accessed=4 * n * rows * cols
        ),
        compiler_params=pltpu.CompilerParams(vmem_limit_bytes=8 * MIB),
        name="assemble",
    )(*pieces)


def finish(wide, other, count):
    rows, cols = wide.shape[1], wide.shape[2] // count

    def kernel(mine_ref, other_ref, *outs):
        own_c = lax.rem(lax.axis_index("seq"), 2)

        def put(first, second):
            for m, src in enumerate((first, second)):
                for i in range(count):
                    for x in range(2):
                        outs[m * count + i][:, x * cols : (x + 1) * cols] = src[
                            x, :, i * cols : (i + 1) * cols
                        ].astype(F32)

        @pl.when(own_c == 0)
        def _():
            put(mine_ref, other_ref)

        @pl.when(own_c == 1)
        def _():
            put(other_ref, mine_ref)

    return pl.pallas_call(
        kernel,
        out_shape=[jax.ShapeDtypeStruct((rows, 2 * cols), F32)] * (2 * count),
        in_specs=[VM] * 2,
        out_specs=[VM] * (2 * count),
        cost_estimate=pl.CostEstimate(
            flops=0, transcendentals=0, bytes_accessed=24 * rows * cols * count
        ),
        compiler_params=pltpu.CompilerParams(vmem_limit_bytes=8 * MIB),
        name="finish",
    )(wide, other)


def attention_front(query, own_kv, other_kv, width):
    rows = query.shape[0]
    block = rows // 2

    def kernel(q_ref, own_ref, oth_ref, c_ref, lt_ref):
        c_ref[:, :width] = jnp.zeros((rows, width), BF)
        for h in range(width // HD):
            cols = slice(h * HD, (h + 1) * HD)
            late = slice(width + h * HD, width + (h + 1) * HD)
            for at in range(0, rows, block):
                qh = q_ref[at : at + block, cols]
                first = 0.125 * mm_nt(qh, own_ref[:, cols])
                second = 0.125 * mm_nt(qh, oth_ref[:, cols])
                row_max = jnp.maximum(
                    jnp.max(first, axis=-1, keepdims=True), jnp.max(second, axis=-1, keepdims=True)
                )
                first = jnp.exp(first - row_max)
                second = jnp.exp(second - row_max)
                row_sum = jnp.sum(first, axis=-1, keepdims=True) + jnp.sum(
                    second, axis=-1, keepdims=True
                )
                total = mm(first.astype(BF), own_ref[:, late]) + mm(
                    second.astype(BF), oth_ref[:, late]
                )
                c_ref[at : at + block, late] = (total / row_sum).astype(BF)
                lt_ref[at : at + block, h : h + 1] = row_max + jnp.log(row_sum)

    return pl.pallas_call(
        kernel,
        out_shape=[
            jax.ShapeDtypeStruct((rows, 2 * width), BF),
            jax.ShapeDtypeStruct((rows, 128), F32),
        ],
        in_specs=[VM] * 3,
        out_specs=[VM] * 2,
        cost_estimate=pl.CostEstimate(
            flops=8 * rows * rows * width,
            transcendentals=2 * rows * rows * (width // HD),
            bytes_accessed=12 * rows * width,
        ),
        compiler_params=pltpu.CompilerParams(vmem_limit_bytes=24 * MIB),
        name="attention_front",
    )(query, own_kv, other_kv)


def attention_back(query, own_kv, other_kv, context, d_context, log_total, width):
    rows = query.shape[0]

    def kernel(
        q_ref, own_ref, oth_ref, c_ref, dc_ref, lt_ref, dq_ref, down_ref, doth_ref, qs_ref, vs_ref
    ):
        dq_ref[:, width:] = jnp.zeros((rows, width), BF)
        for h in range(width // HD):
            cols = slice(h * HD, (h + 1) * HD)
            late = slice(width + h * HD, width + (h + 1) * HD)
            qh, ch, dch = q_ref[:, cols], c_ref[:, late], dc_ref[:, late]
            delta = jnp.sum(dch.astype(F32) * ch.astype(F32), axis=-1, keepdims=True)
            total = lt_ref[:, h : h + 1]
            d_query = jnp.zeros((rows, HD), F32)
            sums = jnp.zeros((1, HD), F32)
            for src, out in ((own_ref, down_ref), (oth_ref, doth_ref)):
                kh, vh = src[:, cols], src[:, late]
                prob = jnp.exp(0.125 * mm_nt(qh, kh) - total)
                d_score = (0.125 * prob * (mm_nt(dch, vh) - delta)).astype(BF)
                d_query = d_query + mm(d_score, kh)
                out[:, cols] = mm_tn(d_score, qh).astype(out.dtype)
                d_value = mm_tn(prob.astype(BF), dch)
                out[:, late] = d_value.astype(out.dtype)
                sums = sums + jnp.sum(d_value, axis=0, keepdims=True)
            dq_ref[:, cols] = d_query.astype(BF)
            qs_ref[:, cols] = jnp.sum(d_query, axis=0, keepdims=True)
            vs_ref[:, cols] = sums

    return pl.pallas_call(
        kernel,
        out_shape=[
            jax.ShapeDtypeStruct((rows, 2 * width), BF),
            jax.ShapeDtypeStruct((rows, 2 * width), F32),
            jax.ShapeDtypeStruct((rows, 2 * width), BF),
            jax.ShapeDtypeStruct((1, width), F32),
            jax.ShapeDtypeStruct((1, width), F32),
        ],
        in_specs=[VM] * 6,
        out_specs=[VM] * 5,
        cost_estimate=pl.CostEstimate(
            flops=20 * rows * rows * width,
            transcendentals=2 * rows * rows * (width // HD),
            bytes_accessed=20 * rows * width,
        ),
        compiler_params=pltpu.CompilerParams(vmem_limit_bytes=24 * MIB),
        name="attention_back",
    )(query, own_kv, other_kv, context, d_context, log_total)


def quarters(pairs, normed=None):
    rows, width = pairs[0][0].shape[0], pairs[0][1].shape[0]
    quarter = rows // 4
    n = len(pairs)
    extra = [] if normed is None else [normed]

    def kernel(*refs):
        outs = refs[2 * n + len(extra) :]
        for i in range(4):
            at = slice(i * quarter, (i + 1) * quarter)
            total = mm_nt(refs[0][at, :], refs[1][...])
            for p in range(1, n):
                total = total + mm_nt(refs[2 * p][at, :], refs[2 * p + 1][...])
            outs[i][...] = total.astype(outs[i].dtype)
            if extra:
                gain_sum = jnp.sum(total * refs[2 * n][at, :], axis=0, keepdims=True)
                shift_sum = jnp.sum(total, axis=0, keepdims=True)
                if i == 0:
                    outs[4][...] = gain_sum
                    outs[5][...] = shift_sum
                else:
                    outs[4][...] += gain_sum
                    outs[5][...] += shift_sum

    return pl.pallas_call(
        kernel,
        out_shape=[jax.ShapeDtypeStruct((quarter, width), F32)]
        + [jax.ShapeDtypeStruct((quarter, width), BF)] * 3
        + [jax.ShapeDtypeStruct((1, width), F32)] * (2 * len(extra)),
        in_specs=[VM] * (2 * n + len(extra)),
        out_specs=[VM] * (4 + 2 * len(extra)),
        cost_estimate=pl.CostEstimate(
            flops=2 * n * rows * width * pairs[0][0].shape[1],
            transcendentals=0,
            bytes_accessed=4 * rows * width,
        ),
        compiler_params=pltpu.CompilerParams(vmem_limit_bytes=16 * MIB),
        name="quarters",
    )(*[a for pair in pairs for a in pair], *extra)


def norm_middle(own, others, rows_in, bias, gain, shift):
    def kernel(own_ref, a_ref, b_ref, c_ref, in_ref, bias_ref, gain_ref, shift_ref, mid_ref, act_ref):
        total = own_ref[...] + a_ref[...].astype(F32)
        total = total + b_ref[...].astype(F32) + c_ref[...].astype(F32)
        mid = in_ref[...].astype(F32) + total + bias_ref[...]
        mid_ref[...] = mid
        act_ref[...] = (norm_parts(mid)[0] * gain_ref[...] + shift_ref[...]).astype(BF)

    return pl.pallas_call(
        kernel,
        out_shape=[jax.ShapeDtypeStruct(own.shape, F32), jax.ShapeDtypeStruct(own.shape, BF)],
        in_specs=[VM] * 8,
        out_specs=[VM] * 2,
        cost_estimate=pl.CostEstimate(
            flops=20 * own.size, transcendentals=0, bytes_accessed=18 * own.size
        ),
        compiler_params=pltpu.CompilerParams(vmem_limit_bytes=8 * MIB),
        name="norm_middle",
    )(own, *others, rows_in, bias[None], gain[None], shift[None])


def norm_middle_back(own, others, mid, cotangent, gain):
    def kernel(own_ref, a_ref, b_ref, c_ref, mid_ref, cot_ref, gain_ref, d_ref, dr_ref, sum_ref):
        grad = own_ref[...] + a_ref[...].astype(F32)
        grad = grad + b_ref[...].astype(F32) + c_ref[...].astype(F32)
        normed, inverse = norm_parts(mid_ref[...])
        cot = cot_ref[...].astype(F32)
        d_mid = cot + norm_backward(grad, normed, inverse, gain_ref[...])
        d_ref[...] = d_mid
        dr_ref[...] = d_mid.astype(BF)
        for i, rows in enumerate((d_mid, cot, grad * normed, grad)):
            sum_ref[i : i + 1, :] = jnp.sum(rows, axis=0, keepdims=True)

    return pl.pallas_call(
        kernel,
        out_shape=[
            jax.ShapeDtypeStruct(own.shape, F32),
            jax.ShapeDtypeStruct(own.shape, BF),
            jax.ShapeDtypeStruct((4, own.shape[1]), F32),
        ],
        in_specs=[VM] * 7,
        out_specs=[VM] * 3,
        cost_estimate=pl.CostEstimate(
            flops=30 * own.size, transcendentals=0, bytes_accessed=24 * own.size
        ),
        compiler_params=pltpu.CompilerParams(vmem_limit_bytes=8 * MIB),
        name="norm_middle_back",
    )(own, *others, mid, cotangent, gain[None])


def packed(q_sum, v_sum, up_sum, gain_sum, shift_sum, middle):
    width, aw = gain_sum.shape[1], q_sum.shape[1]

    def kernel(q_ref, v_ref, up_ref, gain_ref, shift_ref, mid_ref, out_ref):
        own_x = lax.axis_index("seq") // 2
        out_ref[...] = jnp.zeros((16, width), F32)
        for x in range(2):

            @pl.when(own_x == x)
            def _():
                out_ref[x : x + 1, :] = up_ref[...]
                out_ref[2:3, x * aw : (x + 1) * aw] = q_ref[...]
                out_ref[2:3, (2 + x) * aw : (3 + x) * aw] = v_ref[...]

        out_ref[8:12, :] = mid_ref[...]
        out_ref[12:13, :] = gain_ref[...]
        out_ref[13:14, :] = shift_ref[...]

    return pl.pallas_call(
        kernel,
        out_shape=jax.ShapeDtypeStruct((16, width), F32),
        in_specs=[VM] * 6,
        out_specs=VM,
        cost_estimate=pl.CostEstimate(flops=0, transcendentals=0, bytes_accessed=100 * width),
        compiler_params=pltpu.CompilerParams(vmem_limit_bytes=4 * MIB),
        name="packed",
    )(q_sum, v_sum, up_sum, gain_sum, shift_sum, middle)


def make_moves(mesh):
    n_dp, n_seq, n_head = mesh.shape["dp"], mesh.shape["seq"], mesh.shape["head"]

    def core(v):
        return lax.ppermute(v, "seq", [(i, i ^ 1) for i in range(n_seq)])

    def across(v):
        return lax.ppermute(v, "seq", [(i, i ^ 2) for i in range(n_seq)])

    def beside(v):
        return lax.ppermute(v, "head", [(i, i ^ 1) for i in range(n_head)])

    def corner(v):
        pairs = [
            (s * n_head + h, (s ^ 2) * n_head + (h ^ 1))
            for s in range(n_seq)
            for h in range(n_head)
        ]
        return lax.ppermute(v, ("seq", "head"), pairs)

    def along(v, k):
        return lax.ppermute(v, "dp", [(i, i ^ k) for i in range(n_dp)])

    return n_dp, core, across, beside, corner, along


def per_device(
    mesh,
    layer_in,
    cotangent,
    w_query,
    w_key,
    w_value,
    w_out,
    w_up,
    w_down,
    query_bias,
    value_bias,
    out_bias,
    up_bias,
    down_bias,
    attn_gain,
    attn_shift,
    mlp_gain,
    mlp_shift,
):
    n_dp, core, across, beside, corner, along = make_moves(mesh)
    own_z = lax.axis_index("dp")
    own_s = lax.axis_index("seq")
    own_y = lax.axis_index("head")
    own_x, own_c = own_s // 2, own_s % 2
    fr, width = layer_in.shape[1], layer_in.shape[2]
    quarter = fr // 2
    rows = width // n_dp
    aw = w_query.shape[1] // 2
    fw = w_up.shape[1] // 2

    def rolled(a):
        return jnp.concatenate(
            [
                lax.dynamic_slice_in_dim(a, own_y * quarter, quarter, 0),
                lax.dynamic_slice_in_dim(a, (1 - own_y) * quarter, quarter, 0),
            ],
            axis=0,
        )

    def chip_cut(w):
        cols = w.shape[1] // 2
        return jnp.where(own_x == 0, w[:, :cols], w[:, cols:])

    def by_core(first, second):
        return jnp.where(own_c == 0, first, second)

    def gathered(piece):
        pieces = [piece] + [along(piece, k) for k in range(1, n_dp)]
        if rows % 16 == 0:
            mine = assemble(pieces)
        else:
            buf = jnp.zeros((n_dp,) + piece.shape, piece.dtype)
            for k, part in enumerate(pieces):
                buf = lax.dynamic_update_slice(buf, part[None], (own_z ^ k, 0, 0))
            mine = buf.reshape(width, piece.shape[1])
        other = core(mine)
        return by_core(mine, other), by_core(other, mine), mine

    attn_piece = by_core(
        jnp.concatenate([chip_cut(w_key), chip_cut(w_value)], axis=1),
        jnp.concatenate([chip_cut(w_query), chip_cut(w_out)], axis=1),
    )
    wkv, wqo, _ = gathered(attn_piece)
    mine = rolled(layer_in[0])
    rows_in = jnp.concatenate([mine, across(mine)], axis=0)
    inputs = rows_in.astype(F32)
    attn_normed, attn_inverse = norm_parts(inputs)
    attn_act = (attn_normed * attn_gain + attn_shift).astype(BF)
    act_other = core(attn_act)

    zeros_aw = jnp.zeros((aw,), F32)
    q_bias = jnp.concatenate(
        [lax.dynamic_slice_in_dim(query_bias, own_x * aw, aw, 0), zeros_aw]
    )
    v_bias = jnp.concatenate(
        [zeros_aw, lax.dynamic_slice_in_dim(value_bias, own_x * aw, aw, 0)]
    )
    u_bias = lax.dynamic_slice_in_dim(up_bias, own_x * fw, fw, 0)

    query = (mm(attn_act, wqo) + q_bias).astype(BF)
    own_kv = (mm(attn_act, wkv) + v_bias).astype(BF)
    other_kv = (mm(act_other, wkv) + v_bias).astype(BF)

    ff_piece, cot_mine, _, _ = lax.optimization_barrier(
        (by_core(chip_cut(w_up), chip_cut(w_down)), rolled(cotangent[0]), query, own_kv)
    )
    wu, wd, _ = gathered(ff_piece)
    cot = jnp.concatenate([cot_mine, across(cot_mine)], axis=0)
    context, log_total = attention_front(query, own_kv, other_kv, aw)

    def part(a, i):
        return a[i * quarter : (i + 1) * quarter]

    def sent(parts):
        return [move(p) for p, move in zip(parts, (beside, across, corner))]

    def spread(own):
        return jnp.concatenate([own, beside(own), across(own), corner(own)], axis=0)

    def both(own):
        other = beside(own)
        return jnp.where(
            own_y == 0,
            jnp.concatenate([own, other], axis=0),
            jnp.concatenate([other, own], axis=0),
        )

    wu, wd, _ = gathered(ff_piece)
    own_part, *parts = quarters([(context, wqo)])
    parts = sent(parts)
    resid_mid, mlp_own = norm_middle(
        own_part, parts, rows_in[:quarter], out_bias, mlp_gain, mlp_shift
    )
    mlp_act = spread(mlp_own)

    pre_act = mm(mlp_act, wu) + u_bias
    cdf = 0.5 * (1.0 + jax.scipy.special.erf(pre_act * SQRT_HALF))
    hidden = (pre_act * cdf).astype(BF)
    slope = cdf + pre_act * INV_ROOT_TWO_PI * jnp.exp(-0.5 * pre_act * pre_act)
    d_pre = (mm(cot, wd) * slope).astype(BF)
    up_sum = jnp.sum(d_pre.astype(F32), axis=0)[None]
    own_part, *parts = quarters([(d_pre, wu)])
    parts = sent(parts)
    d_mid, d_mid_round, middle_sums = norm_middle_back(
        own_part, parts, resid_mid, cot[:quarter], mlp_gain
    )
    d_mid_all = spread(d_mid_round)

    out_part = mm_nt(after(hidden, d_mid_all), wd)
    out_other = across(out_part[fr:].astype(BF))
    out_part, out_other, _ = lax.optimization_barrier((out_part, out_other, d_mid_all))
    near = out_part[:quarter] + out_other[:quarter].astype(F32) + resid_mid + down_bias
    near = near.astype(BF)
    far = (out_part[quarter:fr] + out_other[quarter:].astype(F32)).astype(BF)
    got = beside(jnp.concatenate([far, near], axis=0)).astype(F32)
    near = (near.astype(F32) + got[:quarter]).astype(BF)
    far = (far.astype(F32) + got[quarter:]).astype(BF)
    layer_out = jnp.where(
        own_y == 0,
        jnp.concatenate([near, far], axis=0),
        jnp.concatenate([far, near], axis=0),
    )

    def shard_sums(first, second):
        keep = by_core(first, second) + core(by_core(second, first).astype(BF)).astype(F32)

        def block(k):
            return lax.dynamic_slice_in_dim(keep, (own_z ^ k) * rows, rows, 0)

        total = block(0)
        sent = [along(block(k).astype(BF), k) for k in range(1, n_dp)]
        for got in sent:
            total = total + got.astype(F32)
        total = total.astype(BF)
        other = across(total)
        left, right = jnp.where(own_x == 0, total, other), jnp.where(own_x == 0, other, total)
        wide = jnp.stack([left, right], axis=0)
        other = core(wide)
        return wide, other

    grad_w_up, grad_w_down = finish(
        *shard_sums(mm_tn(mlp_act, d_pre), mm_tn(cot, hidden)), 1
    )

    d_context = mm(d_mid_all, wqo).astype(BF)
    d_query, kv_own, kv_back, q_sum, v_sum = attention_back(
        query, own_kv, other_kv, context, d_context, log_total, aw
    )
    kv_round = (kv_own + core(kv_back).astype(F32)).astype(BF)
    grad_w_key, grad_w_value, grad_w_query, grad_w_out = finish(
        *shard_sums(
            mm_tn(attn_act, kv_own.astype(BF)) + mm_tn(act_other, kv_back),
            mm_tn(attn_act, d_query) + mm_tn(d_mid_all, context),
        ),
        2,
    )
    own_part, *parts, gain_sum, shift_sum = quarters(
        [(d_query, wqo), (kv_round, wkv)], attn_normed
    )
    parts = sent(parts)
    d_attn_act = own_part
    for p in parts:
        d_attn_act = d_attn_act + p.astype(F32)
    grad_in = d_mid + norm_backward(
        d_attn_act, part(attn_normed, 0), part(attn_inverse, 0), attn_gain
    )
    grad_in = grad_in.astype(BF)
    grad_in = both(grad_in).astype(F32)

    vec = packed(q_sum, v_sum, up_sum, gain_sum, shift_sum, middle_sums)
    k = 1
    while k < n_dp:
        vec = vec + along(vec, k)
        k *= 2
    vec = vec + across(vec)
    vec = vec + core(vec)
    whole = vec[8:]
    whole = whole + beside(whole)
    return (
        layer_out[None],
        grad_in[None],
        grad_w_query,
        grad_w_key,
        grad_w_value,
        grad_w_out,
        grad_w_up,
        grad_w_down,
        vec[2, : 2 * aw],
        vec[2, 2 * aw :],
        whole[0],
        vec[:2].reshape(2 * fw),
        whole[1],
        whole[4],
        whole[5],
        whole[2],
        whole[3],
    )


def solution(mesh):
    square = P("dp", "head")
    acts = P("dp", "seq", None)
    vectors = (P("head"), P("head"), P(), P("head"), P(), P(), P(), P(), P())

    def body(*args):
        return per_device(mesh, *args)

    return jax.shard_map(
        body,
        mesh=mesh,
        in_specs=(acts,) * 2 + (square,) * 6 + vectors,
        out_specs=(acts,) * 2 + (square,) * 6 + vectors,
        check_vma=False,
    )
```

time: 267 us -> 219 us (0.82); the launches traced: 262 us -> 218 us
  Pallas kernels: 0 us -> 20.7 us
  matrix products: 34.2 us -> 16 us
  starting transfers between devices: 66 us -> 49.4 us
  other arithmetic: 27.7 us -> 12.1 us
  local copies, waits for them, and re-layouts: 29.7 us -> 18.6 us
    pallas_call x0 -> x12, Pallas kernels: none -> 20.7 us  [the longest x3 5.48 us: quarters(): pl.pallas_call(kernel, out_shape=[jax.ShapeDtypeStruct((quarter, width),...]
    ppermute x16 -> x14, starting transfers between devices: 32 us -> 17.9 us  [along(): return lax.ppermute(v, 'dp', [(i, i ^ k) for i in range(n_dp)])]
    ppermute x6 -> x5, waiting for transfers between devices: 20.2 us -> 6.1 us  [corner(): return lax.ppermute(v, ('seq', 'head'), pairs)]
    dot_general x12 -> x1, matrix products: 15.9 us -> 2.24 us  [mm_nt(): lax.dot_general(a, b, (((1,), (1,)), ((), ())), preferred_element_type=F32)]
    concatenate x3 -> x4, local copies, waits for them, and re-layouts: 8 us -> 0.11 us  [the longest x1 0.08 us: per_device(): jnp.concatenate([zeros_aw, lax.dynamic_slice_in_dim(value_bias, own_x * a...]
    convert_element_type x13 -> x5, other arithmetic: 8.38 us -> 1.33 us  [the longest x1 0.94 us: per_device(): grad_in = both(grad_in).astype(F32)]
    unnamed x161 -> x113, local copies, waits for them, and re-layouts: 4.19 us -> 10.9 us
    dynamic_slice x8 -> x2, local copies, waits for them, and re-layouts: 6.01 us -> 0.15 us  [the longest x1 0.08 us: per_device(): lax.dynamic_slice_in_dim(query_bias, own_x * aw, aw, 0)]
  transfers between devices with their start and end apart: 54 -> 47, of which waited for: 29 -> 23; matrix products, arithmetic and copies ran while one was open for 27% -> 13% of each run, Pallas kernels for 0% -> 4%
where the time goes in v2:
time: 219 us; the launch traced here: 218 us
  waiting for transfers between devices  99.5 us (45%)
  starting transfers between devices  49.4 us (23%)
  Pallas kernels  20.7 us (9%)
  local copies, waits for them, and re-layouts  18.6 us (8%)
  matrix products  16 us (7%)
  other arithmetic  12.1 us (6%)
    ppermute x14, waiting for transfers between devices, along(): return lax.ppermute(v, 'dp', [(i, i ^ k) for i in range(n_dp)])  58.8 us
    ppermute x11, waiting for transfers between devices, across(): return lax.ppermute(v, 'seq', [(i, i ^ 2) for i in range(n_seq)])  21.1 us
    ppermute x14, starting transfers between devices, along(): return lax.ppermute(v, 'dp', [(i, i ^ k) for i in range(n_dp)])  17.9 us
    ppermute x11, starting transfers between devices, across(): return lax.ppermute(v, 'seq', [(i, i ^ 2) for i in range(n_seq)])  14.6 us
    ppermute x8, waiting for transfers between devices, beside(): return lax.ppermute(v, 'head', [(i, i ^ 1) for i in range(n_head)])  12 us
    unnamed x113, local copies, waits for them, and re-layouts  10.9 us
    ppermute x8, starting transfers between devices, beside(): return lax.ppermute(v, 'head', [(i, i ^ 1) for i in range(n_head)])  7.98 us
    ppermute x5, starting transfers between devices, corner(): return lax.ppermute(v, ('seq', 'head'), pairs)  7.23 us
  transfers between devices with their start and end apart: 47, of which 23 were waited for; matrix products, arithmetic and copies ran while one was open for 13% of the time, Pallas kernels for 4%

profile of v2, /device:TPU:0, one launch (start us, length us, event | category | flops | bytes accessed | tf_op | source)
XLA Modules:
  0.0 217.9 jit_solution(1263966015669898474)
XLA Ops:
  2.1 3.0 %collective-permute-start = (bf16[256,768]{1,0:T(8,128)(2,1)S(1)}, bf16[256,768]{1,0:T(8,128)(2,1)S(1)}, u32[]{:S(2)}, u32[]{:S(2)}) collective-permute-start(bf16[256,768]{1,0:T(8,128)(2,1)S(1)} %pad_maximum_fusion.2), channel_id=1, source_target_pairs={{0,4},{2,6},{4,0},{6,2},{1,5},{3,7},{5,1},{7,3},{8,12},{10,14},{12... | collective-permute-start | bytes 1179656 | tf_op jit(solution)/shard_map/ppermute | solution.py:331
  5.6 3.7 %collective-permute-start.3 = (bf16[192,384]{1,0:T(8,128)(2,1)S(1)}, bf16[192,384]{1,0:T(8,128)(2,1)S(1)}, u32[]{:S(2)}, u32[]{:S(2)}) collective-permute-start(bf16[192,384]{1,0:T(8,128)(2,1)S(1)} %maximum_select_fusion.2.refs_0_), channel_id=1, source_target_pairs={{0,24},{8,16},{16,8},{24,0},{1,25},{9,17},{17,9},{25,1},{2,26},{10... | collective-permute-start | bytes 442376 | tf_op jit(solution)/shard_map/ppermute | solution.py:345
  14.2 7.2 %collective-permute-done.2.refs_2_ = bf16[192,384]{1,0:T(8,128)(2,1)S(1)} collective-permute-done((bf16[192,384]{1,0:T(8,128)(2,1)S(1)}, bf16[192,384]{1,0:T(8,128)(2,1)S(1)}, u32[]{:S(2)}, u32[]{:S(2)}) %collective-permute-start.2) | collective-permute-done | bytes 147488 | tf_op jit(solution)/shard_map/ppermute | solution.py:345
  24.9 2.6 %collective-permute-start.14 = (bf16[192,768]{1,0:T(8,128)(2,1)S(1)}, bf16[192,768]{1,0:T(8,128)(2,1)S(1)}, u32[]{:S(2)}, u32[]{:S(2)}) collective-permute-start(bf16[192,768]{1,0:T(8,128)(2,1)S(1)} %select_select_fusion.refs_0_), channel_id=1, source_target_pairs={{0,24},{8,16},{16,8},{24,0},{1,25},{9,17},{17,9},{25,1},{2,26},{10... | collective-permute-start | bytes 884744 | tf_op jit(solution)/shard_map/ppermute | solution.py:345
  29.4 7.4 %collective-permute-done.14.refs_3_ = bf16[192,768]{1,0:T(8,128)(2,1)S(1)} collective-permute-done((bf16[192,768]{1,0:T(8,128)(2,1)S(1)}, bf16[192,768]{1,0:T(8,128)(2,1)S(1)}, u32[]{:S(2)}, u32[]{:S(2)}) %collective-permute-start.14) | collective-permute-done | bytes 294944 | tf_op jit(solution)/shard_map/ppermute | solution.py:345
  36.8 15.3 %collective-permute-done.13.refs_2_ = bf16[192,768]{1,0:T(8,128)(2,1)S(1)} collective-permute-done((bf16[192,768]{1,0:T(8,128)(2,1)S(1)}, bf16[192,768]{1,0:T(8,128)(2,1)S(1)}, u32[]{:S(2)}, u32[]{:S(2)}) %collective-permute-start.13) | collective-permute-done | bytes 294944 | tf_op jit(solution)/shard_map/ppermute | solution.py:345
  55.4 3.5 %attention_front.1 = (bf16[512,384]{1,0:T(8,128)(2,1)S(1)}, f32[512,128]{1,0:T(8,128)S(1)}) custom-call(bf16[512,384]{1,0:T(8,128)(2,1)S(1)} %fusion.8.q_ref, bf16[512,384]{1,0:T(8,128)(2,1)S(1)} %fusion.9.own_ref, bf16[512,384]{1,0:T(8,128)(2,1)S(1)} %fusion.10.oth_ref), custom_call_target="tpu_custom_call" | custom-call | flops 402653184 | bytes 1179648 | tf_op jit(solution)/shard_map/attention_front/pallas_call | solution.py:137
  68.5 2.3 %collective-permute-done.7.b_ref = bf16[128,768]{1,0:T(8,128)(2,1)} collective-permute-done((bf16[128,768]{1,0:T(8,128)(2,1)}, bf16[128,768]{1,0:T(8,128)(2,1)}, u32[]{:S(2)}, u32[]{:S(2)}) %collective-permute-start.7) | collective-permute-done | bytes 196640 | tf_op jit(solution)/shard_map/ppermute | solution.py:331
  70.8 3.6 %collective-permute-done.8.c_ref = bf16[128,768]{1,0:T(8,128)(2,1)} collective-permute-done((bf16[128,768]{1,0:T(8,128)(2,1)}, bf16[128,768]{1,0:T(8,128)(2,1)}, u32[]{:S(2)}, u32[]{:S(2)}) %collective-permute-start.8) | collective-permute-done | bytes 196640 | tf_op jit(solution)/shard_map/ppermute | solution.py:342
  82.2 5.8 %collective-permute-done.9 = bf16[128,768]{1,0:T(8,128)(2,1)S(1)} collective-permute-done((bf16[128,768]{1,0:T(8,128)(2,1)S(1)}, bf16[128,768]{1,0:T(8,128)(2,1)S(1)}, u32[]{:S(2)}, u32[]{:S(2)}) %collective-permute-start.9) | collective-permute-done | bytes 196640 | tf_op jit(solution)/shard_map/ppermute | solution.py:334
  88.0 2.5 %collective-permute-done.10 = bf16[128,768]{1,0:T(8,128)(2,1)S(1)} collective-permute-done((bf16[128,768]{1,0:T(8,128)(2,1)S(1)}, bf16[128,768]{1,0:T(8,128)(2,1)S(1)}, u32[]{:S(2)}, u32[]{:S(2)}) %collective-permute-start.10) | collective-permute-done | bytes 196640 | tf_op jit(solution)/shard_map/ppermute | solution.py:331
  93.2 2.5 %convert_reduce_fusion.1 = (f32[768]{0:T(1024)S(1)}, bf16[512,768]{1,0:T(8,128)(2,1)S(1)}) fusion(f32[512,768]{1,0:T(8,128)S(1)} %get-tuple-element.125, bf16[512,768]{1,0:T(8,128)(2,1)S(1)} %constant_dynamic-update-slice_fusion.4, bf16[768,768]{1,0:T(8,128)(2,1)} %collective-permute-done.15, bf16[768,768]{1,0:T(8,128)(2,1)S(1)} %assemble.3, pred[]{:T(512)S(6)} %eq.9), kind=kOutput, calls=%fused_computation.13 | convolution fusion | flops 609287424 | bytes 5508097 | tf_op jit(solution)/shard_map/dot_general | solution.py:18
  95.7 2.3 %quarters.4 = (f32[128,768]{1,0:T(8,128)S(1)}, bf16[128,768]{1,0:T(8,128)(2,1)}, bf16[128,768]{1,0:T(8,128)(2,1)}, bf16[128,768]{1,0:T(8,128)(2,1)}) custom-call(bf16[512,768]{1,0:T(8,128)(2,1)S(1)} %get-tuple-element.131.refs_0_, bf16[768,768]{1,0:T(8,128)(2,1)S(1)} %broadcast_select_fusion.1.refs_1_), custom_call_target="tpu_custom_call" | custom-call | flops 603979776 | bytes 1572864 | tf_op jit(solution)/shard_map/quarters/pallas_call | solution.py:228
  103.2 3.7 %collective-permute-done.17.a_ref = bf16[128,768]{1,0:T(8,128)(2,1)} collective-permute-done((bf16[128,768]{1,0:T(8,128)(2,1)}, bf16[128,768]{1,0:T(8,128)(2,1)}, u32[]{:S(2)}, u32[]{:S(2)}) %collective-permute-start.17) | collective-permute-done | bytes 196640 | tf_op jit(solution)/shard_map/ppermute | solution.py:334
  106.9 2.5 %collective-permute-done.19.c_ref = bf16[128,768]{1,0:T(8,128)(2,1)} collective-permute-done((bf16[128,768]{1,0:T(8,128)(2,1)}, bf16[128,768]{1,0:T(8,128)(2,1)}, u32[]{:S(2)}, u32[]{:S(2)}) %collective-permute-start.19) | collective-permute-done | bytes 196640 | tf_op jit(solution)/shard_map/ppermute | solution.py:342
  119.5 4.5 %collective-permute-done.21 = bf16[128,768]{1,0:T(8,128)(2,1)S(1)} collective-permute-done((bf16[128,768]{1,0:T(8,128)(2,1)S(1)}, bf16[128,768]{1,0:T(8,128)(2,1)S(1)}, u32[]{:S(2)}, u32[]{:S(2)}) %collective-permute-start.21) | collective-permute-done | bytes 196640 | tf_op jit(solution)/shard_map/ppermute | solution.py:331
  128.1 5.4 %attention_back.1 = (bf16[512,384]{1,0:T(8,128)(2,1)S(1)}, f32[512,384]{1,0:T(8,128)S(1)}, bf16[512,384]{1,0:T(8,128)(2,1)S(1)}, f32[1,192]{1,0:T(1,128)S(1)}, f32[1,192]{1,0:T(1,128)S(1)}) custom-call(bf16[512,384]{1,0:T(8,128)(2,1)S(1)} %copy-done.18, bf16[512,384]{1,0:T(8,128)(2,1)S(1)} %copy-done.20, bf16[512,384]{1,0:T(8,128)(2,1)S(1)} %copy-done.22, ...), custom_call_target="tpu_custom_call" | custom-call | flops 1006632960 | bytes 1966080 | tf_op jit(solution)/shard_map/attention_back/pallas_call | solution.py:183
  141.8 2.7 %select_convert_fusion = (bf16[768,768]{1,0:T(8,128)(2,1)}, f32[768,768]{1,0:T(8,128)}) fusion(f32[768,768]{1,0:T(8,128)S(1)} %fusion.22, pred[]{:T(512)S(6)} %eq.9, bf16[512,768]{1,0:T(8,128)(2,1)S(1)} %copy-done.37, bf16[512,768]{1,0:T(8,128)(2,1)S(1)} %copy-done.33), kind=kOutput, calls=%fused_computation.2 | convolution fusion | flops 604569600 | bytes 7471105 | tf_op jit(solution)/shard_map/dot_general | solution.py:26
  148.4 5.1 %collective-permute-done.44 = f32[16,768]{1,0:T(8,128)S(1)} collective-permute-done((f32[16,768]{1,0:T(8,128)S(1)}, f32[16,768]{1,0:T(8,128)S(1)}, u32[]{:S(2)}, u32[]{:S(2)}) %collective-permute-start.44) | collective-permute-done | bytes 49184 | tf_op jit(solution)/shard_map/ppermute | solution.py:331
  158.5 2.9 %convert_add_fusion.1 = f32[768,384]{1,0:T(8,128)S(1)} fusion(bf16[768,384]{1,0:T(8,128)(2,1)} %collective-permute-done.30, pred[]{:T(512)S(6)} %eq.9, f32[768,384]{1,0:T(8,128)} %get-tuple-element.127, f32[768,384]{1,0:T(8,128)} %copy-done.27, f32[768,384]{1,0:T(8,128)} %copy-done.29, f32[768,384]{1,0:T(8,128)} %copy-done.28), kind=kLoop, calls=%fused_computation.25 | loop fusion | flops 1474560 | bytes 6488065 | tf_op jit(solution)/shard_map/add | solution.py:495
  176.3 2.7 %collective-permute-done.32 = bf16[192,384]{1,0:T(8,128)(2,1)S(1)} collective-permute-done((bf16[192,384]{1,0:T(8,128)(2,1)S(1)}, bf16[192,384]{1,0:T(8,128)(2,1)S(1)}, u32[]{:S(2)}, u32[]{:S(2)}) %collective-permute-start.32) | collective-permute-done | bytes 147488 | tf_op jit(solution)/shard_map/ppermute | solution.py:345
  183.8 6.3 %collective-permute-done.39 = bf16[192,768]{1,0:T(8,128)(2,1)S(1)} collective-permute-done((bf16[192,768]{1,0:T(8,128)(2,1)S(1)}, bf16[192,768]{1,0:T(8,128)(2,1)S(1)}, u32[]{:S(2)}, u32[]{:S(2)}) %collective-permute-start.39) | collective-permute-done | bytes 294944 | tf_op jit(solution)/shard_map/ppermute | solution.py:345
  190.1 13.7 %collective-permute-done.38 = bf16[192,768]{1,0:T(8,128)(2,1)S(1)} collective-permute-done((bf16[192,768]{1,0:T(8,128)(2,1)S(1)}, bf16[192,768]{1,0:T(8,128)(2,1)S(1)}, u32[]{:S(2)}, u32[]{:S(2)}) %collective-permute-start.38) | collective-permute-done | bytes 294944 | tf_op jit(solution)/shard_map/ppermute | solution.py:345
  205.8 6.7 %collective-permute-done.40 = bf16[192,768]{1,0:T(8,128)(2,1)S(1)} collective-permute-done((bf16[192,768]{1,0:T(8,128)(2,1)S(1)}, bf16[192,768]{1,0:T(8,128)(2,1)S(1)}, u32[]{:S(2)}, u32[]{:S(2)}) %collective-permute-start.40) | collective-permute-done | bytes 294944 | tf_op jit(solution)/shard_map/ppermute | solution.py:331
  (269 shorter events, 98.4 us)
Async XLA Ops:
  2.1 19.5 %collective-permute-start = (bf16[256,768]{1,0:T(8,128)(2,1)S(1)}, bf16[256,768]{1,0:T(8,128)(2,1)S(1)}, u32[]{:S(2)}, u32[]{:S(2)}) collective-permute-start(bf16[256,768]{1,0:T(8,128)(2,1)S(1)} %pad_maximum_fusion.2), channel_id=1, source_target_pairs={{0,4},{2,6},{4,0},{6,2},{1,5},{3,7},{5,1},{7,3},{8,12},{10,14},{12... | collective-permute-start | bytes 1179656 | tf_op jit(solution)/shard_map/ppermute | solution.py:331
  9.2 12.2 %collective-permute-start.2 = (bf16[192,384]{1,0:T(8,128)(2,1)S(1)}, bf16[192,384]{1,0:T(8,128)(2,1)S(1)}, u32[]{:S(2)}, u32[]{:S(2)}) collective-permute-start(bf16[192,384]{1,0:T(8,128)(2,1)S(1)} %maximum_select_fusion.2.refs_0_), channel_id=1, source_target_pairs={{0,16},{8,24},{16,0},{24,8},{1,17},{9,25},{17,1},{25,9},{2,18},{10... | collective-permute-start | bytes 442376 | tf_op jit(solution)/shard_map/ppermute | solution.py:345
  9.2 12.2 %collective-permute-start.1 = (bf16[192,384]{1,0:T(8,128)(2,1)S(1)}, bf16[192,384]{1,0:T(8,128)(2,1)S(1)}, u32[]{:S(2)}, u32[]{:S(2)}) collective-permute-start(bf16[192,384]{1,0:T(8,128)(2,1)S(1)} %maximum_select_fusion.2.refs_0_), channel_id=1, source_target_pairs={{0,8},{8,0},{16,24},{24,16},{1,9},{9,1},{17,25},{25,17},{2,10},{10... | collective-permute-start | bytes 442376 | tf_op jit(solution)/shard_map/ppermute | solution.py:345
  22.8 31.1 %collective-permute-start.5 = (bf16[512,768]{1,0:T(8,128)(2,1)S(1)}, bf16[512,768]{1,0:T(8,128)(2,1)S(1)}, u32[]{:S(2)}, u32[]{:S(2)}) collective-permute-start(bf16[512,768]{1,0:T(8,128)(2,1)S(1)} %get-tuple-element.113), channel_id=1, source_target_pairs={{0,2},{2,0},{4,6},{6,4},{1,3},{3,1},{5,7},{7,5},{8,10},{10,8},{12,... | collective-permute-start | bytes 2359304 | tf_op jit(solution)/shard_map/ppermute | solution.py:328
  24.9 11.9 %collective-permute-start.14 = (bf16[192,768]{1,0:T(8,128)(2,1)S(1)}, bf16[192,768]{1,0:T(8,128)(2,1)S(1)}, u32[]{:S(2)}, u32[]{:S(2)}) collective-permute-start(bf16[192,768]{1,0:T(8,128)(2,1)S(1)} %select_select_fusion.refs_0_), channel_id=1, source_target_pairs={{0,24},{8,16},{16,8},{24,0},{1,25},{9,17},{17,9},{25,1},{2,26},{10... | collective-permute-start | bytes 884744 | tf_op jit(solution)/shard_map/ppermute | solution.py:345
  27.5 24.6 %collective-permute-start.13 = (bf16[192,768]{1,0:T(8,128)(2,1)S(1)}, bf16[192,768]{1,0:T(8,128)(2,1)S(1)}, u32[]{:S(2)}, u32[]{:S(2)}) collective-permute-start(bf16[192,768]{1,0:T(8,128)(2,1)S(1)} %select_select_fusion.refs_0_), channel_id=1, source_target_pairs={{0,16},{8,24},{16,0},{24,8},{1,17},{9,25},{17,1},{25,9},{2,18},{10... | collective-permute-start | bytes 884744 | tf_op jit(solution)/shard_map/ppermute | solution.py:345
  27.5 24.6 %collective-permute-start.12 = (bf16[192,768]{1,0:T(8,128)(2,1)S(1)}, bf16[192,768]{1,0:T(8,128)(2,1)S(1)}, u32[]{:S(2)}, u32[]{:S(2)}) collective-permute-start(bf16[192,768]{1,0:T(8,128)(2,1)S(1)} %select_select_fusion.refs_0_), channel_id=1, source_target_pairs={{0,8},{8,0},{16,24},{24,16},{1,9},{9,1},{17,25},{25,17},{2,10},{10... | collective-permute-start | bytes 884744 | tf_op jit(solution)/shard_map/ppermute | solution.py:345
  53.1 37.4 %collective-permute-start.15 = (bf16[768,768]{1,0:T(8,128)(2,1)S(1)}, bf16[768,768]{1,0:T(8,128)(2,1)}, u32[]{:S(2)}, u32[]{:S(2)}) collective-permute-start(bf16[768,768]{1,0:T(8,128)(2,1)S(1)} %assemble.3), channel_id=1, source_target_pairs={{0,2},{2,0},{4,6},{6,4},{1,3},{3,1},{5,7},{7,5},{8,10},{10,8},{12,... | collective-permute-start | bytes 3538952 | tf_op jit(solution)/shard_map/ppermute | solution.py:328
  53.2 25.4 %collective-permute-start.16 = (bf16[256,768]{1,0:T(8,128)(2,1)}, bf16[256,768]{1,0:T(8,128)(2,1)}, u32[]{:S(2)}, u32[]{:S(2)}) collective-permute-start(bf16[256,768]{1,0:T(8,128)(2,1)} %pad_maximum_fusion.3), channel_id=1, source_target_pairs={{0,4},{2,6},{4,0},{6,2},{1,5},{3,7},{5,1},{7,3},{8,12},{10,14},{12... | collective-permute-start | bytes 1179656 | tf_op jit(solution)/shard_map/ppermute | solution.py:331
  133.6 11.8 %collective-permute-start.23 = (bf16[256,768]{1,0:T(8,128)(2,1)S(1)}, bf16[256,768]{1,0:T(8,128)(2,1)S(1)}, u32[]{:S(2)}, u32[]{:S(2)}) collective-permute-start(bf16[256,768]{1,0:T(8,128)(2,1)S(1)} %slice.182), channel_id=1, source_target_pairs={{0,4},{2,6},{4,0},{6,2},{1,5},{3,7},{5,1},{7,3},{8,12},{10,14},{12... | collective-permute-start | bytes 1179656 | tf_op jit(solution)/shard_map/ppermute | solution.py:331
  139.3 18.9 %collective-permute-start.30 = (bf16[768,384]{1,0:T(8,128)(2,1)}, bf16[768,384]{1,0:T(8,128)(2,1)}, u32[]{:S(2)}, u32[]{:S(2)}) collective-permute-start(bf16[768,384]{1,0:T(8,128)(2,1)} %get-tuple-element.126), channel_id=1, source_target_pairs={{0,2},{2,0},{4,6},{6,4},{1,3},{3,1},{5,7},{7,5},{8,10},{10,8},{12,... | collective-permute-start | bytes 1769480 | tf_op jit(solution)/shard_map/ppermute | solution.py:328
  144.5 23.6 %collective-permute-start.36 = (bf16[768,768]{1,0:T(8,128)(2,1)}, bf16[768,768]{1,0:T(8,128)(2,1)}, u32[]{:S(2)}, u32[]{:S(2)}) collective-permute-start(bf16[768,768]{1,0:T(8,128)(2,1)} %get-tuple-element.128), channel_id=1, source_target_pairs={{0,2},{2,0},{4,6},{6,4},{1,3},{3,1},{5,7},{7,5},{8,10},{10,8},{12,... | collective-permute-start | bytes 3538952 | tf_op jit(solution)/shard_map/ppermute | solution.py:328
  144.5 17.6 %collective-permute-start.26 = (bf16[128,768]{1,0:T(8,128)(2,1)S(1)}, bf16[128,768]{1,0:T(8,128)(2,1)}, u32[]{:S(2)}, u32[]{:S(2)}) collective-permute-start(bf16[128,768]{1,0:T(8,128)(2,1)S(1)} %get-tuple-element.77), channel_id=1, source_target_pairs={{0,1},{1,0},{2,3},{3,2},{4,5},{5,4},{6,7},{7,6},{8,9},{9,8},{10,11... | collective-permute-start | bytes 589832 | tf_op jit(solution)/shard_map/ppermute | solution.py:334
  145.4 18.7 %collective-permute-start.27 = (bf16[128,768]{1,0:T(8,128)(2,1)S(1)}, bf16[128,768]{1,0:T(8,128)(2,1)}, u32[]{:S(2)}, u32[]{:S(2)}) collective-permute-start(bf16[128,768]{1,0:T(8,128)(2,1)S(1)} %get-tuple-element.78), channel_id=1, source_target_pairs={{0,4},{2,6},{4,0},{6,2},{1,5},{3,7},{5,1},{7,3},{8,12},{10,14},{12... | collective-permute-start | bytes 589832 | tf_op jit(solution)/shard_map/ppermute | solution.py:331
  154.8 11.5 %collective-permute-start.28 = (bf16[128,768]{1,0:T(8,128)(2,1)S(1)}, bf16[128,768]{1,0:T(8,128)(2,1)}, u32[]{:S(2)}, u32[]{:S(2)}) collective-permute-start(bf16[128,768]{1,0:T(8,128)(2,1)S(1)} %get-tuple-element.79), channel_id=1, source_target_pairs={{0,5},{1,4},{2,7},{3,6},{4,1},{5,0},{6,3},{7,2},{8,13},{9,12},{10,... | collective-permute-start | bytes 589832 | tf_op jit(solution)/shard_map/ppermute | solution.py:342
  158.2 14.1 %collective-permute-start.46 = (f32[8,768]{1,0:T(8,128)}, f32[8,768]{1,0:T(8,128)S(1)}, u32[]{:S(2)}, u32[]{:S(2)}) collective-permute-start(f32[8,768]{1,0:T(8,128)} %slice.136), channel_id=1, source_target_pairs={{0,1},{1,0},{2,3},{3,2},{4,5},{5,4},{6,7},{7,6},{8,9},{9,8},{10,11... | collective-permute-start | bytes 73736 | tf_op jit(solution)/shard_map/ppermute | solution.py:334
  162.1 12.4 %collective-permute-start.31 = (bf16[192,384]{1,0:T(8,128)(2,1)S(1)}, bf16[192,384]{1,0:T(8,128)(2,1)S(1)}, u32[]{:S(2)}, u32[]{:S(2)}) collective-permute-start(bf16[192,384]{1,0:T(8,128)(2,1)S(1)} %get-tuple-element.107), channel_id=1, source_target_pairs={{0,8},{8,0},{16,24},{24,16},{1,9},{9,1},{17,25},{25,17},{2,10},{10... | collective-permute-start | bytes 442376 | tf_op jit(solution)/shard_map/ppermute | solution.py:345
  166.3 12.7 %collective-permute-start.32 = (bf16[192,384]{1,0:T(8,128)(2,1)S(1)}, bf16[192,384]{1,0:T(8,128)(2,1)S(1)}, u32[]{:S(2)}, u32[]{:S(2)}) collective-permute-start(bf16[192,384]{1,0:T(8,128)(2,1)S(1)} %get-tuple-element.109), channel_id=1, source_target_pairs={{0,16},{8,24},{16,0},{24,8},{1,17},{9,25},{17,1},{25,9},{2,18},{10... | collective-permute-start | bytes 442376 | tf_op jit(solution)/shard_map/ppermute | solution.py:345
  170.0 12.7 %collective-permute-start.37 = (bf16[192,768]{1,0:T(8,128)(2,1)S(1)}, bf16[192,768]{1,0:T(8,128)(2,1)S(1)}, u32[]{:S(2)}, u32[]{:S(2)}) collective-permute-start(bf16[192,768]{1,0:T(8,128)(2,1)S(1)} %get-tuple-element.102), channel_id=1, source_target_pairs={{0,8},{8,0},{16,24},{24,16},{1,9},{9,1},{17,25},{25,17},{2,10},{10... | collective-permute-start | bytes 884744 | tf_op jit(solution)/shard_map/ppermute | solution.py:345
  172.3 17.8 %collective-permute-start.39 = (bf16[192,768]{1,0:T(8,128)(2,1)S(1)}, bf16[192,768]{1,0:T(8,128)(2,1)S(1)}, u32[]{:S(2)}, u32[]{:S(2)}) collective-permute-start(bf16[192,768]{1,0:T(8,128)(2,1)S(1)} %get-tuple-element.103), channel_id=1, source_target_pairs={{0,24},{8,16},{16,8},{24,0},{1,25},{9,17},{17,9},{25,1},{2,26},{10... | collective-permute-start | bytes 884744 | tf_op jit(solution)/shard_map/ppermute | solution.py:345
  174.5 29.3 %collective-permute-start.38 = (bf16[192,768]{1,0:T(8,128)(2,1)S(1)}, bf16[192,768]{1,0:T(8,128)(2,1)S(1)}, u32[]{:S(2)}, u32[]{:S(2)}) collective-permute-start(bf16[192,768]{1,0:T(8,128)(2,1)S(1)} %get-tuple-element.104), channel_id=1, source_target_pairs={{0,16},{8,24},{16,0},{24,8},{1,17},{9,25},{17,1},{25,9},{2,18},{10... | collective-permute-start | bytes 884744 | tf_op jit(solution)/shard_map/ppermute | solution.py:345
  174.5 31.2 %collective-permute-start.24 = (bf16[256,768]{1,0:T(8,128)(2,1)S(1)}, bf16[256,768]{1,0:T(8,128)(2,1)S(1)}, u32[]{:S(2)}, u32[]{:S(2)}) collective-permute-start(bf16[256,768]{1,0:T(8,128)(2,1)S(1)} %pad_maximum_fusion.4), channel_id=1, source_target_pairs={{0,1},{1,0},{2,3},{3,2},{4,5},{5,4},{6,7},{7,6},{8,9},{9,8},{10,11... | collective-permute-start | bytes 1179656 | tf_op jit(solution)/shard_map/ppermute | solution.py:334
  179.0 35.2 %collective-permute-start.29 = (bf16[128,768]{1,0:T(8,128)(2,1)S(1)}, bf16[128,768]{1,0:T(8,128)(2,1)S(1)}, u32[]{:S(2)}, u32[]{:S(2)}) collective-permute-start(bf16[128,768]{1,0:T(8,128)(2,1)S(1)} %add_convert_fusion.3), channel_id=1, source_target_pairs={{0,1},{1,0},{2,3},{3,2},{4,5},{5,4},{6,7},{7,6},{8,9},{9,8},{10,11... | collective-permute-start | bytes 589832 | tf_op jit(solution)/shard_map/ppermute | solution.py:334
  182.7 23.0 %collective-permute-start.34 = (bf16[192,384]{1,0:T(8,128)(2,1)S(1)}, bf16[192,384]{1,0:T(8,128)(2,1)S(1)}, u32[]{:S(2)}, u32[]{:S(2)}) collective-permute-start(bf16[192,384]{1,0:T(8,128)(2,1)S(1)} %add_convert_fusion.6), channel_id=1, source_target_pairs={{0,4},{2,6},{4,0},{6,2},{1,5},{3,7},{5,1},{7,3},{8,12},{10,14},{12... | collective-permute-start | bytes 442376 | tf_op jit(solution)/shard_map/ppermute | solution.py:331
  (77 other events, 508.4 us)

commit v3 on v2

--- a/solution.py
+++ b/solution.py
@@ -156,7 +156,7 @@
     rows = query.shape[0]
 
     def kernel(
-        q_ref, own_ref, oth_ref, c_ref, dc_ref, lt_ref, dq_ref, down_ref, doth_ref, qs_ref, vs_ref
+        q_ref, own_ref, oth_ref, c_ref, dc_ref, lt_ref, dq_ref, down_ref, doth_ref, sum_ref
     ):
         dq_ref[:, width:] = jnp.zeros((rows, width), BF)
         for h in range(width // HD):
@@ -177,8 +177,8 @@
                 out[:, late] = d_value.astype(out.dtype)
                 sums = sums + jnp.sum(d_value, axis=0, keepdims=True)
             dq_ref[:, cols] = d_query.astype(BF)
-            qs_ref[:, cols] = jnp.sum(d_query, axis=0, keepdims=True)
-            vs_ref[:, cols] = sums
+            sum_ref[0:1, cols] = jnp.sum(d_query, axis=0, keepdims=True)
+            sum_ref[0:1, late] = sums
 
     return pl.pallas_call(
         kernel,
@@ -186,11 +186,10 @@
             jax.ShapeDtypeStruct((rows, 2 * width), BF),
             jax.ShapeDtypeStruct((rows, 2 * width), F32),
             jax.ShapeDtypeStruct((rows, 2 * width), BF),
-            jax.ShapeDtypeStruct((1, width), F32),
-            jax.ShapeDtypeStruct((1, width), F32),
+            jax.ShapeDtypeStruct((8, 2 * width), F32),
         ],
         in_specs=[VM] * 6,
-        out_specs=[VM] * 5,
+        out_specs=[VM] * 4,
         cost_estimate=pl.CostEstimate(
             flops=20 * rows * rows * width,
             transcendentals=2 * rows * rows * (width // HD),
@@ -292,10 +291,10 @@
     )(own, *others, mid, cotangent, gain[None])
 
 
-def packed(q_sum, v_sum, up_sum, gain_sum, shift_sum, middle):
-    width, aw = gain_sum.shape[1], q_sum.shape[1]
-
-    def kernel(q_ref, v_ref, up_ref, gain_ref, shift_ref, mid_ref, out_ref):
+def packed(head_sums, up_sum, gain_sum, shift_sum, middle):
+    width, aw = gain_sum.shape[1], head_sums.shape[1] // 2
+
+    def kernel(head_ref, up_ref, gain_ref, shift_ref, mid_ref, out_ref):
         own_x = lax.axis_index("seq") // 2
         out_ref[...] = jnp.zeros((16, width), F32)
         for x in range(2):
@@ -303,8 +302,8 @@
             @pl.when(own_x == x)
             def _():
                 out_ref[x : x + 1, :] = up_ref[...]
-                out_ref[2:3, x * aw : (x + 1) * aw] = q_ref[...]
-                out_ref[2:3, (2 + x) * aw : (3 + x) * aw] = v_ref[...]
+                out_ref[2:3, x * aw : (x + 1) * aw] = head_ref[0:1, :aw]
+                out_ref[2:3, (2 + x) * aw : (3 + x) * aw] = head_ref[0:1, aw:]
 
         out_ref[8:12, :] = mid_ref[...]
         out_ref[12:13, :] = gain_ref[...]
@@ -313,12 +312,62 @@
     return pl.pallas_call(
         kernel,
         out_shape=jax.ShapeDtypeStruct((16, width), F32),
-        in_specs=[VM] * 6,
+        in_specs=[VM] * 5,
         out_specs=VM,
         cost_estimate=pl.CostEstimate(flops=0, transcendentals=0, bytes_accessed=100 * width),
         compiler_params=pltpu.CompilerParams(vmem_limit_bytes=4 * MIB),
         name="packed",
-    )(q_sum, v_sum, up_sum, gain_sum, shift_sum, middle)
+    )(head_sums, up_sum, gain_sum, shift_sum, middle)
+
+
+def feed_forward(acts, cotangent, wu, wd, bias):
+    quarter, width = acts[0].shape
+    rows, hidden = 4 * quarter, wu.shape[1]
+    block = 2 * quarter
+
+    def kernel(*refs):
+        a_refs, (cot_ref, wu_ref, wd_ref, bias_ref) = refs[:4], refs[4:8]
+        act_ref, hid_ref, pre_ref, sum_ref = refs[8:12]
+        outs = refs[12:]
+        for i in range(4):
+            act_ref[i * quarter : (i + 1) * quarter, :] = a_refs[i][...]
+        for i in range(2):
+            at = slice(i * block, (i + 1) * block)
+            pre_act = mm(act_ref[at, :], wu_ref[...]) + bias_ref[...]
+            cdf = 0.5 * (1.0 + lax.erf(pre_act * SQRT_HALF))
+            hid_ref[at, :] = (pre_act * cdf).astype(BF)
+            slope = cdf + pre_act * INV_ROOT_TWO_PI * jnp.exp(-0.5 * pre_act * pre_act)
+            d_pre = (mm(cot_ref[at, :], wd_ref[...]) * slope).astype(BF)
+            pre_ref[at, :] = d_pre
+            total = jnp.sum(d_pre.astype(F32), axis=0, keepdims=True)
+            if i == 0:
+                sum_ref[...] = total
+            else:
+                sum_ref[...] += total
+            grad = mm_nt(d_pre, wu_ref[...])
+            outs[2 * i][...] = grad[:quarter].astype(outs[2 * i].dtype)
+            outs[2 * i + 1][...] = grad[quarter:].astype(BF)
+
+    return pl.pallas_call(
+        kernel,
+        out_shape=[
+            jax.ShapeDtypeStruct((rows, width), BF),
+            jax.ShapeDtypeStruct((rows, hidden), BF),
+            jax.ShapeDtypeStruct((rows, hidden), BF),
+            jax.ShapeDtypeStruct((1, hidden), F32),
+            jax.ShapeDtypeStruct((quarter, width), F32),
+        ]
+        + [jax.ShapeDtypeStruct((quarter, width), BF)] * 3,
+        in_specs=[VM] * 8,
+        out_specs=[VM] * 8,
+        cost_estimate=pl.CostEstimate(
+            flops=6 * rows * width * hidden,
+            transcendentals=2 * rows * hidden,
+            bytes_accessed=4 * width * hidden + 10 * rows * width,
+        ),
+        compiler_params=pltpu.CompilerParams(vmem_limit_bytes=20 * MIB),
+        name="feed_forward",
+    )(*acts, cotangent, wu, wd, bias[None])
 
 
 def make_moves(mesh):
@@ -431,9 +480,10 @@
     own_kv = (mm(attn_act, wkv) + v_bias).astype(BF)
     other_kv = (mm(act_other, wkv) + v_bias).astype(BF)
 
-    ff_piece, cot_mine, _, _ = lax.optimization_barrier(
-        (by_core(chip_cut(w_up), chip_cut(w_down)), rolled(cotangent[0]), query, own_kv)
-    )
+    ff_piece = by_core(chip_cut(w_up), chip_cut(w_down))
+    ff_piece, _, _ = lax.optimization_barrier((ff_piece, query, own_kv))
+    cot_mine = rolled(cotangent[0])
+    cot_mine = after(cot_mine, rows_in)
     wu, wd, _ = gathered(ff_piece)
     cot = jnp.concatenate([cot_mine, across(cot_mine)], axis=0)
     context, log_total = attention_front(query, own_kv, other_kv, aw)
@@ -445,7 +495,7 @@
         return [move(p) for p, move in zip(parts, (beside, across, corner))]
 
     def spread(own):
-        return jnp.concatenate([own, beside(own), across(own), corner(own)], axis=0)
+        return [own, beside(own), across(own), corner(own)]
 
     def both(own):
         other = beside(own)
@@ -461,23 +511,19 @@
     resid_mid, mlp_own = norm_middle(
         own_part, parts, rows_in[:quarter], out_bias, mlp_gain, mlp_shift
     )
-    mlp_act = spread(mlp_own)
-
-    pre_act = mm(mlp_act, wu) + u_bias
-    cdf = 0.5 * (1.0 + jax.scipy.special.erf(pre_act * SQRT_HALF))
-    hidden = (pre_act * cdf).astype(BF)
-    slope = cdf + pre_act * INV_ROOT_TWO_PI * jnp.exp(-0.5 * pre_act * pre_act)
-    d_pre = (mm(cot, wd) * slope).astype(BF)
-    up_sum = jnp.sum(d_pre.astype(F32), axis=0)[None]
-    own_part, *parts = quarters([(d_pre, wu)])
+    mlp_acts = spread(mlp_own)
+    mlp_act, hidden, d_pre, up_sum, own_part, *parts = feed_forward(
+        mlp_acts, cot, wu, wd, u_bias
+    )
     parts = sent(parts)
     d_mid, d_mid_round, middle_sums = norm_middle_back(
         own_part, parts, resid_mid, cot[:quarter], mlp_gain
     )
-    d_mid_all = spread(d_mid_round)
-
-    out_part = mm_nt(after(hidden, d_mid_all), wd)
-    out_other = across(out_part[fr:].astype(BF))
+    d_mid_all = jnp.concatenate(spread(d_mid_round), axis=0)
+
+    out_part = mm_nt(hidden, wd)
+    out_send = after(out_part[fr:].astype(BF), d_mid_all)
+    out_other = across(out_send)
     out_part, out_other, _ = lax.optimization_barrier((out_part, out_other, d_mid_all))
     near = out_part[:quarter] + out_other[:quarter].astype(F32) + resid_mid + down_bias
     near = near.astype(BF)
@@ -497,8 +543,8 @@
         def block(k):
             return lax.dynamic_slice_in_dim(keep, (own_z ^ k) * rows, rows, 0)
 
+        sent = [along(block(k).astype(BF), k) for k in range(1, n_dp)]
         total = block(0)
-        sent = [along(block(k).astype(BF), k) for k in range(1, n_dp)]
         for got in sent:
             total = total + got.astype(F32)
         total = total.astype(BF)
@@ -513,7 +559,7 @@
     )
 
     d_context = mm(d_mid_all, wqo).astype(BF)
-    d_query, kv_own, kv_back, q_sum, v_sum = attention_back(
+    d_query, kv_own, kv_back, head_sums = attention_back(
         query, own_kv, other_kv, context, d_context, log_total, aw
     )
     kv_round = (kv_own + core(kv_back).astype(F32)).astype(BF)
@@ -537,7 +583,7 @@
     grad_in = grad_in.astype(BF)
     grad_in = both(grad_in).astype(F32)
 
-    vec = packed(q_sum, v_sum, up_sum, gain_sum, shift_sum, middle_sums)
+    vec = packed(head_sums, up_sum, gain_sum, shift_sum, middle_sums)
     k = 1
     while k < n_dp:
         vec = vec + along(vec, k)

time: 219 us -> 215 us (0.982)
  local copies, waits for them, and re-layouts: 18.6 us -> 8.69 us
  starting transfers between devices: 49.4 us -> 57.3 us
  Pallas kernels: 20.7 us -> 18.4 us
    unnamed x113 -> x54, local copies, waits for them, and re-layouts: 10.9 us -> 1.49 us
    ppermute x14, starting transfers between devices: 17.9 us -> 26.7 us  [along(): return lax.ppermute(v, 'dp', [(i, i ^ k) for i in range(n_dp)])]
    ppermute x5, waiting for transfers between devices: 6.1 us -> 14 us  [corner(): return lax.ppermute(v, ('seq', 'head'), pairs)]
    ppermute x14, waiting for transfers between devices: 58.8 us -> 53.1 us  [along(): return lax.ppermute(v, 'dp', [(i, i ^ k) for i in range(n_dp)])]
    add x2, other arithmetic: 4.54 us -> 1.99 us  [shard_sums(): by_core(first, second) + core(by_core(second, first).astype(BF)).astype(F32)]
    pallas_call x3 -> x2, Pallas kernels: 5.48 us -> 3.13 us  [quarters(): pl.pallas_call(kernel, out_shape=[jax.ShapeDtypeStruct((quarter, width),...]
    pallas_call x0 -> x1, Pallas kernels: none -> 2.34 us  [feed_forward(): pl.pallas_call(kernel, out_shape=[jax.ShapeDtypeStruct((rows, width), BF)...]
    dot_general x6 -> x4, matrix products: 6.56 us -> 7.47 us  [mm(): return jnp.dot(a, b, preferred_element_type=F32)]
  transfers between devices with their start and end apart: 47 -> 47, of which waited for: 23 -> 22; matrix products, arithmetic and copies ran while one was open for 13% -> 13% of each run, Pallas kernels for 4% -> 6%
where the time goes in v3:
time: 215 us
  waiting for transfers between devices  99.3 us (46%)
  starting transfers between devices  57.3 us (27%)
  Pallas kernels  18.4 us (9%)
  matrix products  17.6 us (8%)
  other arithmetic  11.9 us (6%)
  local copies, waits for them, and re-layouts  8.69 us (4%)
    ppermute x14, waiting for transfers between devices, along(): return lax.ppermute(v, 'dp', [(i, i ^ k) for i in range(n_dp)])  53.1 us
    ppermute x14, starting transfers between devices, along(): return lax.ppermute(v, 'dp', [(i, i ^ k) for i in range(n_dp)])  26.7 us
    ppermute x11, waiting for transfers between devices, across(): return lax.ppermute(v, 'seq', [(i, i ^ 2) for i in range(n_seq)])  20.4 us
    ppermute x5, waiting for transfers between devices, corner(): return lax.ppermute(v, ('seq', 'head'), pairs)  14 us
    ppermute x11, starting transfers between devices, across(): return lax.ppermute(v, 'seq', [(i, i ^ 2) for i in range(n_seq)])  13.3 us
    ppermute x8, waiting for transfers between devices, beside(): return lax.ppermute(v, 'head', [(i, i ^ 1) for i in range(n_head)])  10.5 us
    dot_general x6, matrix products, mm_tn(): lax.dot_general(a, b, (((0,), (0,)), ((), ())), preferred_element_type=F32)  9.32 us
    ppermute x5, starting transfers between devices, corner(): return lax.ppermute(v, ('seq', 'head'), pairs)  8.75 us
  transfers between devices with their start and end apart: 47, of which 22 were waited for; matrix products, arithmetic and copies ran while one was open for 13% of the time, Pallas kernels for 6%

profile of v3, /device:TPU:0, one launch (start us, length us, event | category | flops | bytes accessed | tf_op | source)
XLA Modules:
  0.0 214.5 jit_solution(13242660203046518174)
XLA Ops:
  2.8 3.0 %collective-permute-start = (bf16[256,768]{1,0:T(8,128)(2,1)S(1)}, bf16[256,768]{1,0:T(8,128)(2,1)S(1)}, u32[]{:S(2)}, u32[]{:S(2)}) collective-permute-start(bf16[256,768]{1,0:T(8,128)(2,1)S(1)} %pad_maximum_fusion.2), channel_id=1, source_target_pairs={{0,4},{2,6},{4,0},{6,2},{1,5},{3,7},{5,1},{7,3},{8,12},{10,14},{12... | collective-permute-start | bytes 1179656 | tf_op jit(solution)/shard_map/ppermute | solution.py:380
  7.9 2.6 %collective-permute-start.2 = (bf16[192,384]{1,0:T(8,128)(2,1)S(1)}, bf16[192,384]{1,0:T(8,128)(2,1)S(1)}, u32[]{:S(2)}, u32[]{:S(2)}) collective-permute-start(bf16[192,384]{1,0:T(8,128)(2,1)S(1)} %maximum_select_fusion.2.refs_0_), channel_id=1, source_target_pairs={{0,16},{8,24},{16,0},{24,8},{1,17},{9,25},{17,1},{25,9},{2,18},{10... | collective-permute-start | bytes 442376 | tf_op jit(solution)/shard_map/ppermute | solution.py:394
  13.5 8.3 %collective-permute-done.2.refs_2_ = bf16[192,384]{1,0:T(8,128)(2,1)S(1)} collective-permute-done((bf16[192,384]{1,0:T(8,128)(2,1)S(1)}, bf16[192,384]{1,0:T(8,128)(2,1)S(1)}, u32[]{:S(2)}, u32[]{:S(2)}) %collective-permute-start.2) | collective-permute-done | bytes 147488 | tf_op jit(solution)/shard_map/ppermute | solution.py:394
  24.1 2.7 %fusion.3.q_ref = bf16[512,384]{1,0:T(8,128)(2,1)} fusion(bf16[512,768]{1,0:T(8,128)(2,1)} %get-tuple-element.123, bf16[768,384]{1,0:T(8,128)(2,1)S(1)} %get-tuple-element.121.refs_1_, f32[384]{0:T(512)S(1)} %concatenate.83), kind=kOutput, calls=%fused_computation.11 | convolution fusion | flops 302383104 | bytes 1771008 | tf_op jit(solution)/shard_map/dot_general | solution.py:18
  33.9 10.9 %collective-permute-done.13.refs_1_ = bf16[192,768]{1,0:T(8,128)(2,1)S(1)} collective-permute-done((bf16[192,768]{1,0:T(8,128)(2,1)S(1)}, bf16[192,768]{1,0:T(8,128)(2,1)S(1)}, u32[]{:S(2)}, u32[]{:S(2)}) %collective-permute-start.13) | collective-permute-done | bytes 294944 | tf_op jit(solution)/shard_map/ppermute | solution.py:394
  44.7 10.1 %collective-permute-done.14.refs_2_ = bf16[192,768]{1,0:T(8,128)(2,1)S(1)} collective-permute-done((bf16[192,768]{1,0:T(8,128)(2,1)S(1)}, bf16[192,768]{1,0:T(8,128)(2,1)S(1)}, u32[]{:S(2)}, u32[]{:S(2)}) %collective-permute-start.14) | collective-permute-done | bytes 294944 | tf_op jit(solution)/shard_map/ppermute | solution.py:394
  60.1 3.5 %attention_front.1 = (bf16[512,384]{1,0:T(8,128)(2,1)S(1)}, f32[512,128]{1,0:T(8,128)S(1)}) custom-call(bf16[512,384]{1,0:T(8,128)(2,1)S(1)} %copy-done.4, bf16[512,384]{1,0:T(8,128)(2,1)S(1)} %copy-done.5, bf16[512,384]{1,0:T(8,128)(2,1)S(1)} %fusion.5.oth_ref), custom_call_target="tpu_custom_call" | custom-call | flops 402653184 | bytes 1179648 | tf_op jit(solution)/shard_map/attention_front/pallas_call | solution.py:137
  73.9 4.6 %collective-permute-done.8.c_ref = bf16[128,768]{1,0:T(8,128)(2,1)S(1)} collective-permute-done((bf16[128,768]{1,0:T(8,128)(2,1)S(1)}, bf16[128,768]{1,0:T(8,128)(2,1)S(1)}, u32[]{:S(2)}, u32[]{:S(2)}) %collective-permute-start.8) | collective-permute-done | bytes 196640 | tf_op jit(solution)/shard_map/ppermute | solution.py:391
  87.2 3.5 %collective-permute-done.11.refs_3_ = bf16[128,768]{1,0:T(8,128)(2,1)S(1)} collective-permute-done((bf16[128,768]{1,0:T(8,128)(2,1)S(1)}, bf16[128,768]{1,0:T(8,128)(2,1)S(1)}, u32[]{:S(2)}, u32[]{:S(2)}) %collective-permute-start.11) | collective-permute-done | bytes 196640 | tf_op jit(solution)/shard_map/ppermute | solution.py:391
  94.1 2.5 %collective-permute-start.19 = (bf16[128,768]{1,0:T(8,128)(2,1)S(1)}, bf16[128,768]{1,0:T(8,128)(2,1)S(1)}, u32[]{:S(2)}, u32[]{:S(2)}) collective-permute-start(bf16[128,768]{1,0:T(8,128)(2,1)S(1)} %get-tuple-element.69), channel_id=1, source_target_pairs={{0,5},{1,4},{2,7},{3,6},{4,1},{5,0},{6,3},{7,2},{8,13},{9,12},{10,... | collective-permute-start | bytes 589832 | tf_op jit(solution)/shard_map/ppermute | solution.py:391
  97.4 3.4 %collective-permute-done.17.a_ref = bf16[128,768]{1,0:T(8,128)(2,1)S(1)} collective-permute-done((bf16[128,768]{1,0:T(8,128)(2,1)S(1)}, bf16[128,768]{1,0:T(8,128)(2,1)S(1)}, u32[]{:S(2)}, u32[]{:S(2)}) %collective-permute-start.17) | collective-permute-done | bytes 196640 | tf_op jit(solution)/shard_map/ppermute | solution.py:383
  100.8 3.0 %collective-permute-done.19.c_ref = bf16[128,768]{1,0:T(8,128)(2,1)S(1)} collective-permute-done((bf16[128,768]{1,0:T(8,128)(2,1)S(1)}, bf16[128,768]{1,0:T(8,128)(2,1)S(1)}, u32[]{:S(2)}, u32[]{:S(2)}) %collective-permute-start.19) | collective-permute-done | bytes 196640 | tf_op jit(solution)/shard_map/ppermute | solution.py:391
  108.9 3.3 %collective-permute-done.20 = bf16[128,768]{1,0:T(8,128)(2,1)S(1)} collective-permute-done((bf16[128,768]{1,0:T(8,128)(2,1)S(1)}, bf16[128,768]{1,0:T(8,128)(2,1)S(1)}, u32[]{:S(2)}, u32[]{:S(2)}) %collective-permute-start.20) | collective-permute-done | bytes 196640 | tf_op jit(solution)/shard_map/ppermute | solution.py:383
  112.3 2.9 %collective-permute-done.22 = bf16[128,768]{1,0:T(8,128)(2,1)S(1)} collective-permute-done((bf16[128,768]{1,0:T(8,128)(2,1)S(1)}, bf16[128,768]{1,0:T(8,128)(2,1)S(1)}, u32[]{:S(2)}, u32[]{:S(2)}) %collective-permute-start.22) | collective-permute-done | bytes 196640 | tf_op jit(solution)/shard_map/ppermute | solution.py:391
  116.7 5.4 %attention_back.1 = (bf16[512,384]{1,0:T(8,128)(2,1)S(1)}, f32[512,384]{1,0:T(8,128)S(1)}, bf16[512,384]{1,0:T(8,128)(2,1)S(1)}, f32[8,384]{1,0:T(8,128)S(1)}) custom-call(bf16[512,384]{1,0:T(8,128)(2,1)S(1)} %copy-done.4, bf16[512,384]{1,0:T(8,128)(2,1)S(1)} %copy-done.5, bf16[512,384]{1,0:T(8,128)(2,1)S(1)} %fusion.5.oth_ref, ...), custom_call_target="tpu_custom_call" | custom-call | flops 1006632960 | bytes 1966080 | tf_op jit(solution)/shard_map/attention_back/pallas_call | solution.py:183
  128.2 6.0 %collective-permute-start.42 = (f32[16,768]{1,0:T(8,128)S(1)}, f32[16,768]{1,0:T(8,128)S(1)}, u32[]{:S(2)}, u32[]{:S(2)}) collective-permute-start(f32[16,768]{1,0:T(8,128)S(1)} %packed.1), channel_id=1, source_target_pairs={{0,8},{8,0},{16,24},{24,16},{1,9},{9,1},{17,25},{25,17},{2,10},{10... | collective-permute-start | bytes 147464 | tf_op jit(solution)/shard_map/ppermute | solution.py:394
  136.6 2.8 %collective-permute-start.43 = (f32[16,768]{1,0:T(8,128)S(1)}, f32[16,768]{1,0:T(8,128)S(1)}, u32[]{:S(2)}, u32[]{:S(2)}) collective-permute-start(f32[16,768]{1,0:T(8,128)S(1)} %add.209), channel_id=1, source_target_pairs={{0,16},{8,24},{16,0},{24,8},{1,17},{9,25},{17,1},{25,9},{2,18},{10... | collective-permute-start | bytes 147464 | tf_op jit(solution)/shard_map/ppermute | solution.py:394
  139.5 2.7 %select_convert_fusion = (bf16[768,768]{1,0:T(8,128)(2,1)}, f32[768,768]{1,0:T(8,128)}) fusion(f32[768,768]{1,0:T(8,128)S(1)} %fusion.17, pred[]{:T(512)S(6)} %eq.9, bf16[512,768]{1,0:T(8,128)(2,1)S(1)} %constant_dynamic-update-slice_fusion.refs_4_, bf16[512,768]{1,0:T(8,128)(2,1)S(1)} %get-tuple-element.65), kind=kOutput, calls=%fused_computation.1 | convolution fusion | flops 604569600 | bytes 7471105 | tf_op jit(solution)/shard_map/dot_general | solution.py:26
  145.6 9.4 %collective-permute-done.44 = f32[16,768]{1,0:T(8,128)S(1)} collective-permute-done((f32[16,768]{1,0:T(8,128)S(1)}, f32[16,768]{1,0:T(8,128)S(1)}, u32[]{:S(2)}, u32[]{:S(2)}) %collective-permute-start.44) | collective-permute-done | bytes 49184 | tf_op jit(solution)/shard_map/ppermute | solution.py:380
  163.4 2.6 %collective-permute-start.31 = (bf16[192,384]{1,0:T(8,128)(2,1)}, bf16[192,384]{1,0:T(8,128)(2,1)S(1)}, u32[]{:S(2)}, u32[]{:S(2)}) collective-permute-start(bf16[192,384]{1,0:T(8,128)(2,1)} %get-tuple-element.117), channel_id=1, source_target_pairs={{0,8},{8,0},{16,24},{24,16},{1,9},{9,1},{17,25},{25,17},{2,10},{10... | collective-permute-start | bytes 442376 | tf_op jit(solution)/shard_map/ppermute | solution.py:394
  172.1 2.9 %collective-permute-start.37 = (bf16[192,768]{1,0:T(8,128)(2,1)S(1)}, bf16[192,768]{1,0:T(8,128)(2,1)S(1)}, u32[]{:S(2)}, u32[]{:S(2)}) collective-permute-start(bf16[192,768]{1,0:T(8,128)(2,1)S(1)} %get-tuple-element.110), channel_id=1, source_target_pairs={{0,8},{8,0},{16,24},{24,16},{1,9},{9,1},{17,25},{25,17},{2,10},{10... | collective-permute-start | bytes 884744 | tf_op jit(solution)/shard_map/ppermute | solution.py:394
  174.9 14.3 %collective-permute-done.32 = bf16[192,384]{1,0:T(8,128)(2,1)S(1)} collective-permute-done((bf16[192,384]{1,0:T(8,128)(2,1)}, bf16[192,384]{1,0:T(8,128)(2,1)S(1)}, u32[]{:S(2)}, u32[]{:S(2)}) %collective-permute-start.32) | collective-permute-done | bytes 147488 | tf_op jit(solution)/shard_map/ppermute | solution.py:394
  194.1 6.7 %collective-permute-done.38 = bf16[192,768]{1,0:T(8,128)(2,1)S(1)} collective-permute-done((bf16[192,768]{1,0:T(8,128)(2,1)S(1)}, bf16[192,768]{1,0:T(8,128)(2,1)S(1)}, u32[]{:S(2)}, u32[]{:S(2)}) %collective-permute-start.38) | collective-permute-done | bytes 294944 | tf_op jit(solution)/shard_map/ppermute | solution.py:394
  203.6 5.5 %collective-permute-done.40 = bf16[192,768]{1,0:T(8,128)(2,1)S(1)} collective-permute-done((bf16[192,768]{1,0:T(8,128)(2,1)S(1)}, bf16[192,768]{1,0:T(8,128)(2,1)S(1)}, u32[]{:S(2)}, u32[]{:S(2)}) %collective-permute-start.40) | collective-permute-done | bytes 294944 | tf_op jit(solution)/shard_map/ppermute | solution.py:380
  (207 shorter events, 90.6 us)
Async XLA Ops:
  2.8 19.2 %collective-permute-start = (bf16[256,768]{1,0:T(8,128)(2,1)S(1)}, bf16[256,768]{1,0:T(8,128)(2,1)S(1)}, u32[]{:S(2)}, u32[]{:S(2)}) collective-permute-start(bf16[256,768]{1,0:T(8,128)(2,1)S(1)} %pad_maximum_fusion.2), channel_id=1, source_target_pairs={{0,4},{2,6},{4,0},{6,2},{1,5},{3,7},{5,1},{7,3},{8,12},{10,14},{12... | collective-permute-start | bytes 1179656 | tf_op jit(solution)/shard_map/ppermute | solution.py:380
  7.9 13.9 %collective-permute-start.2 = (bf16[192,384]{1,0:T(8,128)(2,1)S(1)}, bf16[192,384]{1,0:T(8,128)(2,1)S(1)}, u32[]{:S(2)}, u32[]{:S(2)}) collective-permute-start(bf16[192,384]{1,0:T(8,128)(2,1)S(1)} %maximum_select_fusion.2.refs_0_), channel_id=1, source_target_pairs={{0,16},{8,24},{16,0},{24,8},{1,17},{9,25},{17,1},{25,9},{2,18},{10... | collective-permute-start | bytes 442376 | tf_op jit(solution)/shard_map/ppermute | solution.py:394
  10.5 11.3 %collective-permute-start.3 = (bf16[192,384]{1,0:T(8,128)(2,1)S(1)}, bf16[192,384]{1,0:T(8,128)(2,1)S(1)}, u32[]{:S(2)}, u32[]{:S(2)}) collective-permute-start(bf16[192,384]{1,0:T(8,128)(2,1)S(1)} %maximum_select_fusion.2.refs_0_), channel_id=1, source_target_pairs={{0,24},{8,16},{16,8},{24,0},{1,25},{9,17},{17,9},{25,1},{2,26},{10... | collective-permute-start | bytes 442376 | tf_op jit(solution)/shard_map/ppermute | solution.py:394
  29.2 15.5 %collective-permute-start.13 = (bf16[192,768]{1,0:T(8,128)(2,1)S(1)}, bf16[192,768]{1,0:T(8,128)(2,1)S(1)}, u32[]{:S(2)}, u32[]{:S(2)}) collective-permute-start(bf16[192,768]{1,0:T(8,128)(2,1)S(1)} %select_select_fusion.refs_0_), channel_id=1, source_target_pairs={{0,8},{8,0},{16,24},{24,16},{1,9},{9,1},{17,25},{25,17},{2,10},{10... | collective-permute-start | bytes 884744 | tf_op jit(solution)/shard_map/ppermute | solution.py:394
  31.4 23.5 %collective-permute-start.14 = (bf16[192,768]{1,0:T(8,128)(2,1)S(1)}, bf16[192,768]{1,0:T(8,128)(2,1)S(1)}, u32[]{:S(2)}, u32[]{:S(2)}) collective-permute-start(bf16[192,768]{1,0:T(8,128)(2,1)S(1)} %select_select_fusion.refs_0_), channel_id=1, source_target_pairs={{0,16},{8,24},{16,0},{24,8},{1,17},{9,25},{17,1},{25,9},{2,18},{10... | collective-permute-start | bytes 884744 | tf_op jit(solution)/shard_map/ppermute | solution.py:394
  32.5 22.4 %collective-permute-start.15 = (bf16[192,768]{1,0:T(8,128)(2,1)S(1)}, bf16[192,768]{1,0:T(8,128)(2,1)S(1)}, u32[]{:S(2)}, u32[]{:S(2)}) collective-permute-start(bf16[192,768]{1,0:T(8,128)(2,1)S(1)} %select_select_fusion.refs_0_), channel_id=1, source_target_pairs={{0,24},{8,16},{16,8},{24,0},{1,25},{9,17},{17,9},{25,1},{2,26},{10... | collective-permute-start | bytes 884744 | tf_op jit(solution)/shard_map/ppermute | solution.py:394
  33.9 24.4 %collective-permute-start.5 = (bf16[512,768]{1,0:T(8,128)(2,1)}, bf16[512,768]{1,0:T(8,128)(2,1)}, u32[]{:S(2)}, u32[]{:S(2)}) collective-permute-start(bf16[512,768]{1,0:T(8,128)(2,1)} %get-tuple-element.123), channel_id=1, source_target_pairs={{0,2},{2,0},{4,6},{6,4},{1,3},{3,1},{5,7},{7,5},{8,10},{10,8},{12,... | collective-permute-start | bytes 2359304 | tf_op jit(solution)/shard_map/ppermute | solution.py:377
  55.0 27.5 %collective-permute-start.16 = (bf16[768,768]{1,0:T(8,128)(2,1)S(1)}, bf16[768,768]{1,0:T(8,128)(2,1)}, u32[]{:S(2)}, u32[]{:S(2)}) collective-permute-start(bf16[768,768]{1,0:T(8,128)(2,1)S(1)} %assemble.3), channel_id=1, source_target_pairs={{0,2},{2,0},{4,6},{6,4},{1,3},{3,1},{5,7},{7,5},{8,10},{10,8},{12,... | collective-permute-start | bytes 3538952 | tf_op jit(solution)/shard_map/ppermute | solution.py:377
  57.6 12.1 %collective-permute-start.12 = (bf16[256,768]{1,0:T(8,128)(2,1)S(1)}, bf16[256,768]{1,0:T(8,128)(2,1)S(1)}, u32[]{:S(2)}, u32[]{:S(2)}) collective-permute-start(bf16[256,768]{1,0:T(8,128)(2,1)S(1)} %pad_maximum_fusion.3), channel_id=1, source_target_pairs={{0,4},{2,6},{4,0},{6,2},{1,5},{3,7},{5,1},{7,3},{8,12},{10,14},{12... | collective-permute-start | bytes 1179656 | tf_op jit(solution)/shard_map/ppermute | solution.py:380
  67.6 11.0 %collective-permute-start.8 = (bf16[128,768]{1,0:T(8,128)(2,1)S(1)}, bf16[128,768]{1,0:T(8,128)(2,1)S(1)}, u32[]{:S(2)}, u32[]{:S(2)}) collective-permute-start(bf16[128,768]{1,0:T(8,128)(2,1)S(1)} %get-tuple-element.61), channel_id=1, source_target_pairs={{0,5},{1,4},{2,7},{3,6},{4,1},{5,0},{6,3},{7,2},{8,13},{9,12},{10,... | collective-permute-start | bytes 589832 | tf_op jit(solution)/shard_map/ppermute | solution.py:391
  116.4 25.8 %collective-permute-start.23 = (bf16[256,768]{1,0:T(8,128)(2,1)S(1)}, bf16[256,768]{1,0:T(8,128)(2,1)S(1)}, u32[]{:S(2)}, u32[]{:S(2)}) collective-permute-start(bf16[256,768]{1,0:T(8,128)(2,1)S(1)} %slice.182), channel_id=1, source_target_pairs={{0,4},{2,6},{4,0},{6,2},{1,5},{3,7},{5,1},{7,3},{8,12},{10,14},{12... | collective-permute-start | bytes 1179656 | tf_op jit(solution)/shard_map/ppermute | solution.py:380
  136.0 22.3 %collective-permute-start.30 = (bf16[768,384]{1,0:T(8,128)(2,1)S(1)}, bf16[768,384]{1,0:T(8,128)(2,1)S(1)}, u32[]{:S(2)}, u32[]{:S(2)}) collective-permute-start(bf16[768,384]{1,0:T(8,128)(2,1)S(1)} %get-tuple-element.134), channel_id=1, source_target_pairs={{0,2},{2,0},{4,6},{6,4},{1,3},{3,1},{5,7},{7,5},{8,10},{10,8},{12,... | collective-permute-start | bytes 1769480 | tf_op jit(solution)/shard_map/ppermute | solution.py:377
  142.1 26.3 %collective-permute-start.36 = (bf16[768,768]{1,0:T(8,128)(2,1)}, bf16[768,768]{1,0:T(8,128)(2,1)}, u32[]{:S(2)}, u32[]{:S(2)}) collective-permute-start(bf16[768,768]{1,0:T(8,128)(2,1)} %get-tuple-element.136), channel_id=1, source_target_pairs={{0,2},{2,0},{4,6},{6,4},{1,3},{3,1},{5,7},{7,5},{8,10},{10,8},{12,... | collective-permute-start | bytes 3538952 | tf_op jit(solution)/shard_map/ppermute | solution.py:377
  142.2 20.9 %collective-permute-start.28 = (bf16[128,768]{1,0:T(8,128)(2,1)}, bf16[128,768]{1,0:T(8,128)(2,1)}, u32[]{:S(2)}, u32[]{:S(2)}) collective-permute-start(bf16[128,768]{1,0:T(8,128)(2,1)} %get-tuple-element.83), channel_id=1, source_target_pairs={{0,5},{1,4},{2,7},{3,6},{4,1},{5,0},{6,3},{7,2},{8,13},{9,12},{10,... | collective-permute-start | bytes 589832 | tf_op jit(solution)/shard_map/ppermute | solution.py:391
  143.4 20.0 %collective-permute-start.27 = (bf16[128,768]{1,0:T(8,128)(2,1)}, bf16[128,768]{1,0:T(8,128)(2,1)}, u32[]{:S(2)}, u32[]{:S(2)}) collective-permute-start(bf16[128,768]{1,0:T(8,128)(2,1)} %get-tuple-element.82), channel_id=1, source_target_pairs={{0,4},{2,6},{4,0},{6,2},{1,5},{3,7},{5,1},{7,3},{8,12},{10,14},{12... | collective-permute-start | bytes 589832 | tf_op jit(solution)/shard_map/ppermute | solution.py:380
  160.5 11.6 %collective-permute-start.33 = (bf16[192,384]{1,0:T(8,128)(2,1)}, bf16[192,384]{1,0:T(8,128)(2,1)S(1)}, u32[]{:S(2)}, u32[]{:S(2)}) collective-permute-start(bf16[192,384]{1,0:T(8,128)(2,1)} %get-tuple-element.118), channel_id=1, source_target_pairs={{0,24},{8,16},{16,8},{24,0},{1,25},{9,17},{17,9},{25,1},{2,26},{10... | collective-permute-start | bytes 442376 | tf_op jit(solution)/shard_map/ppermute | solution.py:394
  163.0 26.2 %collective-permute-start.32 = (bf16[192,384]{1,0:T(8,128)(2,1)}, bf16[192,384]{1,0:T(8,128)(2,1)S(1)}, u32[]{:S(2)}, u32[]{:S(2)}) collective-permute-start(bf16[192,384]{1,0:T(8,128)(2,1)} %get-tuple-element.119), channel_id=1, source_target_pairs={{0,16},{8,24},{16,0},{24,8},{1,17},{9,25},{17,1},{25,9},{2,18},{10... | collective-permute-start | bytes 442376 | tf_op jit(solution)/shard_map/ppermute | solution.py:394
  163.4 26.3 %collective-permute-start.31 = (bf16[192,384]{1,0:T(8,128)(2,1)}, bf16[192,384]{1,0:T(8,128)(2,1)S(1)}, u32[]{:S(2)}, u32[]{:S(2)}) collective-permute-start(bf16[192,384]{1,0:T(8,128)(2,1)} %get-tuple-element.117), channel_id=1, source_target_pairs={{0,8},{8,0},{16,24},{24,16},{1,9},{9,1},{17,25},{25,17},{2,10},{10... | collective-permute-start | bytes 442376 | tf_op jit(solution)/shard_map/ppermute | solution.py:394
  170.4 21.8 %collective-permute-start.39 = (bf16[192,768]{1,0:T(8,128)(2,1)S(1)}, bf16[192,768]{1,0:T(8,128)(2,1)S(1)}, u32[]{:S(2)}, u32[]{:S(2)}) collective-permute-start(bf16[192,768]{1,0:T(8,128)(2,1)S(1)} %get-tuple-element.111), channel_id=1, source_target_pairs={{0,24},{8,16},{16,8},{24,0},{1,25},{9,17},{17,9},{25,1},{2,26},{10... | collective-permute-start | bytes 884744 | tf_op jit(solution)/shard_map/ppermute | solution.py:394
  171.9 29.0 %collective-permute-start.38 = (bf16[192,768]{1,0:T(8,128)(2,1)S(1)}, bf16[192,768]{1,0:T(8,128)(2,1)S(1)}, u32[]{:S(2)}, u32[]{:S(2)}) collective-permute-start(bf16[192,768]{1,0:T(8,128)(2,1)S(1)} %get-tuple-element.112), channel_id=1, source_target_pairs={{0,16},{8,24},{16,0},{24,8},{1,17},{9,25},{17,1},{25,9},{2,18},{10... | collective-permute-start | bytes 884744 | tf_op jit(solution)/shard_map/ppermute | solution.py:394
  172.1 28.8 %collective-permute-start.37 = (bf16[192,768]{1,0:T(8,128)(2,1)S(1)}, bf16[192,768]{1,0:T(8,128)(2,1)S(1)}, u32[]{:S(2)}, u32[]{:S(2)}) collective-permute-start(bf16[192,768]{1,0:T(8,128)(2,1)S(1)} %get-tuple-element.110), channel_id=1, source_target_pairs={{0,8},{8,0},{16,24},{24,16},{1,9},{9,1},{17,25},{25,17},{2,10},{10... | collective-permute-start | bytes 884744 | tf_op jit(solution)/shard_map/ppermute | solution.py:394
  189.2 14.3 %collective-permute-start.24 = (bf16[256,768]{1,0:T(8,128)(2,1)S(1)}, bf16[256,768]{1,0:T(8,128)(2,1)S(1)}, u32[]{:S(2)}, u32[]{:S(2)}) collective-permute-start(bf16[256,768]{1,0:T(8,128)(2,1)S(1)} %pad_maximum_fusion.4), channel_id=1, source_target_pairs={{0,1},{1,0},{2,3},{3,2},{4,5},{5,4},{6,7},{7,6},{8,9},{9,8},{10,11... | collective-permute-start | bytes 1179656 | tf_op jit(solution)/shard_map/ppermute | solution.py:383
  189.8 21.1 %collective-permute-start.29 = (bf16[128,768]{1,0:T(8,128)(2,1)S(1)}, bf16[128,768]{1,0:T(8,128)(2,1)S(1)}, u32[]{:S(2)}, u32[]{:S(2)}) collective-permute-start(bf16[128,768]{1,0:T(8,128)(2,1)S(1)} %add_convert_fusion.3), channel_id=1, source_target_pairs={{0,1},{1,0},{2,3},{3,2},{4,5},{5,4},{6,7},{7,6},{8,9},{9,8},{10,11... | collective-permute-start | bytes 589832 | tf_op jit(solution)/shard_map/ppermute | solution.py:383
  192.3 11.3 %collective-permute-start.34 = (bf16[192,384]{1,0:T(8,128)(2,1)S(1)}, bf16[192,384]{1,0:T(8,128)(2,1)S(1)}, u32[]{:S(2)}, u32[]{:S(2)}) collective-permute-start(bf16[192,384]{1,0:T(8,128)(2,1)S(1)} %add_convert_fusion.6), channel_id=1, source_target_pairs={{0,4},{2,6},{4,0},{6,2},{1,5},{3,7},{5,1},{7,3},{8,12},{10,14},{12... | collective-permute-start | bytes 442376 | tf_op jit(solution)/shard_map/ppermute | solution.py:380
  (49 other events, 380.1 us)

commit v4 on v3

--- a/solution.py
+++ b/solution.py
@@ -67,7 +67,7 @@
         cost_estimate=pl.CostEstimate(
             flops=0, transcendentals=0, bytes_accessed=4 * n * rows * cols
         ),
-        compiler_params=pltpu.CompilerParams(vmem_limit_bytes=8 * MIB),
+        compiler_params=pltpu.CompilerParams(vmem_limit_bytes=6 * MIB),
         name="assemble",
     )(*pieces)
 
@@ -147,7 +147,7 @@
             transcendentals=2 * rows * rows * (width // HD),
             bytes_accessed=12 * rows * width,
         ),
-        compiler_params=pltpu.CompilerParams(vmem_limit_bytes=24 * MIB),
+        compiler_params=pltpu.CompilerParams(vmem_limit_bytes=14 * MIB),
         name="attention_front",
     )(query, own_kv, other_kv)
 
@@ -195,7 +195,7 @@
             transcendentals=2 * rows * rows * (width // HD),
             bytes_accessed=20 * rows * width,
         ),
-        compiler_params=pltpu.CompilerParams(vmem_limit_bytes=24 * MIB),
+        compiler_params=pltpu.CompilerParams(vmem_limit_bytes=16 * MIB),
         name="attention_back",
     )(query, own_kv, other_kv, context, d_context, log_total)
 
@@ -236,7 +236,7 @@
             transcendentals=0,
             bytes_accessed=4 * rows * width,
         ),
-        compiler_params=pltpu.CompilerParams(vmem_limit_bytes=16 * MIB),
+        compiler_params=pltpu.CompilerParams(vmem_limit_bytes=12 * MIB),
         name="quarters",
     )(*[a for pair in pairs for a in pair], *extra)
 
@@ -257,7 +257,7 @@
         cost_estimate=pl.CostEstimate(
             flops=20 * own.size, transcendentals=0, bytes_accessed=18 * own.size
         ),
-        compiler_params=pltpu.CompilerParams(vmem_limit_bytes=8 * MIB),
+        compiler_params=pltpu.CompilerParams(vmem_limit_bytes=4 * MIB),
         name="norm_middle",
     )(own, *others, rows_in, bias[None], gain[None], shift[None])
 
@@ -286,7 +286,7 @@
         cost_estimate=pl.CostEstimate(
             flops=30 * own.size, transcendentals=0, bytes_accessed=24 * own.size
         ),
-        compiler_params=pltpu.CompilerParams(vmem_limit_bytes=8 * MIB),
+        compiler_params=pltpu.CompilerParams(vmem_limit_bytes=5 * MIB),
         name="norm_middle_back",
     )(own, *others, mid, cotangent, gain[None])
 
@@ -365,7 +365,7 @@
             transcendentals=2 * rows * hidden,
             bytes_accessed=4 * width * hidden + 10 * rows * width,
         ),
-        compiler_params=pltpu.CompilerParams(vmem_limit_bytes=20 * MIB),
+        compiler_params=pltpu.CompilerParams(vmem_limit_bytes=16 * MIB),
         name="feed_forward",
     )(*acts, cotangent, wu, wd, bias[None])
 

time: 215 us -> 216 us (level)
  transfers between devices with their start and end apart: 47 -> 47, of which waited for: 22 -> 21; matrix products, arithmetic and copies ran while one was open for 13% -> 13% of each run, Pallas kernels for 6% -> 7%
where the time goes in v4:
time: 216 us; the launch traced here: 215 us
  waiting for transfers between devices  99.3 us (46%)
  starting transfers between devices  57.3 us (27%)
  Pallas kernels  18.6 us (9%)
  matrix products  17.5 us (8%)
  other arithmetic  12.8 us (6%)
  local copies, waits for them, and re-layouts  7.99 us (4%)
    ppermute x14, waiting for transfers between devices, along(): return lax.ppermute(v, 'dp', [(i, i ^ k) for i in range(n_dp)])  53.3 us
    ppermute x14, starting transfers between devices, along(): return lax.ppermute(v, 'dp', [(i, i ^ k) for i in range(n_dp)])  27 us
    ppermute x11, waiting for transfers between devices, across(): return lax.ppermute(v, 'seq', [(i, i ^ 2) for i in range(n_seq)])  20.3 us
    ppermute x5, waiting for transfers between devices, corner(): return lax.ppermute(v, ('seq', 'head'), pairs)  14 us
    ppermute x11, starting transfers between devices, across(): return lax.ppermute(v, 'seq', [(i, i ^ 2) for i in range(n_seq)])  13.3 us
    ppermute x8, waiting for transfers between devices, beside(): return lax.ppermute(v, 'head', [(i, i ^ 1) for i in range(n_head)])  10.5 us
    dot_general x6, matrix products, mm_tn(): lax.dot_general(a, b, (((0,), (0,)), ((), ())), preferred_element_type=F32)  9.25 us
    ppermute x5, starting transfers between devices, corner(): return lax.ppermute(v, ('seq', 'head'), pairs)  8.55 us
  transfers between devices with their start and end apart: 47, of which 21 were waited for; matrix products, arithmetic and copies ran while one was open for 13% of the time, Pallas kernels for 7%

profile of v4, /device:TPU:0, one launch (start us, length us, event | category | flops | bytes accessed | tf_op | source)
XLA Modules:
  0.0 215.0 jit_solution(2488890504041151159)
XLA Ops:
  2.8 3.0 %collective-permute-start = (bf16[256,768]{1,0:T(8,128)(2,1)S(1)}, bf16[256,768]{1,0:T(8,128)(2,1)}, u32[]{:S(2)}, u32[]{:S(2)}) collective-permute-start(bf16[256,768]{1,0:T(8,128)(2,1)S(1)} %pad_maximum_fusion.2), channel_id=1, source_target_pairs={{0,4},{2,6},{4,0},{6,2},{1,5},{3,7},{5,1},{7,3},{8,12},{10,14},{12... | collective-permute-start | bytes 1179656 | tf_op jit(solution)/shard_map/ppermute | solution.py:380
  7.9 2.6 %collective-permute-start.2 = (bf16[192,384]{1,0:T(8,128)(2,1)S(1)}, bf16[192,384]{1,0:T(8,128)(2,1)S(1)}, u32[]{:S(2)}, u32[]{:S(2)}) collective-permute-start(bf16[192,384]{1,0:T(8,128)(2,1)S(1)} %maximum_select_fusion.2.refs_0_), channel_id=1, source_target_pairs={{0,16},{8,24},{16,0},{24,8},{1,17},{9,25},{17,1},{25,9},{2,18},{10... | collective-permute-start | bytes 442376 | tf_op jit(solution)/shard_map/ppermute | solution.py:394
  13.5 8.3 %collective-permute-done.2.refs_2_ = bf16[192,384]{1,0:T(8,128)(2,1)S(1)} collective-permute-done((bf16[192,384]{1,0:T(8,128)(2,1)S(1)}, bf16[192,384]{1,0:T(8,128)(2,1)S(1)}, u32[]{:S(2)}, u32[]{:S(2)}) %collective-permute-start.2) | collective-permute-done | bytes 147488 | tf_op jit(solution)/shard_map/ppermute | solution.py:394
  25.0 2.7 %fusion.3.q_ref = bf16[512,384]{1,0:T(8,128)(2,1)} fusion(bf16[512,768]{1,0:T(8,128)(2,1)} %get-tuple-element.123, bf16[768,384]{1,0:T(8,128)(2,1)S(1)} %get-tuple-element.121.refs_1_, f32[384]{0:T(512)S(1)} %concatenate.83), kind=kOutput, calls=%fused_computation.11 | convolution fusion | flops 302383104 | bytes 1771008 | tf_op jit(solution)/shard_map/dot_general | solution.py:18
  34.8 11.1 %collective-permute-done.13.refs_1_ = bf16[192,768]{1,0:T(8,128)(2,1)S(1)} collective-permute-done((bf16[192,768]{1,0:T(8,128)(2,1)S(1)}, bf16[192,768]{1,0:T(8,128)(2,1)S(1)}, u32[]{:S(2)}, u32[]{:S(2)}) %collective-permute-start.13) | collective-permute-done | bytes 294944 | tf_op jit(solution)/shard_map/ppermute | solution.py:394
  45.9 9.9 %collective-permute-done.14.refs_2_ = bf16[192,768]{1,0:T(8,128)(2,1)S(1)} collective-permute-done((bf16[192,768]{1,0:T(8,128)(2,1)S(1)}, bf16[192,768]{1,0:T(8,128)(2,1)S(1)}, u32[]{:S(2)}, u32[]{:S(2)}) %collective-permute-start.14) | collective-permute-done | bytes 294944 | tf_op jit(solution)/shard_map/ppermute | solution.py:394
  60.4 3.6 %attention_front.1 = (bf16[512,384]{1,0:T(8,128)(2,1)S(1)}, f32[512,128]{1,0:T(8,128)S(1)}) custom-call(bf16[512,384]{1,0:T(8,128)(2,1)S(1)} %copy-done.2, bf16[512,384]{1,0:T(8,128)(2,1)S(1)} %copy-done.3, bf16[512,384]{1,0:T(8,128)(2,1)S(1)} %fusion.5.oth_ref), custom_call_target="tpu_custom_call" | custom-call | flops 402653184 | bytes 1179648 | tf_op jit(solution)/shard_map/attention_front/pallas_call | solution.py:137
  74.2 4.6 %collective-permute-done.8.c_ref = bf16[128,768]{1,0:T(8,128)(2,1)S(1)} collective-permute-done((bf16[128,768]{1,0:T(8,128)(2,1)S(1)}, bf16[128,768]{1,0:T(8,128)(2,1)S(1)}, u32[]{:S(2)}, u32[]{:S(2)}) %collective-permute-start.8) | collective-permute-done | bytes 196640 | tf_op jit(solution)/shard_map/ppermute | solution.py:391
  87.5 3.5 %collective-permute-done.11.refs_3_ = bf16[128,768]{1,0:T(8,128)(2,1)S(1)} collective-permute-done((bf16[128,768]{1,0:T(8,128)(2,1)S(1)}, bf16[128,768]{1,0:T(8,128)(2,1)S(1)}, u32[]{:S(2)}, u32[]{:S(2)}) %collective-permute-start.11) | collective-permute-done | bytes 196640 | tf_op jit(solution)/shard_map/ppermute | solution.py:391
  94.5 2.5 %collective-permute-start.19 = (bf16[128,768]{1,0:T(8,128)(2,1)S(1)}, bf16[128,768]{1,0:T(8,128)(2,1)S(1)}, u32[]{:S(2)}, u32[]{:S(2)}) collective-permute-start(bf16[128,768]{1,0:T(8,128)(2,1)S(1)} %get-tuple-element.69), channel_id=1, source_target_pairs={{0,5},{1,4},{2,7},{3,6},{4,1},{5,0},{6,3},{7,2},{8,13},{9,12},{10,... | collective-permute-start | bytes 589832 | tf_op jit(solution)/shard_map/ppermute | solution.py:391
  97.8 3.4 %collective-permute-done.17.a_ref = bf16[128,768]{1,0:T(8,128)(2,1)S(1)} collective-permute-done((bf16[128,768]{1,0:T(8,128)(2,1)S(1)}, bf16[128,768]{1,0:T(8,128)(2,1)S(1)}, u32[]{:S(2)}, u32[]{:S(2)}) %collective-permute-start.17) | collective-permute-done | bytes 196640 | tf_op jit(solution)/shard_map/ppermute | solution.py:383
  101.2 3.0 %collective-permute-done.19.c_ref = bf16[128,768]{1,0:T(8,128)(2,1)S(1)} collective-permute-done((bf16[128,768]{1,0:T(8,128)(2,1)S(1)}, bf16[128,768]{1,0:T(8,128)(2,1)S(1)}, u32[]{:S(2)}, u32[]{:S(2)}) %collective-permute-start.19) | collective-permute-done | bytes 196640 | tf_op jit(solution)/shard_map/ppermute | solution.py:391
  109.3 3.3 %collective-permute-done.20 = bf16[128,768]{1,0:T(8,128)(2,1)S(1)} collective-permute-done((bf16[128,768]{1,0:T(8,128)(2,1)S(1)}, bf16[128,768]{1,0:T(8,128)(2,1)S(1)}, u32[]{:S(2)}, u32[]{:S(2)}) %collective-permute-start.20) | collective-permute-done | bytes 196640 | tf_op jit(solution)/shard_map/ppermute | solution.py:383
  112.7 2.9 %collective-permute-done.22 = bf16[128,768]{1,0:T(8,128)(2,1)S(1)} collective-permute-done((bf16[128,768]{1,0:T(8,128)(2,1)S(1)}, bf16[128,768]{1,0:T(8,128)(2,1)S(1)}, u32[]{:S(2)}, u32[]{:S(2)}) %collective-permute-start.22) | collective-permute-done | bytes 196640 | tf_op jit(solution)/shard_map/ppermute | solution.py:391
  117.1 5.4 %attention_back.1 = (bf16[512,384]{1,0:T(8,128)(2,1)S(1)}, f32[512,384]{1,0:T(8,128)S(1)}, bf16[512,384]{1,0:T(8,128)(2,1)S(1)}, f32[8,384]{1,0:T(8,128)S(1)}) custom-call(bf16[512,384]{1,0:T(8,128)(2,1)S(1)} %copy-done.2, bf16[512,384]{1,0:T(8,128)(2,1)S(1)} %copy-done.3, bf16[512,384]{1,0:T(8,128)(2,1)S(1)} %fusion.5.oth_ref, ...), custom_call_target="tpu_custom_call" | custom-call | flops 1006632960 | bytes 1966080 | tf_op jit(solution)/shard_map/attention_back/pallas_call | solution.py:183
  128.7 6.2 %collective-permute-start.42 = (f32[16,768]{1,0:T(8,128)S(1)}, f32[16,768]{1,0:T(8,128)S(1)}, u32[]{:S(2)}, u32[]{:S(2)}) collective-permute-start(f32[16,768]{1,0:T(8,128)S(1)} %packed.1), channel_id=1, source_target_pairs={{0,8},{8,0},{16,24},{24,16},{1,9},{9,1},{17,25},{25,17},{2,10},{10... | collective-permute-start | bytes 147464 | tf_op jit(solution)/shard_map/ppermute | solution.py:394
  137.3 2.8 %collective-permute-start.43 = (f32[16,768]{1,0:T(8,128)S(1)}, f32[16,768]{1,0:T(8,128)S(1)}, u32[]{:S(2)}, u32[]{:S(2)}) collective-permute-start(f32[16,768]{1,0:T(8,128)S(1)} %add.209), channel_id=1, source_target_pairs={{0,16},{8,24},{16,0},{24,8},{1,17},{9,25},{17,1},{25,9},{2,18},{10... | collective-permute-start | bytes 147464 | tf_op jit(solution)/shard_map/ppermute | solution.py:394
  140.1 2.6 %select_convert_fusion = (bf16[768,768]{1,0:T(8,128)(2,1)}, f32[768,768]{1,0:T(8,128)}) fusion(f32[768,768]{1,0:T(8,128)S(1)} %fusion.17, pred[]{:T(512)S(6)} %eq.9, bf16[512,768]{1,0:T(8,128)(2,1)S(1)} %constant_dynamic-update-slice_fusion.refs_4_, bf16[512,768]{1,0:T(8,128)(2,1)S(1)} %get-tuple-element.65), kind=kOutput, calls=%fused_computation.1 | convolution fusion | flops 604569600 | bytes 7471105 | tf_op jit(solution)/shard_map/dot_general | solution.py:26
  146.2 9.4 %collective-permute-done.44 = f32[16,768]{1,0:T(8,128)S(1)} collective-permute-done((f32[16,768]{1,0:T(8,128)S(1)}, f32[16,768]{1,0:T(8,128)S(1)}, u32[]{:S(2)}, u32[]{:S(2)}) %collective-permute-start.44) | collective-permute-done | bytes 49184 | tf_op jit(solution)/shard_map/ppermute | solution.py:380
  164.0 2.6 %collective-permute-start.31 = (bf16[192,384]{1,0:T(8,128)(2,1)}, bf16[192,384]{1,0:T(8,128)(2,1)S(1)}, u32[]{:S(2)}, u32[]{:S(2)}) collective-permute-start(bf16[192,384]{1,0:T(8,128)(2,1)} %get-tuple-element.117), channel_id=1, source_target_pairs={{0,8},{8,0},{16,24},{24,16},{1,9},{9,1},{17,25},{25,17},{2,10},{10... | collective-permute-start | bytes 442376 | tf_op jit(solution)/shard_map/ppermute | solution.py:394
  172.5 2.9 %collective-permute-start.37 = (bf16[192,768]{1,0:T(8,128)(2,1)S(1)}, bf16[192,768]{1,0:T(8,128)(2,1)S(1)}, u32[]{:S(2)}, u32[]{:S(2)}) collective-permute-start(bf16[192,768]{1,0:T(8,128)(2,1)S(1)} %get-tuple-element.110), channel_id=1, source_target_pairs={{0,8},{8,0},{16,24},{24,16},{1,9},{9,1},{17,25},{25,17},{2,10},{10... | collective-permute-start | bytes 884744 | tf_op jit(solution)/shard_map/ppermute | solution.py:394
  175.4 14.3 %collective-permute-done.32 = bf16[192,384]{1,0:T(8,128)(2,1)S(1)} collective-permute-done((bf16[192,384]{1,0:T(8,128)(2,1)}, bf16[192,384]{1,0:T(8,128)(2,1)S(1)}, u32[]{:S(2)}, u32[]{:S(2)}) %collective-permute-start.32) | collective-permute-done | bytes 147488 | tf_op jit(solution)/shard_map/ppermute | solution.py:394
  194.6 6.8 %collective-permute-done.38 = bf16[192,768]{1,0:T(8,128)(2,1)S(1)} collective-permute-done((bf16[192,768]{1,0:T(8,128)(2,1)S(1)}, bf16[192,768]{1,0:T(8,128)(2,1)S(1)}, u32[]{:S(2)}, u32[]{:S(2)}) %collective-permute-start.38) | collective-permute-done | bytes 294944 | tf_op jit(solution)/shard_map/ppermute | solution.py:394
  204.1 5.5 %collective-permute-done.40 = bf16[192,768]{1,0:T(8,128)(2,1)S(1)} collective-permute-done((bf16[192,768]{1,0:T(8,128)(2,1)S(1)}, bf16[192,768]{1,0:T(8,128)(2,1)S(1)}, u32[]{:S(2)}, u32[]{:S(2)}) %collective-permute-start.40) | collective-permute-done | bytes 294944 | tf_op jit(solution)/shard_map/ppermute | solution.py:380
  (205 shorter events, 90.7 us)
Async XLA Ops:
  2.8 19.2 %collective-permute-start = (bf16[256,768]{1,0:T(8,128)(2,1)S(1)}, bf16[256,768]{1,0:T(8,128)(2,1)}, u32[]{:S(2)}, u32[]{:S(2)}) collective-permute-start(bf16[256,768]{1,0:T(8,128)(2,1)S(1)} %pad_maximum_fusion.2), channel_id=1, source_target_pairs={{0,4},{2,6},{4,0},{6,2},{1,5},{3,7},{5,1},{7,3},{8,12},{10,14},{12... | collective-permute-start | bytes 1179656 | tf_op jit(solution)/shard_map/ppermute | solution.py:380
  7.9 13.9 %collective-permute-start.2 = (bf16[192,384]{1,0:T(8,128)(2,1)S(1)}, bf16[192,384]{1,0:T(8,128)(2,1)S(1)}, u32[]{:S(2)}, u32[]{:S(2)}) collective-permute-start(bf16[192,384]{1,0:T(8,128)(2,1)S(1)} %maximum_select_fusion.2.refs_0_), channel_id=1, source_target_pairs={{0,16},{8,24},{16,0},{24,8},{1,17},{9,25},{17,1},{25,9},{2,18},{10... | collective-permute-start | bytes 442376 | tf_op jit(solution)/shard_map/ppermute | solution.py:394
  10.5 11.3 %collective-permute-start.3 = (bf16[192,384]{1,0:T(8,128)(2,1)S(1)}, bf16[192,384]{1,0:T(8,128)(2,1)S(1)}, u32[]{:S(2)}, u32[]{:S(2)}) collective-permute-start(bf16[192,384]{1,0:T(8,128)(2,1)S(1)} %maximum_select_fusion.2.refs_0_), channel_id=1, source_target_pairs={{0,24},{8,16},{16,8},{24,0},{1,25},{9,17},{17,9},{25,1},{2,26},{10... | collective-permute-start | bytes 442376 | tf_op jit(solution)/shard_map/ppermute | solution.py:394
  30.1 15.7 %collective-permute-start.13 = (bf16[192,768]{1,0:T(8,128)(2,1)S(1)}, bf16[192,768]{1,0:T(8,128)(2,1)S(1)}, u32[]{:S(2)}, u32[]{:S(2)}) collective-permute-start(bf16[192,768]{1,0:T(8,128)(2,1)S(1)} %select_select_fusion.refs_0_), channel_id=1, source_target_pairs={{0,8},{8,0},{16,24},{24,16},{1,9},{9,1},{17,25},{25,17},{2,10},{10... | collective-permute-start | bytes 884744 | tf_op jit(solution)/shard_map/ppermute | solution.py:394
  32.3 23.5 %collective-permute-start.14 = (bf16[192,768]{1,0:T(8,128)(2,1)S(1)}, bf16[192,768]{1,0:T(8,128)(2,1)S(1)}, u32[]{:S(2)}, u32[]{:S(2)}) collective-permute-start(bf16[192,768]{1,0:T(8,128)(2,1)S(1)} %select_select_fusion.refs_0_), channel_id=1, source_target_pairs={{0,16},{8,24},{16,0},{24,8},{1,17},{9,25},{17,1},{25,9},{2,18},{10... | collective-permute-start | bytes 884744 | tf_op jit(solution)/shard_map/ppermute | solution.py:394
  33.4 22.4 %collective-permute-start.15 = (bf16[192,768]{1,0:T(8,128)(2,1)S(1)}, bf16[192,768]{1,0:T(8,128)(2,1)S(1)}, u32[]{:S(2)}, u32[]{:S(2)}) collective-permute-start(bf16[192,768]{1,0:T(8,128)(2,1)S(1)} %select_select_fusion.refs_0_), channel_id=1, source_target_pairs={{0,24},{8,16},{16,8},{24,0},{1,25},{9,17},{17,9},{25,1},{2,26},{10... | collective-permute-start | bytes 884744 | tf_op jit(solution)/shard_map/ppermute | solution.py:394
  34.8 23.8 %collective-permute-start.5 = (bf16[512,768]{1,0:T(8,128)(2,1)}, bf16[512,768]{1,0:T(8,128)(2,1)}, u32[]{:S(2)}, u32[]{:S(2)}) collective-permute-start(bf16[512,768]{1,0:T(8,128)(2,1)} %get-tuple-element.123), channel_id=1, source_target_pairs={{0,2},{2,0},{4,6},{6,4},{1,3},{3,1},{5,7},{7,5},{8,10},{10,8},{12,... | collective-permute-start | bytes 2359304 | tf_op jit(solution)/shard_map/ppermute | solution.py:377
  55.9 26.8 %collective-permute-start.16 = (bf16[768,768]{1,0:T(8,128)(2,1)S(1)}, bf16[768,768]{1,0:T(8,128)(2,1)}, u32[]{:S(2)}, u32[]{:S(2)}) collective-permute-start(bf16[768,768]{1,0:T(8,128)(2,1)S(1)} %assemble.3), channel_id=1, source_target_pairs={{0,2},{2,0},{4,6},{6,4},{1,3},{3,1},{5,7},{7,5},{8,10},{10,8},{12,... | collective-permute-start | bytes 3538952 | tf_op jit(solution)/shard_map/ppermute | solution.py:377
  57.9 12.1 %collective-permute-start.12 = (bf16[256,768]{1,0:T(8,128)(2,1)S(1)}, bf16[256,768]{1,0:T(8,128)(2,1)S(1)}, u32[]{:S(2)}, u32[]{:S(2)}) collective-permute-start(bf16[256,768]{1,0:T(8,128)(2,1)S(1)} %pad_maximum_fusion.3), channel_id=1, source_target_pairs={{0,4},{2,6},{4,0},{6,2},{1,5},{3,7},{5,1},{7,3},{8,12},{10,14},{12... | collective-permute-start | bytes 1179656 | tf_op jit(solution)/shard_map/ppermute | solution.py:380
  67.9 10.9 %collective-permute-start.8 = (bf16[128,768]{1,0:T(8,128)(2,1)S(1)}, bf16[128,768]{1,0:T(8,128)(2,1)S(1)}, u32[]{:S(2)}, u32[]{:S(2)}) collective-permute-start(bf16[128,768]{1,0:T(8,128)(2,1)S(1)} %get-tuple-element.61), channel_id=1, source_target_pairs={{0,5},{1,4},{2,7},{3,6},{4,1},{5,0},{6,3},{7,2},{8,13},{9,12},{10,... | collective-permute-start | bytes 589832 | tf_op jit(solution)/shard_map/ppermute | solution.py:391
  116.8 26.0 %collective-permute-start.23 = (bf16[256,768]{1,0:T(8,128)(2,1)S(1)}, bf16[256,768]{1,0:T(8,128)(2,1)S(1)}, u32[]{:S(2)}, u32[]{:S(2)}) collective-permute-start(bf16[256,768]{1,0:T(8,128)(2,1)S(1)} %slice.182), channel_id=1, source_target_pairs={{0,4},{2,6},{4,0},{6,2},{1,5},{3,7},{5,1},{7,3},{8,12},{10,14},{12... | collective-permute-start | bytes 1179656 | tf_op jit(solution)/shard_map/ppermute | solution.py:380
  136.6 22.3 %collective-permute-start.30 = (bf16[768,384]{1,0:T(8,128)(2,1)S(1)}, bf16[768,384]{1,0:T(8,128)(2,1)S(1)}, u32[]{:S(2)}, u32[]{:S(2)}) collective-permute-start(bf16[768,384]{1,0:T(8,128)(2,1)S(1)} %get-tuple-element.134), channel_id=1, source_target_pairs={{0,2},{2,0},{4,6},{6,4},{1,3},{3,1},{5,7},{7,5},{8,10},{10,8},{12,... | collective-permute-start | bytes 1769480 | tf_op jit(solution)/shard_map/ppermute | solution.py:377
  142.8 26.1 %collective-permute-start.36 = (bf16[768,768]{1,0:T(8,128)(2,1)}, bf16[768,768]{1,0:T(8,128)(2,1)}, u32[]{:S(2)}, u32[]{:S(2)}) collective-permute-start(bf16[768,768]{1,0:T(8,128)(2,1)} %get-tuple-element.136), channel_id=1, source_target_pairs={{0,2},{2,0},{4,6},{6,4},{1,3},{3,1},{5,7},{7,5},{8,10},{10,8},{12,... | collective-permute-start | bytes 3538952 | tf_op jit(solution)/shard_map/ppermute | solution.py:377
  142.8 20.8 %collective-permute-start.28 = (bf16[128,768]{1,0:T(8,128)(2,1)}, bf16[128,768]{1,0:T(8,128)(2,1)}, u32[]{:S(2)}, u32[]{:S(2)}) collective-permute-start(bf16[128,768]{1,0:T(8,128)(2,1)} %get-tuple-element.83), channel_id=1, source_target_pairs={{0,5},{1,4},{2,7},{3,6},{4,1},{5,0},{6,3},{7,2},{8,13},{9,12},{10,... | collective-permute-start | bytes 589832 | tf_op jit(solution)/shard_map/ppermute | solution.py:391
  143.9 20.0 %collective-permute-start.27 = (bf16[128,768]{1,0:T(8,128)(2,1)}, bf16[128,768]{1,0:T(8,128)(2,1)}, u32[]{:S(2)}, u32[]{:S(2)}) collective-permute-start(bf16[128,768]{1,0:T(8,128)(2,1)} %get-tuple-element.82), channel_id=1, source_target_pairs={{0,4},{2,6},{4,0},{6,2},{1,5},{3,7},{5,1},{7,3},{8,12},{10,14},{12... | collective-permute-start | bytes 589832 | tf_op jit(solution)/shard_map/ppermute | solution.py:380
  161.0 11.5 %collective-permute-start.33 = (bf16[192,384]{1,0:T(8,128)(2,1)}, bf16[192,384]{1,0:T(8,128)(2,1)S(1)}, u32[]{:S(2)}, u32[]{:S(2)}) collective-permute-start(bf16[192,384]{1,0:T(8,128)(2,1)} %get-tuple-element.118), channel_id=1, source_target_pairs={{0,24},{8,16},{16,8},{24,0},{1,25},{9,17},{17,9},{25,1},{2,26},{10... | collective-permute-start | bytes 442376 | tf_op jit(solution)/shard_map/ppermute | solution.py:394
  163.6 26.1 %collective-permute-start.32 = (bf16[192,384]{1,0:T(8,128)(2,1)}, bf16[192,384]{1,0:T(8,128)(2,1)S(1)}, u32[]{:S(2)}, u32[]{:S(2)}) collective-permute-start(bf16[192,384]{1,0:T(8,128)(2,1)} %get-tuple-element.119), channel_id=1, source_target_pairs={{0,16},{8,24},{16,0},{24,8},{1,17},{9,25},{17,1},{25,9},{2,18},{10... | collective-permute-start | bytes 442376 | tf_op jit(solution)/shard_map/ppermute | solution.py:394
  164.0 26.2 %collective-permute-start.31 = (bf16[192,384]{1,0:T(8,128)(2,1)}, bf16[192,384]{1,0:T(8,128)(2,1)S(1)}, u32[]{:S(2)}, u32[]{:S(2)}) collective-permute-start(bf16[192,384]{1,0:T(8,128)(2,1)} %get-tuple-element.117), channel_id=1, source_target_pairs={{0,8},{8,0},{16,24},{24,16},{1,9},{9,1},{17,25},{25,17},{2,10},{10... | collective-permute-start | bytes 442376 | tf_op jit(solution)/shard_map/ppermute | solution.py:394
  170.9 21.9 %collective-permute-start.39 = (bf16[192,768]{1,0:T(8,128)(2,1)S(1)}, bf16[192,768]{1,0:T(8,128)(2,1)S(1)}, u32[]{:S(2)}, u32[]{:S(2)}) collective-permute-start(bf16[192,768]{1,0:T(8,128)(2,1)S(1)} %get-tuple-element.111), channel_id=1, source_target_pairs={{0,24},{8,16},{16,8},{24,0},{1,25},{9,17},{17,9},{25,1},{2,26},{10... | collective-permute-start | bytes 884744 | tf_op jit(solution)/shard_map/ppermute | solution.py:394
  172.3 29.0 %collective-permute-start.38 = (bf16[192,768]{1,0:T(8,128)(2,1)S(1)}, bf16[192,768]{1,0:T(8,128)(2,1)S(1)}, u32[]{:S(2)}, u32[]{:S(2)}) collective-permute-start(bf16[192,768]{1,0:T(8,128)(2,1)S(1)} %get-tuple-element.112), channel_id=1, source_target_pairs={{0,16},{8,24},{16,0},{24,8},{1,17},{9,25},{17,1},{25,9},{2,18},{10... | collective-permute-start | bytes 884744 | tf_op jit(solution)/shard_map/ppermute | solution.py:394
  172.5 28.9 %collective-permute-start.37 = (bf16[192,768]{1,0:T(8,128)(2,1)S(1)}, bf16[192,768]{1,0:T(8,128)(2,1)S(1)}, u32[]{:S(2)}, u32[]{:S(2)}) collective-permute-start(bf16[192,768]{1,0:T(8,128)(2,1)S(1)} %get-tuple-element.110), channel_id=1, source_target_pairs={{0,8},{8,0},{16,24},{24,16},{1,9},{9,1},{17,25},{25,17},{2,10},{10... | collective-permute-start | bytes 884744 | tf_op jit(solution)/shard_map/ppermute | solution.py:394
  189.7 14.3 %collective-permute-start.24 = (bf16[256,768]{1,0:T(8,128)(2,1)S(1)}, bf16[256,768]{1,0:T(8,128)(2,1)S(1)}, u32[]{:S(2)}, u32[]{:S(2)}) collective-permute-start(bf16[256,768]{1,0:T(8,128)(2,1)S(1)} %pad_maximum_fusion.4), channel_id=1, source_target_pairs={{0,1},{1,0},{2,3},{3,2},{4,5},{5,4},{6,7},{7,6},{8,9},{9,8},{10,11... | collective-permute-start | bytes 1179656 | tf_op jit(solution)/shard_map/ppermute | solution.py:383
  190.1 21.2 %collective-permute-start.29 = (bf16[128,768]{1,0:T(8,128)(2,1)S(1)}, bf16[128,768]{1,0:T(8,128)(2,1)S(1)}, u32[]{:S(2)}, u32[]{:S(2)}) collective-permute-start(bf16[128,768]{1,0:T(8,128)(2,1)S(1)} %add_convert_fusion.3), channel_id=1, source_target_pairs={{0,1},{1,0},{2,3},{3,2},{4,5},{5,4},{6,7},{7,6},{8,9},{9,8},{10,11... | collective-permute-start | bytes 589832 | tf_op jit(solution)/shard_map/ppermute | solution.py:383
  192.8 11.2 %collective-permute-start.34 = (bf16[192,384]{1,0:T(8,128)(2,1)S(1)}, bf16[192,384]{1,0:T(8,128)(2,1)S(1)}, u32[]{:S(2)}, u32[]{:S(2)}) collective-permute-start(bf16[192,384]{1,0:T(8,128)(2,1)S(1)} %add_convert_fusion.6), channel_id=1, source_target_pairs={{0,4},{2,6},{4,0},{6,2},{1,5},{3,7},{5,1},{7,3},{8,12},{10,14},{12... | collective-permute-start | bytes 442376 | tf_op jit(solution)/shard_map/ppermute | solution.py:380
  (48 other events, 394.5 us)
